TPU v7x, 32 devices: a whole 2x2x4 slice. The times are simulated.
32 devices in a mesh: dp: 8 (over y, x, core), tensor: 4 (over z).
Axes of the slice: x: 2, y: 2, z: 4, core: 2. Of those that a mesh axis runs over, the one named last changes fastest.
Arguments:
- inputs: float32 [4096, 768], P(('dp', 'tensor')), may hold values from -6 to 6
- qkv_weight: bfloat16 [1, 768, 3, 768], P(None, 'dp', None, 'tensor')
- out_weight: bfloat16 [1, 768, 768], P(None, 'tensor', 'dp'), may hold values from -1.75 to 1.75
- fc_weight: bfloat16 [1, 768, 3072], P(None, 'dp', 'tensor'), may hold values from -0.21875 to 0.21875
- proj_weight: bfloat16 [1, 3072, 768], P(None, 'tensor', 'dp'), may hold values from -0.109375 to 0.109375
- vectors: float32 [1, 12, 768], P(None, None, ('dp', 'tensor')), as said below
- out_grad: float32 [4096, 768], P(('dp', 'tensor')), may hold values from -6 to 6
Outputs:
- outputs: float32 [4096, 768], P(('dp', 'tensor'))
- input_grad: float32 [4096, 768], P(('dp', 'tensor'))
- qkv_grad: float32 [1, 768, 3, 768], P(None, 'dp', None, 'tensor')
- out_weight_grad: float32 [1, 768, 768], P(None, 'tensor', 'dp')
- fc_grad: float32 [1, 768, 3072], P(None, 'dp', 'tensor')
- proj_grad: float32 [1, 3072, 768], P(None, 'tensor', 'dp')
- vector_grad: float32 [1, 12, 768], P(None, None, ('dp', 'tensor'))
Inputs may be any that keep to these rules, and one draw needn't show every extreme that they name: `vectors`: gains lie near one, biases are of order 0.3.
All inputs are finite; a program needn't handle non-finite values.
Results may differ from a plain program's by a relative error of at most 0.018.
Values may be sent and summed in bfloat16 or wider, within the bound.
No kernel may reach another device: no remote copies, remote signals or barrier semaphores. Data moves between devices by JAX's collectives and lax.ppermute only.
A program may use at most 64 MiB of HBM per device.

v0:
```python
import jax
import jax.numpy as jnp
from jax import lax
from jax.sharding import PartitionSpec as P

HEAD_DIM = 64
FF = 3072
LAYERS = 1
SEQ_LEN = 256


NORM_EPS = 1e-05
GELU_COEF = 0.7978845608028654
MASK_LOW = -1000000000.0


def layer_norm(rows, gain, shift):
    mean = jnp.mean(rows, axis=-1, keepdims=True)
    centred = rows - mean
    variance = jnp.mean(centred * centred, axis=-1, keepdims=True)
    inv_std = lax.rsqrt(variance + NORM_EPS)
    normed = centred * inv_std
    return (normed * gain + shift, normed, inv_std)


def layer_norm_back(grad_out, normed, inv_std, gain):
    grad_normed = grad_out * gain
    mean_one = jnp.mean(grad_normed, axis=-1, keepdims=True)
    mean_two = jnp.mean(grad_normed * normed, axis=-1, keepdims=True)
    grad_rows = inv_std * (grad_normed - mean_one - normed * mean_two)
    return (grad_rows, jnp.sum(grad_out * normed, 0), jnp.sum(grad_out, 0))


def gelu_parts(pre):
    inner = GELU_COEF * (pre + 0.044715 * pre * pre * pre)
    tanh_val = jnp.tanh(inner)
    value = 0.5 * pre * (1.0 + tanh_val)
    slope = 0.5 * (1.0 + tanh_val) + 0.5 * pre * (1.0 - tanh_val * tanh_val) * GELU_COEF * (
        1.0 + 3.0 * 0.044715 * pre * pre
    )
    return (value, slope)


def causal_mask(length):
    rows = lax.broadcasted_iota(jnp.int32, (length, length), 0)
    cols = lax.broadcasted_iota(jnp.int32, (length, length), 1)
    return rows >= cols


def masked_scores(query, keys):
    scores = jnp.einsum(
        "qhd,khd->hqk", query, keys, preferred_element_type=jnp.float32
    ) * HEAD_DIM ** (-0.5)
    return jnp.where(causal_mask(query.shape[0])[None], scores, MASK_LOW)


def attend(operands):
    query, keys, values = operands
    scores = masked_scores(query, keys)
    top = jnp.max(scores, axis=-1, keepdims=True)
    total = jnp.sum(jnp.exp(scores - top), axis=-1, keepdims=True)
    log_total = top + jnp.log(total)
    probs = jnp.exp(scores - log_total).astype(jnp.bfloat16)
    context = jnp.einsum("hqk,khd->qhd", probs, values, preferred_element_type=jnp.float32).astype(
        jnp.bfloat16
    )
    return (context, log_total)


def attend_back(operands):
    query, keys, values, log_total, grad_ctx = operands
    probs = jnp.exp(masked_scores(query, keys) - log_total)
    probs_low = probs.astype(jnp.bfloat16)
    grad_values = jnp.einsum(
        "hqk,qhd->khd", probs_low, grad_ctx, preferred_element_type=jnp.float32
    )
    grad_probs = jnp.einsum("qhd,khd->hqk", grad_ctx, values, preferred_element_type=jnp.float32)
    row_sum = jnp.sum(probs * grad_probs, axis=-1, keepdims=True)
    grad_scores = (probs * (grad_probs - row_sum) * HEAD_DIM ** (-0.5)).astype(jnp.bfloat16)
    grad_query = jnp.einsum("hqk,khd->qhd", grad_scores, keys, preferred_element_type=jnp.float32)
    grad_keys = jnp.einsum("hqk,qhd->khd", grad_scores, query, preferred_element_type=jnp.float32)
    return (grad_query, grad_keys, grad_values)


def gather_rows(rows):
    return lax.all_gather(rows, "tensor", axis=0, tiled=True)


def sum_rows(partial_value):
    return lax.psum_scatter(
        partial_value.astype(jnp.bfloat16), "tensor", scatter_dimension=0, tiled=True
    ).astype(jnp.float32)


def gather_grads(rows):
    return lax.all_gather(rows, "tensor", axis=0, tiled=True)


def sum_input_grads(partial_value):
    return lax.psum_scatter(
        partial_value.astype(jnp.bfloat16), "tensor", scatter_dimension=0, tiled=True
    ).astype(jnp.float32)


def shards(inputs, qkv_weight, out_weight, fc_weight, proj_weight, vectors, out_grad):
    width = inputs.shape[1]
    head_cols = qkv_weight.shape[3]
    hidden_cols = fc_weight.shape[2]
    heads_here = head_cols // HEAD_DIM
    part = lax.axis_index("tensor")
    whole_vec = lax.all_gather(vectors, ("dp", "tensor"), axis=2, tiled=True)
    kept_weights = []
    resid = inputs
    layer = 0
    vec = whole_vec[layer]
    bias_q = lax.dynamic_slice_in_dim(vec[2], part * head_cols, head_cols)
    bias_v = lax.dynamic_slice_in_dim(vec[3], part * head_cols, head_cols)
    bias_fc = lax.dynamic_slice_in_dim(vec[8:].reshape(FF), part * hidden_cols, hidden_cols)
    w_qkv = lax.all_gather(qkv_weight[layer], "dp", axis=0, tiled=True)
    w_out = lax.all_gather(out_weight[layer], "dp", axis=1, tiled=True)
    w_qkv = w_qkv.reshape(width, 3 * head_cols)
    normed_out, normed1, inv1 = layer_norm(resid, vec[0], vec[1])
    a_rows = gather_rows(normed_out.astype(jnp.bfloat16))
    count = a_rows.shape[0]
    seq_count = count // SEQ_LEN
    qkv = jnp.dot(a_rows, w_qkv, preferred_element_type=jnp.float32).reshape(count, 3, head_cols)
    query = (
        (qkv[:, 0] + bias_q).astype(jnp.bfloat16).reshape(seq_count, SEQ_LEN, heads_here, HEAD_DIM)
    )
    keys = qkv[:, 1].astype(jnp.bfloat16).reshape(seq_count, SEQ_LEN, heads_here, HEAD_DIM)
    values = (
        (qkv[:, 2] + bias_v).astype(jnp.bfloat16).reshape(seq_count, SEQ_LEN, heads_here, HEAD_DIM)
    )
    context, log_total = lax.map(attend, (query, keys, values))
    ctx_flat = context.reshape(count, head_cols)
    attn_rows = sum_rows(jnp.dot(ctx_flat, w_out, preferred_element_type=jnp.float32))
    resid1 = resid + attn_rows + vec[4]
    w_fc = lax.all_gather(fc_weight[layer], "dp", axis=0, tiled=True)
    w_proj = lax.all_gather(proj_weight[layer], "dp", axis=1, tiled=True)
    normed_out2, normed2, inv2 = layer_norm(resid1, vec[5], vec[6])
    m_rows = gather_rows(normed_out2.astype(jnp.bfloat16))
    pre = jnp.dot(m_rows, w_fc, preferred_element_type=jnp.float32) + bias_fc
    act, slope = gelu_parts(pre)
    act_low = act.astype(jnp.bfloat16)
    resid = resid1 + sum_rows(jnp.dot(act_low, w_proj, preferred_element_type=jnp.float32)) + vec[7]
    saved = [
        (
            a_rows,
            normed1,
            inv1,
            query,
            keys,
            values,
            log_total,
            ctx_flat,
            normed2,
            inv2,
            m_rows,
            slope,
            act_low,
        )
    ]
    kept_weights.append((w_qkv, w_out, w_fc, w_proj))
    grad = out_grad
    qkv_list = [None] * LAYERS
    out_list = [None] * LAYERS
    fc_list = [None] * LAYERS
    proj_list = [None] * LAYERS
    vec_list = [None] * LAYERS
    for layer in reversed(range(LAYERS)):
        vec = whole_vec[layer]
        w_fc, w_proj = (
            lax.all_gather(fc_weight[layer], "dp", axis=0, tiled=True),
            lax.all_gather(proj_weight[layer], "dp", axis=1, tiled=True),
        )
        w_qkv, w_out = (
            lax.all_gather(qkv_weight[layer], "dp", axis=0, tiled=True),
            lax.all_gather(out_weight[layer], "dp", axis=1, tiled=True),
        )
        w_qkv = w_qkv.reshape(width, 3 * head_cols)
        (
            a_rows,
            normed1,
            inv1,
            query,
            keys,
            values,
            log_total,
            ctx_flat,
            normed2,
            inv2,
            m_rows,
            slope,
            act_low,
        ) = saved[layer]
        count = a_rows.shape[0]
        g_bias_proj = jnp.sum(grad, 0)
        grad_full = gather_grads(grad.astype(jnp.bfloat16))
        g_proj = jnp.dot(act_low.T, grad_full, preferred_element_type=jnp.float32)
        d_pre = jnp.dot(grad_full, w_proj.T, preferred_element_type=jnp.float32) * slope
        g_bias_fc = jnp.sum(d_pre, 0)
        d_pre_low = d_pre.astype(jnp.bfloat16)
        g_fc = jnp.dot(m_rows.T, d_pre_low, preferred_element_type=jnp.float32)
        d_m = sum_input_grads(jnp.dot(d_pre_low, w_fc.T, preferred_element_type=jnp.float32))
        d_in, g_gain2, g_shift2 = layer_norm_back(d_m, normed2, inv2, vec[5])
        grad1 = grad + d_in
        g_bias_out = jnp.sum(grad1, 0)
        grad1_full = gather_grads(grad1.astype(jnp.bfloat16))
        g_out = jnp.dot(ctx_flat.T, grad1_full, preferred_element_type=jnp.float32)
        d_ctx = jnp.dot(grad1_full, w_out.T, preferred_element_type=jnp.float32).astype(
            jnp.bfloat16
        )
        d_ctx = d_ctx.reshape(count // SEQ_LEN, SEQ_LEN, heads_here, HEAD_DIM)
        d_query, d_keys, d_values = lax.map(attend_back, (query, keys, values, log_total, d_ctx))
        d_query = d_query.reshape(count, head_cols)
        d_keys = d_keys.reshape(count, head_cols)
        d_values = d_values.reshape(count, head_cols)
        g_bias_q = jnp.sum(d_query, 0)
        g_bias_v = jnp.sum(d_values, 0)
        d_qkv = (
            jnp.stack([d_query, d_keys, d_values], axis=1)
            .astype(jnp.bfloat16)
            .reshape(count, 3 * head_cols)
        )
        g_qkv = jnp.dot(a_rows.T, d_qkv, preferred_element_type=jnp.float32).reshape(
            width, 3, head_cols
        )
        d_a = sum_input_grads(jnp.dot(d_qkv, w_qkv.T, preferred_element_type=jnp.float32))
        d_in1, g_gain1, g_shift1 = layer_norm_back(d_a, normed1, inv1, vec[0])
        grad = grad1 + d_in1
        fc_list[layer], proj_list[layer] = (
            lax.psum_scatter(g_fc, "dp", scatter_dimension=0, tiled=True),
            lax.psum_scatter(g_proj, "dp", scatter_dimension=1, tiled=True),
        )
        qkv_list[layer], out_list[layer] = (
            lax.psum_scatter(g_qkv, "dp", scatter_dimension=0, tiled=True),
            lax.psum_scatter(g_out, "dp", scatter_dimension=1, tiled=True),
        )
        zero_row = jnp.zeros((width,), jnp.float32)
        row_q = lax.dynamic_update_slice_in_dim(zero_row, g_bias_q, part * head_cols, 0)
        row_v = lax.dynamic_update_slice_in_dim(zero_row, g_bias_v, part * head_cols, 0)
        fc_rows = lax.dynamic_update_slice_in_dim(
            jnp.zeros((FF,), jnp.float32), g_bias_fc, part * hidden_cols, 0
        )
        head_rows = jnp.stack(
            [g_gain1, g_shift1, row_q, row_v, g_bias_out, g_gain2, g_shift2, g_bias_proj]
        )
        vec_list[layer] = jnp.concatenate([head_rows, fc_rows.reshape(FF // width, width)], axis=0)
    qkv_grad = jnp.stack(qkv_list)
    out_weight_grad = jnp.stack(out_list)
    fc_grad = jnp.stack(fc_list)
    proj_grad = jnp.stack(proj_list)
    vector_grad = lax.psum_scatter(
        jnp.stack(vec_list), ("dp", "tensor"), scatter_dimension=2, tiled=True
    )
    return (resid, grad, qkv_grad, out_weight_grad, fc_grad, proj_grad, vector_grad)


def solution(mesh):
    placed = (
        P(("dp", "tensor"), None),
        P(None, "dp", None, "tensor"),
        P(None, "tensor", "dp"),
        P(None, "dp", "tensor"),
        P(None, "tensor", "dp"),
        P(None, None, ("dp", "tensor")),
        P(("dp", "tensor"), None),
    )
    return jax.shard_map(
        shards,
        mesh=mesh,
        in_specs=placed,
        out_specs=(
            P(("dp", "tensor"), None),
            P(("dp", "tensor"), None),
            P(None, "dp", None, "tensor"),
            P(None, "tensor", "dp"),
            P(None, "dp", "tensor"),
            P(None, "tensor", "dp"),
            P(None, None, ("dp", "tensor")),
        ),
        check_vma=False,
    )
```

profile of v0, /device:TPU:0, one launch (start us, length us, event | category | flops | bytes accessed | tf_op | source)
XLA Modules:
  0.0 484.5 jit_solution(4905431145666434416)
XLA Ops:
  8.0 0.8 copy.66
  8.8 72.8 %all_gather.31 = f32[1,12,768]{1,0,2:T(1,128)S(1)} all-gather(f32[1,12,24]{1,0,2:T(1,128)S(1)} %copy.66), channel_id=1, replica_groups=mesh['dp'=8,'tensor'=4] {'dp','tensor'}, dimensions={2}, use_global_device_ids=true | all-gather | bytes 38016 | tf_op jit(solution)/shard_map/all_gather | solution.py:111
  81.7 14.2 %fusion.100 = (f32[1,1,768]{1,0,2:T(1,128)}, f32[1,1,768]{1,0,2:T(1,128)}, f32[768]{0:T(1024)S(1)}, f32[768]{0:T(1024)S(1)}, f32[768]{0:T(1024)S(1)}, /*index=5*...) fusion(f32[1,12,768]{1,0,2:T(1,128)S(1)} %all_gather.31), kind=kLoop, calls=%fused_computation.156 | loop fusion | bytes 49152 | tf_op jit(solution)/shard_map/slice | solution.py:116
  96.4 17.6 %all_gather.32 = bf16[512,768]{1,0:T(8,128)(2,1)} all-gather(bf16[128,768]{1,0:T(8,128)(2,1)S(1)} %add_convert_fusion.1), channel_id=1, replica_groups=mesh['dp'=8,'tensor'=4] {'tensor'}, dimensions={0}, use_global_device_ids=true | all-gather | bytes 983040 | tf_op jit(solution)/shard_map/all_gather | solution.py:86
  114.1 12.2 %all-gather = bf16[1,768,3,192]{3,2,0,1:T(4,128)(2,1)S(1)} all-gather(bf16[1,96,3,192]{3,2,0,1:T(4,128)(2,1)S(1)} %copy.67), channel_id=2, replica_groups=mesh['dp'=8,'tensor'=4] {'dp'}, dimensions={1}, use_global_device_ids=true | all-gather | bytes 995328 | tf_op jit(solution)/shard_map/all_gather | solution.py:119
  126.2 0.9 copy.68
  127.1 2.1 fusion.63
  129.6 2.0 dynamic-slice_reduce_fusion
  132.1 0.7 copy.71
  133.0 3.3 while.26
  133.1 1.2 fusion.130
  134.7 1.2 fusion.130
  136.7 9.3 %all-gather.1 = bf16[1,192,768]{1,0,2:T(2,128)(2,1)S(1)} all-gather(bf16[1,192,96]{1,0,2:T(2,128)(2,1)S(1)} %copy.73), channel_id=3, replica_groups=mesh['dp'=8,'tensor'=4] {'dp'}, dimensions={2}, use_global_device_ids=true | all-gather | bytes 331776 | tf_op jit(solution)/shard_map/all_gather | solution.py:120
  146.0 0.5 copy.74
  146.5 1.3 convolution_convert_fusion.3
  147.9 0.5 all-gather.7.cloned.1.call-update
  148.5 0.5 all-gather.9.cloned.1.call-update
  149.3 0.9 slice.70
  150.6 29.8 %all_gather.38 = bf16[512,768]{1,0:T(8,128)(2,1)} all-gather(bf16[128,768]{1,0:T(8,128)(2,1)S(1)} %get-tuple-element.209), channel_id=1, replica_groups=mesh['dp'=8,'tensor'=4] {'tensor'}, dimensions={0}, use_global_device_ids=true | all-gather | bytes 983040 | tf_op jit(solution)/shard_map/all_gather | solution.py:96
  180.4 0.5 reduce-scatter.12.cloned.1.call-done
  180.8 1.1 fusion.96
  182.3 17.8 %all_gather.35 = bf16[512,768]{1,0:T(8,128)(2,1)S(1)} all-gather(bf16[128,768]{1,0:T(8,128)(2,1)S(1)} %add_convert_fusion), channel_id=1, replica_groups=mesh['dp'=8,'tensor'=4] {'tensor'}, dimensions={0}, use_global_device_ids=true | all-gather | bytes 983040 | tf_op jit(solution)/shard_map/all_gather | solution.py:86
  200.0 3.2 convolution_add_fusion
  203.2 3.5 fusion.101
  206.8 0.9 copy-done.13
  207.7 1.7 convolution_convert_fusion.1
  209.5 3.7 convolution_convert_fusion.2
  213.3 19.0 %reduce-scatter.16.cloned.1.call-done = bf16[128,768]{1,0:T(8,128)(2,1)} async-done(((bf16[512,768]{1,0:T(8,128)(2,1)}), bf16[128,768]{1,0:T(8,128)(2,1)}) %reduce-scatter.16.cloned.1.call-update) | async-done | bytes 196624 | tf_op jit(solution)/shard_map/reduce_scatter | solution.py:100
  232.3 1.2 fusion.84
  233.5 23.7 %reduce-scatter.14.cloned.1.call-done = bf16[128,768]{1,0:T(8,128)(2,1)} async-done(((bf16[512,768]{1,0:T(8,128)(2,1)}), bf16[128,768]{1,0:T(8,128)(2,1)}) %reduce-scatter.14.cloned.1.call-update) | async-done | bytes 196624 | tf_op jit(solution)/shard_map/reduce_scatter | solution.py:90
  257.2 1.9 fusion.94
  259.2 18.0 %all_gather.39 = bf16[512,768]{1,0:T(8,128)(2,1)S(1)} all-gather(bf16[128,768]{1,0:T(8,128)(2,1)S(1)} %convert_element_type.94), channel_id=1, replica_groups=mesh['dp'=8,'tensor'=4] {'tensor'}, dimensions={0}, use_global_device_ids=true | all-gather | bytes 983040 | tf_op jit(solution)/shard_map/all_gather | solution.py:96
  277.2 0.4 convolution_convert_fusion.4
  277.6 1.3 convolution_bitcast_fusion.3
  279.1 19.8 %while.27 = (s32[]{:T(128)}, f32[2,256,3,64]{1,3,2,0:T(8,128)}, bf16[2,256,3,64]{1,0,3,2:T(2,128)(2,1)}, f32[2,256,3,64]{1,3,2,0:T(8,128)}, bf16[2,256,3,64]{1,3...) while((s32[]{:T(128)}, f32[2,256,3,64]{1,3,2,0:T(8,128)}, ...), condition=%wide.region_15.16_spmd, body=%wide.region_13.15_spmd.sunk | while | flops 128649216 | bytes 11942065 | solution.py:214
  279.1 1.3 fusion.142
  280.8 0.4 convolution_bitcast_fusion.5
  281.3 4.8 dynamic_update_slice.45
  286.0 1.9 fusion.144
  288.0 1.0 fusion.145
  289.0 1.3 fusion.142
  290.6 0.4 convolution_bitcast_fusion.5
  291.2 4.8 dynamic_update_slice.45
  295.9 1.9 fusion.144
  297.9 0.9 fusion.145
  298.8 1.4 copy.80
  300.4 1.3 copy.78
  302.0 1.8 bitcast_convert_fusion
  303.9 2.2 fusion.88
  306.2 1.1 copy-done.12
  307.2 0.5 copy-done.19
  307.7 2.4 fusion.93
  310.4 0.8 copy-done.5
  311.3 2.3 fusion.66
  313.9 0.6 copy-done.8
  315.4 1.6 copy.90
  317.0 21.7 %reduce-scatter.18.cloned.1.call-done = bf16[128,768]{1,0:T(8,128)(2,1)} async-done(((bf16[512,768]{1,0:T(8,128)(2,1)}), bf16[128,768]{1,0:T(8,128)(2,1)}) %reduce-scatter.18.cloned.1.call-update) | async-done | bytes 196624 | tf_op jit(solution)/shard_map/reduce_scatter | solution.py:100
  338.7 1.2 fusion.85
  340.0 39.0 %all-reduce = f32[1,12,768]{2,0,1:T(1,128)S(1)} all-reduce(f32[1,12,768]{2,0,1:T(1,128)S(1)} %stack.55), channel_id=14, replica_groups=mesh['dp'=8,'tensor'=4] {'dp','tensor'}, use_global_device_ids=true, to_apply=%region_32.33.clone | all-reduce | flops 9216 | bytes 73728
  379.0 0.7 constant_dynamic-slice_fusion
  379.7 1.8 fusion.78
  381.5 3.0 reduce-scatter.22.cloned.1.call-done
  384.6 46.7 %reduce-scatter.24.cloned.1.call-done = f32[768,96]{0,1:T(8,128)} async-done(((f32[768,768]{0,1:T(8,128)}), f32[768,96]{0,1:T(8,128)}) %reduce-scatter.24.cloned.1.call-update) | async-done | bytes 294928 | tf_op jit(solution)/shard_map/reduce_scatter | solution.py:233
  431.2 46.1 %reduce-scatter.20.cloned.1.call-done = f32[96,3,192]{2,0,1:T(8,128)} async-done(((f32[768,3,192]{2,0,1:T(8,128)}), f32[96,3,192]{2,0,1:T(8,128)}) %reduce-scatter.20.cloned.1.call-update) | async-done | bytes 221200 | tf_op jit(solution)/shard_map/reduce_scatter | solution.py:236
  (136 shorter events, 7.2 us)
Async XLA Ops:
  8.0 172.8 %reduce-scatter.12.cloned.1.call-start = ((), (), s32[]{:S(2)}) async-start(), calls=%async_computation.8 | async-start | bytes 983040 | tf_op jit(solution)/shard_map/reduce_scatter | solution.py:90
  81.6 14.2 %copy-start = (f32[128,768]{1,0:T(8,128)S(1)}, f32[128,768]{1,0:T(8,128)}, u32[]{:S(2)}) copy-start(f32[128,768]{1,0:T(8,128)} %param.11) | copy-start | bytes 1179652
  95.9 18.1 %copy-start.16 = (bf16[1,96,3,192]{3,1,2,0:T(8,128)(2,1)S(1)}, bf16[1,96,3,192]{3,1,2,0:T(8,128)(2,1)}, u32[]{:S(2)}) copy-start(bf16[1,96,3,192]{3,1,2,0:T(8,128)(2,1)} %param.12) | copy-start | bytes 331780
  127.1 2.2 copy-start.1
  133.0 3.6 copy-start.17
  146.0 3.2 copy-start.10
  147.9 52.2 %all-gather.7.cloned.1.call-start = ((), (), s32[]{:S(2)}) async-start(), calls=%async_computation.15 | async-start | bytes 1327104 | tf_op jit(solution)/shard_map/all_gather | solution.py:138
  148.4 54.8 %all-gather.9.cloned.1.call-start = ((), (), s32[]{:S(2)}) async-start(), calls=%async_computation.16 | async-start | bytes 1327104 | tf_op jit(solution)/shard_map/all_gather | solution.py:139
  149.0 83.3 %reduce-scatter.16.cloned.1.call-start = ((), (), s32[]{:S(2)}) async-start(), calls=%async_computation.10 | async-start | bytes 983040 | tf_op jit(solution)/shard_map/reduce_scatter | solution.py:100
  203.2 4.4 copy-start.18
  206.8 0.9 copy-start.13
  209.4 47.8 %reduce-scatter.14.cloned.1.call-start = ((), (), s32[]{:S(2)}) async-start(), calls=%async_computation.9 | async-start | bytes 983040 | tf_op jit(solution)/shard_map/reduce_scatter | solution.py:90
  213.2 44.0 %copy-start.11 = (f32[128,768]{1,0:T(8,128)S(1)}, f32[128,768]{1,0:T(8,128)}, u32[]{:S(2)}) copy-start(f32[128,768]{1,0:T(8,128)} %param.17) | copy-start | bytes 1179652
  213.2 102.2 %reduce-scatter.26.cloned.1.call-start = ((), (), s32[]{:S(2)}) async-start(), calls=%async_computation.17 | async-start | bytes 884736
  259.1 19.7 %copy-start.3 = (f32[128,768]{1,0:T(8,128)}, f32[128,768]{1,0:T(8,128)S(1)}, u32[]{:S(2)}) copy-start(f32[128,768]{1,0:T(8,128)S(1)} %get-tuple-element.201) | copy-start | bytes 1179652
  279.0 59.7 %reduce-scatter.18.cloned.1.call-start = ((), (), s32[]{:S(2)}) async-start(), calls=%async_computation.11 | async-start | bytes 983040 | tf_op jit(solution)/shard_map/reduce_scatter | solution.py:100
  279.1 1.7 copy-start.6
  286.0 2.9 copy-start.7
  288.9 1.7 copy-start.6
  295.9 2.9 copy-start.7
  298.8 3.0 copy-start.15
  298.8 3.1 copy-start.2
  302.0 1.9 copy-start.14
  303.8 80.8 %reduce-scatter.22.cloned.1.call-start = ((), (), s32[]{:S(2)}) async-start(), calls=%async_computation.13 | async-start | bytes 2654208 | tf_op jit(solution)/shard_map/reduce_scatter | solution.py:232
  306.1 1.1 copy-start.12
  306.1 1.7 copy-start.19
  306.1 125.1 %reduce-scatter.24.cloned.1.call-start = ((), (), s32[]{:S(2)}) async-start(), calls=%async_computation.14 | async-start | bytes 2654208 | tf_op jit(solution)/shard_map/reduce_scatter | solution.py:233
  310.1 1.1 copy-start.5
  310.2 167.2 %reduce-scatter.20.cloned.1.call-start = ((), (), s32[]{:S(2)}) async-start(), calls=%async_computation.12 | async-start | bytes 2654208 | tf_op jit(solution)/shard_map/reduce_scatter | solution.py:236
  313.5 1.0 copy-start.8
  313.5 1.2 copy-start.9
  313.6 66.1 %copy-start.4 = (f32[128,768]{1,0:T(8,128)S(1)}, f32[128,768]{1,0:T(8,128)}, u32[]{:S(2)}) copy-start(f32[128,768]{1,0:T(8,128)} %copy-done.3) | copy-start | bytes 1179652
Sparse Core Ops, SparseCore 0:
  148.0 32.8 reduce-scatter.11
  209.5 22.6 reduce-scatter.15
  234.6 22.5 reduce-scatter.13
Sparse Core Ops, SparseCore 1:
  150.2 21.6 all-gather.6
  173.6 23.9 all-gather.8
  279.1 34.2 reduce-scatter.25
  315.7 23.0 reduce-scatter.17
  342.6 41.9 reduce-scatter.21
  388.9 42.3 reduce-scatter.23
  435.0 42.3 reduce-scatter.19
where the time goes:
time: 486 us; the launch traced here: 484 us
  blocking collectives  216 us (44%)
  waiting for transfers between devices  162 us (33%)
  local copies, waits for them, and re-layouts  41.8 us (9%)
  matrix products  38.7 us (8%)
  between operations  15.8 us (3%)
  other arithmetic  8.88 us (2%)
    all_gather x1, blocking collectives, shards(): whole_vec = lax.all_gather(vectors, ('dp', 'tensor'), axis=2, tiled=True)  72.8 us
    all_gather x2, blocking collectives, gather_grads(): return lax.all_gather(rows, 'tensor', axis=0, tiled=True)  47.8 us
    reduce_scatter x1, waiting for transfers between devices, shards(): lax.psum_scatter(g_proj, 'dp', scatter_dimension=1, tiled=True)  46.7 us
    reduce_scatter x1, waiting for transfers between devices, shards(): lax.psum_scatter(g_qkv, 'dp', scatter_dimension=0, tiled=True)  46.1 us
    reduce_scatter x2, waiting for transfers between devices, sum_input_grads(): lax.psum_scatter(partial_value.astype(jnp.bfloat16), 'tensor', scatter_di...  40.7 us
    unnamed x1, blocking collectives  39 us
    all_gather x2, blocking collectives, gather_rows(): return lax.all_gather(rows, 'tensor', axis=0, tiled=True)  35.3 us
    reduce_scatter x2, waiting for transfers between devices, sum_rows(): lax.psum_scatter(partial_value.astype(jnp.bfloat16), 'tensor', scatter_di...  24.2 us
  transfers between devices with their start and end apart: 10, of which 7 were waited for; matrix products, arithmetic and copies ran while one was open for 10% of the time, Pallas kernels for 0%

commit v1 on v0

v1 whole, which is shorter than its diff:
```python
import jax
import jax.numpy as jnp
from jax import lax
from jax.experimental import pallas as pl
from jax.experimental.pallas import tpu as pltpu
from jax.sharding import PartitionSpec as P

HEAD_DIM = 64
NORM_EPS = 1e-05
GELU_COEF = 0.7978845608028654
MASK_LOW = -1000000000.0
SCALE = HEAD_DIM ** (-0.5)
BF16 = jnp.bfloat16
F32 = jnp.float32
NN = ((1,), (0,))
NT = ((1,), (1,))
TN = ((0,), (0,))


def dot(a, b, dims=NN):
    return lax.dot_general(a, b, (dims, ((), ())), preferred_element_type=F32)


def swap(value, axis, bits):
    size = lax.axis_size(axis)
    return lax.ppermute(value, axis, [(i, i ^ bits) for i in range(size)])


def normalize(rows):
    mean = jnp.mean(rows, axis=-1, keepdims=True)
    centred = rows - mean
    variance = jnp.mean(centred * centred, axis=-1, keepdims=True)
    inv_std = lax.rsqrt(variance + NORM_EPS)
    return (centred * inv_std, inv_std)


def norm_back(grad_out, normed, inv_std, gain):
    grad_normed = grad_out * gain
    mean_one = jnp.mean(grad_normed, axis=-1, keepdims=True)
    mean_two = jnp.mean(grad_normed * normed, axis=-1, keepdims=True)
    return inv_std * (grad_normed - mean_one - normed * mean_two)


def gelu_parts(pre):
    square = pre * pre
    inner = GELU_COEF * (pre + 0.044715 * square * pre)
    tanh_val = jnp.tanh(inner)
    half = 0.5 * (1.0 + tanh_val)
    value = pre * half
    slope = half + 0.5 * pre * (1.0 - tanh_val * tanh_val) * GELU_COEF * (
        1.0 + 3.0 * 0.044715 * square
    )
    return (value, slope)


def column_sum(value):
    return jnp.sum(value, axis=0, keepdims=True)


def call(body, name, outs, args, scratch=(), spaces=None):
    spaces = spaces or {}
    in_specs = [
        pl.BlockSpec(memory_space=spaces.get(n, pltpu.VMEM)) for n in range(len(args))
    ]
    return pl.pallas_call(
        body,
        name=name,
        out_shape=[jax.ShapeDtypeStruct(shape, dtype) for shape, dtype in outs],
        in_specs=in_specs,
        out_specs=[pl.BlockSpec(memory_space=pltpu.VMEM) for _ in outs],
        scratch_shapes=list(scratch),
        compiler_params=pltpu.CompilerParams(vmem_limit_bytes=56 * 1024 * 1024),
    )(*args)


def bit_orders():
    count = lax.axis_size("dp").bit_length() - 1
    bits = [1 << b for b in range(1, count)]
    return (bits + [1], bits[::-1] + [1])


def gather_pieces(piece):
    shards_held = []
    for value, order in zip((piece[None], swap(piece[None], "tensor", 2)), bit_orders()):
        held = [((0,), value)]
        for bit in order:
            while len(held) > 4:
                held = [
                    (held[n][0] + held[n + 1][0], jnp.concatenate([held[n][1], held[n + 1][1]]))
                    for n in range(0, len(held), 2)
                ]
            held = held + [
                (tuple(k ^ bit for k in ks), swap(v, "dp", bit)) for ks, v in held
            ]
        shards_held.append(held)
    return shards_held


def assembled(held):
    ks = [k for group, _ in held for k in group]
    stacked = jnp.concatenate([v for _, v in held])
    slot = [ks.index(k) for k in range(len(ks))]
    stacked = jnp.stack([stacked[n] for n in slot])
    whole = jnp.take(stacked, lax.axis_index("dp") ^ jnp.arange(len(ks)), axis=0)
    return whole.reshape(1, -1, whole.shape[-1])


def piece_plan(pieces):
    aligned = pieces[0][0][1].shape[1] % 16 == 0
    arrays, plan = [], []
    for s, held in enumerate(pieces):
        if not aligned:
            plan.append((len(arrays), 0, s, None))
            arrays.append(assembled(held))
            continue
        for ks, value in held:
            plan += [(len(arrays), slot, s, k) for slot, k in enumerate(ks)]
            arrays.append(value)
    return arrays, plan


def place_pieces(refs, plan, dst_ref, sems, me):
    copies = []
    for n, (array, slot, s, k) in enumerate(plan):
        rows = refs[array].shape[1]
        if k is None:
            target = dst_ref.at[s]
        else:
            start = pl.multiple_of(jnp.bitwise_xor(me, k) * rows, 16)
            target = dst_ref.at[s, pl.ds(start, rows), :]
        copies.append(pltpu.make_async_copy(refs[array].at[slot], target, sems.at[n]))
    for copy in copies:
        copy.start()
    return copies


def relative_evens(shard):
    count = lax.axis_size("dp")
    bits = count.bit_length() - 1
    evens = list(range(0, count, 2))
    if shard == 1:
        evens.sort(key=lambda k: [k >> b & 1 for b in range(1, bits)])
    return evens


def put_grad(grad, s, scratch, keep_ref, send_ref, me, rows):
    if rows % 16:
        keep_ref[...] = grad
        return
    scratch[...] = grad
    for n, k in enumerate(relative_evens(s)):
        for k_of, ref in ((k, keep_ref), (k ^ 1, send_ref)):
            start = pl.multiple_of(jnp.bitwise_xor(me, k_of) * rows, 16)
            ref[n] = scratch[pl.ds(start, rows), :].astype(ref.dtype)


def grad_shapes(width, rows, cols):
    if rows % 16:
        return [((width, cols), F32), ((8, 128), BF16)] * 2
    half = width // rows // 2
    return [((half, rows, cols), F32), ((half, rows, cols), BF16)] * 2


def scatter_grad(parts, rows):
    sums = []
    me = lax.axis_index("dp")
    for s in range(2):
        keep, send = parts[2 * s : 2 * s + 2]
        if rows % 16:
            blocks = keep.reshape(-1, rows, keep.shape[-1])
            evens = jnp.array(relative_evens(s))
            keep = jnp.take(blocks, me ^ evens, axis=0)
            send = jnp.take(blocks, me ^ evens ^ 1, axis=0).astype(BF16)
        now = keep + swap(send, "dp", 1).astype(F32)
        for bit in bit_orders()[s][:-1][::-1]:
            half = now.shape[0] // 2
            sent = now[half:].astype(BF16)
            now = now[:half] + swap(sent, "dp", bit).astype(F32)
        sums.append(now[0])
    return sums[0] + swap(sums[1].astype(BF16), "tensor", 2).astype(F32)


def gather_vectors(value, index, count):
    rows, cols = value.shape
    spread = lax.dynamic_update_slice(jnp.zeros((rows, count * cols), F32), value, (0, index * cols))
    return sum_everywhere(spread)


def sum_everywhere(value):
    for bit in bit_orders()[0][::-1]:
        value = value + swap(value, "dp", bit)
    value = value + swap(value, "tensor", 2)
    return value + swap(value, "tensor", 1)


def norm_first_body(x_ref, g_ref, xh_ref, dy_ref, sum_ref):
    xh_ref[...] = normalize(x_ref[...])[0].astype(BF16)
    grad = g_ref[...]
    dy_ref[...] = grad.astype(BF16)
    sum_ref[...] = column_sum(grad)


def causal_mask(length):
    rows = lax.broadcasted_iota(jnp.int32, (length, length), 0)
    cols = lax.broadcasted_iota(jnp.int32, (length, length), 1)
    return rows >= cols


def attend_body(plan, n_arrays, head_cols, *refs):
    ids, own, other, vec, biases = refs[:5]
    pieces = refs[5 : 5 + n_arrays]
    w, qkv_out, ctx_out, lse_out, a_out, keep, send, total, sems = refs[5 + n_arrays :]
    me, role = ids[0], ids[1]
    copies = place_pieces(pieces, plan, w, sems, me)
    rows = own.shape[0]
    gain, shift = vec[0:1, :], vec[1:2, :]
    for ref, at in ((own, role), (other, 1 - role)):
        a_rows = ref[...].astype(F32) * gain + shift
        a_out[pl.ds(pl.multiple_of(at * rows, rows), rows), :] = a_rows.astype(BF16)
    for copy in copies:
        copy.wait()
    seq = 2 * rows
    a_rows = a_out[...]
    mask = causal_mask(seq)
    lane = lax.broadcasted_iota(jnp.int32, (seq, 128), 1)
    lse_all = jnp.zeros((seq, 128), F32)
    heads = head_cols // HEAD_DIM
    attn = None
    for s in range(2):
        qkv = dot(a_rows, w[s, :, : 3 * head_cols]) + biases[s : s + 1, :]
        qkv = qkv.astype(BF16)
        qkv_out[s] = qkv
        parts = []
        for h in range(heads):
            q, k, v = (
                qkv[:, n * head_cols + h * HEAD_DIM : n * head_cols + (h + 1) * HEAD_DIM]
                for n in range(3)
            )
            scores = jnp.where(mask, dot(q, k, NT) * SCALE, MASK_LOW)
            top = jnp.max(scores, axis=-1, keepdims=True)
            lse = top + jnp.log(jnp.sum(jnp.exp(scores - top), axis=-1, keepdims=True))
            lse_all = jnp.where(lane == s * heads + h, lse, lse_all)
            probs = jnp.exp(scores - lse).astype(BF16)
            parts.append(dot(probs, v).astype(BF16))
        ctx = jnp.concatenate(parts, axis=1)
        ctx_out[s] = ctx
        add = dot(ctx, w[s, :, 3 * head_cols :], NT)
        attn = add if attn is None else attn + add
    lse_out[...] = lse_all
    total[...] = attn
    keep[...] = total[pl.ds(pl.multiple_of(role * rows, rows), rows), :]
    send[...] = total[pl.ds(pl.multiple_of((1 - role) * rows, rows), rows), :].astype(BF16)


def norm_second_body(x_ref, keep_ref, recv_ref, vec_ref, resid_ref, m_ref):
    resid = x_ref[...] + (keep_ref[...] + recv_ref[...].astype(F32)) + vec_ref[4:5, :]
    resid_ref[...] = resid
    normed, _ = normalize(resid)
    m_ref[...] = (normed * vec_ref[5:6, :] + vec_ref[6:7, :]).astype(BF16)


def feed_body(plan, n_arrays, hidden, *refs):
    ids, m_own, m_other, dy_own, dy_other, bias = refs[:6]
    pieces = refs[6 : 6 + n_arrays]
    m_out, dy_out, act_out, dpre_out, dm_keep, dm_send, br_keep, br_send, sum_out, w, sems = refs[
        6 + n_arrays :
    ]
    copies = place_pieces(pieces, plan, w, sems, ids[0])
    rows = m_own.shape[0]
    m_out[:rows] = m_own[...]
    m_out[rows:] = m_other[...]
    dy_out[:rows] = dy_own[...]
    dy_out[rows:] = dy_other[...]
    m, dy = m_out[...], dy_out[...]
    for copy in copies:
        copy.wait()
    d_m = branch = None
    for s in range(2):
        w_fc, w_proj = w[s, :, :hidden], w[s, :, hidden:]
        pre = dot(m, w_fc) + bias[s : s + 1, :]
        act, slope = gelu_parts(pre)
        act_low = act.astype(BF16)
        act_out[s] = act_low
        d_pre = dot(dy, w_proj) * slope
        sum_out[s : s + 1, :] = column_sum(d_pre)
        d_pre_low = d_pre.astype(BF16)
        dpre_out[s] = d_pre_low
        one, two = dot(d_pre_low, w_fc, NT), dot(act_low, w_proj, NT)
        d_m = one if d_m is None else d_m + one
        branch = two if branch is None else branch + two
    dm_keep[...] = d_m[:rows]
    dm_send[...] = d_m[rows:].astype(BF16)
    br_keep[...] = branch[:rows]
    br_send[...] = branch[rows:].astype(BF16)


def feed_grad_body(block_rows, hidden, ids, m_ref, dy_ref, act_ref, dpre_ref, *refs):
    outs, scratch = refs[:4], refs[4]
    for s in range(2):
        grad = jnp.concatenate(
            [dot(m_ref[...], dpre_ref[s], TN), dot(dy_ref[...], act_ref[s], TN)], axis=1
        )
        put_grad(grad, s, scratch, outs[2 * s], outs[2 * s + 1], ids[0], block_rows)


def norm_second_back_body(resid_ref, keep_ref, recv_ref, grad_ref, vec_ref, grad1_ref, dz_ref, sum_ref):
    d_m = keep_ref[...] + recv_ref[...].astype(F32)
    normed, inv = normalize(resid_ref[...])
    grad1 = grad_ref[...] + norm_back(d_m, normed, inv, vec_ref[5:6, :])
    grad1_ref[...] = grad1
    dz_ref[...] = grad1.astype(BF16)
    sum_ref[0:1, :] = column_sum(grad1)
    sum_ref[1:2, :] = column_sum(d_m * normed)
    sum_ref[2:3, :] = column_sum(d_m)


def attend_back_body(head_cols, ids, own, other, xh_own, xh_other, w, qkv_ref, lse_ref, *refs):
    dz_out, dqkv_out, keep, send, sum_wide, sum_heads, total, normed = refs
    role = ids[1]
    rows = own.shape[0]
    seq = 2 * rows
    for ref, to, kind in ((own, dz_out, 0), (other, dz_out, 1), (xh_own, normed, 0), (xh_other, normed, 1)):
        at = role if kind == 0 else 1 - role
        to[pl.ds(pl.multiple_of(at * rows, rows), rows), :] = ref[...]
    dz = dz_out[...]
    mask = causal_mask(seq)
    heads = head_cols // HEAD_DIM
    d_a = None
    for s in range(2):
        d_ctx_all = dot(dz, w[s, :, 3 * head_cols :]).astype(BF16)
        d_parts = [[], [], []]
        qkv = qkv_ref[s]
        for h in range(heads):
            q, k, v = (
                qkv[:, n * head_cols + h * HEAD_DIM : n * head_cols + (h + 1) * HEAD_DIM]
                for n in range(3)
            )
            d_ctx = d_ctx_all[:, h * HEAD_DIM : (h + 1) * HEAD_DIM]
            head = s * heads + h
            scores = jnp.where(mask, dot(q, k, NT) * SCALE, MASK_LOW)
            probs = jnp.exp(scores - lse_ref[:, head : head + 1])
            d_parts[2].append(dot(probs.astype(BF16), d_ctx, TN))
            d_probs = dot(d_ctx, v, NT)
            row_sum = jnp.sum(probs * d_probs, axis=-1, keepdims=True)
            d_scores = (probs * (d_probs - row_sum) * SCALE).astype(BF16)
            d_parts[0].append(dot(d_scores, k))
            d_parts[1].append(dot(d_scores, q, TN))
        d_qkv = jnp.concatenate(d_parts[0] + d_parts[1] + d_parts[2], axis=1)
        sum_heads[s : s + 1, :] = column_sum(d_qkv)
        d_qkv = d_qkv.astype(BF16)
        dqkv_out[s] = d_qkv
        add = dot(d_qkv, w[s, :, : 3 * head_cols], NT)
        d_a = add if d_a is None else d_a + add
    total[...] = d_a
    sum_wide[0:1, :] = column_sum(d_a * normed[...].astype(F32))
    sum_wide[1:2, :] = column_sum(d_a)
    keep[...] = total[pl.ds(pl.multiple_of(role * rows, rows), rows), :]
    send[...] = total[pl.ds(pl.multiple_of((1 - role) * rows, rows), rows), :].astype(BF16)


def attend_grad_body(block_rows, head_cols, ids, a_ref, dz_ref, dqkv_ref, ctx_ref, *refs):
    wide, heads_sum, second, fc_sum, bp_sum = refs[:5]
    outs, vec_out, scratch = refs[5:9], refs[9], refs[10]
    z = ids[2]
    for s in range(2):
        grad = jnp.concatenate(
            [dot(a_ref[...], dqkv_ref[s], TN), dot(dz_ref[...], ctx_ref[s], TN)], axis=1
        )
        put_grad(grad, s, scratch, outs[2 * s], outs[2 * s + 1], ids[0], block_rows)
    vec_out[0:2, :] = wide[0:2, :]
    vec_out[4:7, :] = second[0:3, :]
    vec_out[7:8, :] = bp_sum[...]

    def placed(value, t):
        here = jnp.where(z == t, value[0:1, :], jnp.zeros_like(value[0:1, :]))
        return here + jnp.where(jnp.bitwise_xor(z, 2) == t, value[1:2, :], jnp.zeros_like(here))

    sums = heads_sum[...]
    n_z = vec_out.shape[1] // head_cols
    for row, part in ((2, 0), (3, 2)):
        value = sums[:, part * head_cols : (part + 1) * head_cols]
        vec_out[row : row + 1, :] = jnp.concatenate([placed(value, t) for t in range(n_z)], axis=1)
    for t in range(vec_out.shape[0] - 8):
        vec_out[8 + t : 9 + t, :] = placed(fc_sum[...], t)


def norm_first_back_body(x_ref, keep_ref, recv_ref, grad1_ref, vec_ref, out_ref):
    d_a = keep_ref[...] + recv_ref[...].astype(F32)
    normed, inv = normalize(x_ref[...])
    out_ref[...] = grad1_ref[...] + norm_back(d_a, normed, inv, vec_ref[0:1, :])


def shards(inputs, qkv_weight, out_weight, fc_weight, proj_weight, vectors, out_grad):
    rows, width = inputs.shape
    head_cols = qkv_weight.shape[3]
    hidden = fc_weight.shape[2]
    block_rows = qkv_weight.shape[1]
    vec_rows, vec_cols = vectors.shape[1:]
    n_z = lax.axis_size("tensor")
    n_dp = lax.axis_size("dp")
    z = lax.axis_index("tensor")
    me = lax.axis_index("dp")
    shard_ids = (z, z ^ 2)
    ids = jnp.stack([me, z & 1, z]).astype(jnp.int32)
    smem = {0: pltpu.SMEM}
    row = (rows, width)
    seq = 2 * rows
    both = (seq, width)

    part_a = jnp.concatenate(
        [qkv_weight[0].reshape(block_rows, 3 * head_cols), out_weight[0].T], axis=1
    )
    part_b = jnp.concatenate([fc_weight[0], proj_weight[0].T], axis=1)
    normed1, dy, bp_sum = call(
        norm_first_body, "norm_first", [(row, BF16), (row, BF16), ((1, width), F32)], (inputs, out_grad)
    )
    normed1_other = swap(normed1, "tensor", 1)
    arrays_a, plan_a = piece_plan(gather_pieces(part_a))
    vec = gather_vectors(vectors[0], me * n_z + z, n_dp * n_z)
    dy_other = swap(dy, "tensor", 1)
    arrays_b, plan_b = piece_plan(gather_pieces(part_b))

    def of_shard(table):
        return jnp.stack([lax.dynamic_index_in_dim(table, s, 0, False) for s in shard_ids])

    bias_q = of_shard(vec[2].reshape(n_z, head_cols))
    bias_v = of_shard(vec[3].reshape(n_z, head_cols))
    biases = jnp.concatenate([bias_q, jnp.zeros_like(bias_q), bias_v], axis=1)
    bias_fc = of_shard(vec[8:].reshape(n_z, hidden))

    def any_space(first, arrays):
        return {**smem, **{first + n: pl.ANY for n in range(len(arrays))}}

    w_a, qkv, ctx, lse, a_seq, attn_keep, attn_send = call(
        lambda *refs: attend_body(plan_a, len(arrays_a), head_cols, *refs),
        "attend",
        [
            ((2, width, 4 * head_cols), BF16),
            ((2, seq, 3 * head_cols), BF16),
            ((2, seq, head_cols), BF16),
            ((seq, 128), F32),
            (both, BF16),
            (row, F32),
            (row, BF16),
        ],
        (ids, normed1, normed1_other, vec, biases, *arrays_a),
        [pltpu.VMEM(both, F32), pltpu.SemaphoreType.DMA((len(plan_a),))],
        any_space(5, arrays_a),
    )
    resid1, m = call(
        norm_second_body,
        "norm_second",
        [(row, F32), (row, BF16)],
        (inputs, attn_keep, swap(attn_send, "tensor", 1), vec),
    )
    m_other = swap(m, "tensor", 1)
    m_both, dy_both, act, d_pre, dm_keep, dm_send, br_keep, br_send, fc_sum = call(
        lambda *refs: feed_body(plan_b, len(arrays_b), hidden, *refs),
        "feed",
        [
            (both, BF16),
            (both, BF16),
            ((2, seq, hidden), BF16),
            ((2, seq, hidden), BF16),
            (row, F32),
            (row, BF16),
            (row, F32),
            (row, BF16),
            ((2, hidden), F32),
        ],
        (ids, m, m_other, dy, dy_other, bias_fc, *arrays_b),
        [pltpu.VMEM((2, width, 2 * hidden), BF16), pltpu.SemaphoreType.DMA((len(plan_b),))],
        any_space(6, arrays_b),
    )
    dm_recv = swap(dm_send, "tensor", 1)
    parts_b = call(
        lambda *refs: feed_grad_body(block_rows, hidden, *refs),
        "feed_grad",
        grad_shapes(width, block_rows, 2 * hidden),
        (ids, m_both, dy_both, act, d_pre),
        [pltpu.VMEM((width, 2 * hidden), F32)],
        smem,
    )
    grad1, dz, second_sums = call(
        norm_second_back_body,
        "norm_second_back",
        [(row, F32), (row, BF16), ((3, width), F32)],
        (resid1, dm_keep, dm_recv, out_grad, vec),
    )
    dz_other = swap(dz, "tensor", 1)
    outputs = resid1 + (br_keep + swap(br_send, "tensor", 1).astype(F32)) + vec[7]
    b_grad = scatter_grad(parts_b, block_rows)
    dz_seq, d_qkv, da_keep, da_send, wide_sums, head_sums = call(
        lambda *refs: attend_back_body(head_cols, *refs),
        "attend_back",
        [
            (both, BF16),
            ((2, seq, 3 * head_cols), BF16),
            (row, F32),
            (row, BF16),
            ((2, width), F32),
            ((2, 3 * head_cols), F32),
        ],
        (ids, dz, dz_other, normed1, normed1_other, w_a, qkv, lse),
        [pltpu.VMEM(both, F32), pltpu.VMEM(both, BF16)],
        smem,
    )
    da_recv = swap(da_send, "tensor", 1)
    *parts_a, vec_sum = call(
        lambda *refs: attend_grad_body(block_rows, head_cols, *refs),
        "attend_grad",
        grad_shapes(width, block_rows, 4 * head_cols) + [((vec_rows, width), F32)],
        (ids, a_seq, dz_seq, d_qkv, ctx, wide_sums, head_sums, second_sums, fc_sum, bp_sum),
        [pltpu.VMEM((width, 4 * head_cols), F32)],
        smem,
    )
    a_grad = scatter_grad(parts_a, block_rows)
    vec_sum = sum_everywhere(vec_sum)
    vector_grad = lax.dynamic_slice_in_dim(vec_sum, (me * n_z + z) * vec_cols, vec_cols, 1)
    (input_grad,) = call(
        norm_first_back_body,
        "norm_first_back",
        [(row, F32)],
        (inputs, da_keep, da_recv, grad1, vec),
    )
    qkv_grad = a_grad[:, : 3 * head_cols].reshape(block_rows, 3, head_cols)
    return (
        outputs,
        input_grad,
        qkv_grad[None],
        a_grad[:, 3 * head_cols :].T[None],
        b_grad[None, :, :hidden],
        b_grad[:, hidden:].T[None],
        vector_grad[None],
    )


def solution(mesh):
    rows = P(("dp", "tensor"), None)
    weights = (
        P(None, "dp", None, "tensor"),
        P(None, "tensor", "dp"),
        P(None, "dp", "tensor"),
        P(None, "tensor", "dp"),
        P(None, None, ("dp", "tensor")),
    )
    return jax.shard_map(
        shards,
        mesh=mesh,
        in_specs=(rows, *weights, rows),
        out_specs=(rows, rows, *weights),
        check_vma=False,
    )
```

time: 486 us -> 209 us (0.43)
  blocking collectives: 216 us -> 0 us
  waiting for transfers between devices: 162 us -> 97 us
  starting transfers between devices: 0.83 us -> 52.2 us
  Pallas kernels: 0 us -> 41 us
  matrix products: 38.7 us -> 0 us
  local copies, waits for them, and re-layouts: 41.8 us -> 11.5 us
  between operations: 15.8 us -> 1.39 us
    all_gather x7 -> x0, blocking collectives: 177 us -> none  [the longest x1 72.8 us: shards(): whole_vec = lax.all_gather(vectors, ('dp', 'tensor'), axis=2, tiled=True)]
    reduce_scatter x7 -> x0, waiting for transfers between devices: 161 us -> none  [the longest x1 46.7 us: shards(): lax.psum_scatter(g_proj, 'dp', scatter_dimension=1, tiled=True)]
    ppermute x0 -> x62, waiting for transfers between devices: none -> 97 us  [swap(): return lax.ppermute(value, axis, [(i, i ^ bits) for i in range(size)])]
    ppermute x0 -> x62, starting transfers between devices: none -> 52.2 us  [swap(): return lax.ppermute(value, axis, [(i, i ^ bits) for i in range(size)])]
    pallas_call x0 -> x9, Pallas kernels: none -> 41 us  [call(): pl.pallas_call(body, name=name, out_shape=[jax.ShapeDtypeStruct(shape, dt...]
    unnamed x1 -> x0, blocking collectives: 39 us -> none
    dot_general x25 -> x0, matrix products: 37.3 us -> none  [the longest x4 5.05 us: masked_scores(): jnp.einsum('qhd,khd->hqk', query, keys, preferred_element_type=jnp.float32)]
    slice x5 -> x12, local copies, waits for them, and re-layouts: 15.4 us -> 1.22 us  [the longest x1 0.74 us: shards(): bias_fc = of_shard(vec[8:].reshape(n_z, hidden))]
  transfers between devices with their start and end apart: 10 -> 62, of which waited for: 7 -> 22; matrix products, arithmetic and copies ran while one was open for 10% -> 5% of each run, Pallas kernels for 0% -> 9%
where the time goes in v1:
time: 209 us; the launch traced here: 208 us
  waiting for transfers between devices  97 us (46%)
  starting transfers between devices  52.2 us (25%)
  Pallas kernels  41 us (20%)
  local copies, waits for them, and re-layouts  11.5 us (6%)
  other arithmetic  5.16 us (2%)
    ppermute x62, waiting for transfers between devices, swap(): return lax.ppermute(value, axis, [(i, i ^ bits) for i in range(size)])  97 us
    ppermute x62, starting transfers between devices, swap(): return lax.ppermute(value, axis, [(i, i ^ bits) for i in range(size)])  52.2 us
    pallas_call x9, Pallas kernels, call(): pl.pallas_call(body, name=name, out_shape=[jax.ShapeDtypeStruct(shape, dt...  41 us
    unnamed x95, local copies, waits for them, and re-layouts  7.88 us
  transfers between devices with their start and end apart: 62, of which 22 were waited for; matrix products, arithmetic and copies ran while one was open for 5% of the time, Pallas kernels for 9%

profile of v1, /device:TPU:0, one launch (start us, length us, event | category | flops | bytes accessed | tf_op | source)
XLA Modules:
  0.0 208.1 jit_solution(12963457630927397837)
XLA Ops:
  2.2 0.9 copy.19
  3.1 1.1 copy.18
  4.4 3.7 %collective-permute-start.13 = (bf16[1,96,768]{2,1,0:T(8,128)(2,1)S(1)}, bf16[1,96,768]{2,1,0:T(8,128)(2,1)S(1)}, u32[]{:S(2)}, u32[]{:S(2)}) collective-permute-start(bf16[1,96,768]{2,1,0:T(8,128)(2,1)S(1)} %maximum_bitcast_fusion.1.refs_5_), channel_id=1, source_target_pairs={{0,2},{1,3},{2,0},{3,1},{4,6},{5,7},{6,4},{7,5},{8,10},{9,11},{10,... | collective-permute-start | bytes 442376 | tf_op jit(solution)/shard_map/ppermute | solution.py:26
  8.1 0.8 dynamic-slice_add_fusion.1
  9.1 1.6 collective-permute-start.2
  10.6 2.6 %collective-permute-done.2 = f32[12,768]{1,0:T(8,128)S(1)} collective-permute-done((f32[12,768]{1,0:T(8,128)S(1)}, f32[12,768]{1,0:T(8,128)S(1)}, u32[]{:S(2)}, u32[]{:S(2)}) %collective-permute-start.2) | collective-permute-done | bytes 36896 | tf_op jit(solution)/shard_map/ppermute | solution.py:26
  13.2 1.6 collective-permute-start.3
  14.8 2.0 norm_first.1
  16.9 1.6 collective-permute-start.23
  19.3 8.0 %collective-permute-done.4 = f32[12,768]{1,0:T(8,128)S(1)} collective-permute-done((f32[12,768]{1,0:T(8,128)S(1)}, f32[12,768]{1,0:T(8,128)S(1)}, u32[]{:S(2)}, u32[]{:S(2)}) %collective-permute-start.4) | collective-permute-done | bytes 36896 | tf_op jit(solution)/shard_map/ppermute | solution.py:26
  27.3 1.4 collective-permute-start.7
  29.4 1.3 collective-permute-start.5
  30.7 1.8 collective-permute-done.7.refs_7_
  32.5 1.4 collective-permute-done.6.refs_6_
  35.6 3.4 %collective-permute-start.31 = (bf16[1,96,1536]{2,1,0:T(8,128)(2,1)S(1)}, bf16[1,96,1536]{2,1,0:T(8,128)(2,1)S(1)}, u32[]{:S(2)}, u32[]{:S(2)}) collective-permute-start(bf16[1,96,1536]{2,1,0:T(8,128)(2,1)S(1)} %maximum_bitcast_fusion.refs_6_), channel_id=1, source_target_pairs={{0,2},{1,3},{2,0},{3,1},{4,6},{5,7},{6,4},{7,5},{8,10},{9,11},{10,... | collective-permute-start | bytes 884744 | tf_op jit(solution)/shard_map/ppermute | solution.py:26
  39.8 0.9 collective-permute-start.25
  40.7 1.3 collective-permute-start.24
  42.0 1.1 collective-permute-start.8
  43.2 8.5 %collective-permute-done.8.refs_8_ = bf16[1,96,768]{2,1,0:T(8,128)(2,1)S(1)} collective-permute-done((bf16[1,96,768]{2,1,0:T(8,128)(2,1)S(1)}, bf16[1,96,768]{2,1,0:T(8,128)(2,1)S(1)}, u32[]{:S(2)}, u32[]{:S(2)}) %collective-permute-start.8) | collective-permute-done | bytes 147488 | tf_op jit(solution)/shard_map/ppermute | solution.py:26
  51.7 1.0 collective-permute-done.31.refs_14_
  52.6 1.4 collective-permute-start.16
  54.7 1.5 collective-permute-start.32
  56.9 1.7 collective-permute-done.16.refs_16_
  58.9 1.5 collective-permute-start.33
  60.7 1.4 collective-permute-start.26
  62.1 1.6 collective-permute-done.32.refs_15_
  64.9 6.6 %attend.1 = (bf16[2,768,768]{2,1,0:T(8,128)(2,1)}, bf16[2,256,576]{2,1,0:T(8,128)(2,1)}, bf16[2,256,192]{2,1,0:T(8,128)(2,1)}, f32[256,128]{1,0:T(8,128)}, bf16[...) custom-call(s32[3]{0:T(128)} %pad_add_fusion.refs_0_, ...), custom_call_target="tpu_custom_call" | custom-call | tf_op jit(solution)/shard_map/attend/pallas_call | solution.py:65
  72.8 5.1 %collective-permute-done.21.recv_ref = bf16[128,768]{1,0:T(8,128)(2,1)S(1)} collective-permute-done((bf16[128,768]{1,0:T(8,128)(2,1)}, bf16[128,768]{1,0:T(8,128)(2,1)S(1)}, u32[]{:S(2)}, u32[]{:S(2)}) %collective-permute-start.21) | collective-permute-done | bytes 196640 | tf_op jit(solution)/shard_map/ppermute | solution.py:26
  79.2 2.1 %norm_second.1 = (f32[128,768]{1,0:T(8,128)}, bf16[128,768]{1,0:T(8,128)(2,1)}) custom-call(f32[128,768]{1,0:T(8,128)} %x_ref.5, f32[128,768]{1,0:T(8,128)} %get-tuple-element.47.keep_ref, bf16[128,768]{1,0:T(8,128)(2,1)} %copy-done.29, f32[12,768]{1,0:T(8,128)} %copy-done.3), custom_call_target="tpu_custom_call" | custom-call | tf_op jit(solution)/shard_map/norm_second/pallas_call | solution.py:65
  82.4 6.1 %collective-permute-done.22.refs_2_ = bf16[128,768]{1,0:T(8,128)(2,1)S(1)} collective-permute-done((bf16[128,768]{1,0:T(8,128)(2,1)}, bf16[128,768]{1,0:T(8,128)(2,1)S(1)}, u32[]{:S(2)}, u32[]{:S(2)}) %collective-permute-start.22) | collective-permute-done | bytes 196640 | tf_op jit(solution)/shard_map/ppermute | solution.py:26
  89.9 7.4 %feed.1 = (bf16[256,768]{1,0:T(8,128)(2,1)}, bf16[256,768]{1,0:T(8,128)(2,1)}, bf16[2,256,768]{2,1,0:T(8,128)(2,1)}, bf16[2,256,768]{2,1,0:T(8,128)(2,1)}, f32[1...) custom-call(s32[3]{0:T(128)} %pad_add_fusion.refs_0_, ...), custom_call_target="tpu_custom_call" | custom-call | tf_op jit(solution)/shard_map/feed/pallas_call | solution.py:65
  97.7 5.9 %collective-permute-done.40.recv_ref = bf16[128,768]{1,0:T(8,128)(2,1)S(1)} collective-permute-done((bf16[128,768]{1,0:T(8,128)(2,1)}, bf16[128,768]{1,0:T(8,128)(2,1)S(1)}, u32[]{:S(2)}, u32[]{:S(2)}) %collective-permute-start.40) | collective-permute-done | bytes 196640 | tf_op jit(solution)/shard_map/ppermute | solution.py:26
  104.3 2.4 %norm_second_back.1 = (f32[128,768]{1,0:T(8,128)}, bf16[128,768]{1,0:T(8,128)(2,1)}, f32[3,768]{1,0:T(4,128)}) custom-call(f32[128,768]{1,0:T(8,128)} %get-tuple-element.49.resid_ref, f32[128,768]{1,0:T(8,128)} %get-tuple-element.54.keep_ref, bf16[128,768]{1,0:T(8,128)(2,1)} %copy-done.30, f32[128,768]{1,0:T(8,128)} %grad_ref.1, f32[12,768]{1,0:T(8,128)} %copy-done.3), custom_call_target="tpu_custom_call" | custom-call | tf_op jit(solution)/shard_map/norm_second_back/pallas_call | solution.py:65
  107.1 5.5 %collective-permute-done.41.refs_2_ = bf16[128,768]{1,0:T(8,128)(2,1)S(1)} collective-permute-done((bf16[128,768]{1,0:T(8,128)(2,1)}, bf16[128,768]{1,0:T(8,128)(2,1)S(1)}, u32[]{:S(2)}, u32[]{:S(2)}) %collective-permute-start.41) | collective-permute-done | bytes 196640 | tf_op jit(solution)/shard_map/ppermute | solution.py:26
  113.3 7.8 %attend_back.1 = (bf16[256,768]{1,0:T(8,128)(2,1)}, bf16[2,256,576]{2,1,0:T(8,128)(2,1)}, f32[128,768]{1,0:T(8,128)}, bf16[128,768]{1,0:T(8,128)(2,1)}, f32[2,768]{1,0:T(2,128)}, /*index=5*/f32[2,576]{1,0:T(2,128)}) custom-call(s32[3]{0:T(128)} %pad_add_fusion.refs_0_, bf16[128,768]{1,0:T(8,128)(2,1)} %get-tuple-element.56.refs_1_, ...), custom_call_target="tpu_custom_call" | custom-call | tf_op jit(solution)/shard_map/attend_back/pallas_call | solution.py:65
  121.1 4.6 %attend_grad.1 = (f32[4,96,768]{2,1,0:T(8,128)}, bf16[4,96,768]{2,1,0:T(8,128)(2,1)}, f32[4,96,768]{2,1,0:T(8,128)}, bf16[4,96,768]{2,1,0:T(8,128)(2,1)}, f32[12,768]{1,0:T(8,128)}) custom-call(s32[3]{0:T(128)} %pad_add_fusion.refs_0_, bf16[256,768]{1,0:T(8,128)(2,1)} %get-tuple-element.63.refs_1_, bf16[256,768]{1,0:T(8,128)(2,1)} %get-tuple-element.64.refs_2_, ...), custom_call_target="tpu_custom_call" | custom-call | tf_op jit(solution)/shard_map/attend_grad/pallas_call | solution.py:65
  125.7 5.7 %feed_grad.1 = (f32[4,96,1536]{2,1,0:T(8,128)}, bf16[4,96,1536]{2,1,0:T(8,128)(2,1)}, f32[4,96,1536]{2,1,0:T(8,128)}, bf16[4,96,1536]{2,1,0:T(8,128)(2,1)}) custom-call(s32[3]{0:T(128)} %pad_add_fusion.refs_0_, bf16[256,768]{1,0:T(8,128)(2,1)} %get-tuple-element.76.refs_1_, bf16[256,768]{1,0:T(8,128)(2,1)} %get-tuple-element.77.refs_2_, ...), custom_call_target="tpu_custom_call" | custom-call | tf_op jit(solution)/shard_map/feed_grad/pallas_call | solution.py:65
  132.3 2.2 %collective-permute-done.57 = f32[12,768]{1,0:T(8,128)S(1)} collective-permute-done((f32[12,768]{1,0:T(8,128)S(1)}, f32[12,768]{1,0:T(8,128)S(1)}, u32[]{:S(2)}, u32[]{:S(2)}) %collective-permute-start.57) | collective-permute-done | bytes 36896 | tf_op jit(solution)/shard_map/ppermute | solution.py:26
  134.5 1.1 collective-permute-start.58
  135.6 3.0 %collective-permute-done.58 = f32[12,768]{1,0:T(8,128)S(1)} collective-permute-done((f32[12,768]{1,0:T(8,128)S(1)}, f32[12,768]{1,0:T(8,128)S(1)}, u32[]{:S(2)}, u32[]{:S(2)}) %collective-permute-start.58) | collective-permute-done | bytes 36896 | tf_op jit(solution)/shard_map/ppermute | solution.py:26
  138.6 1.1 collective-permute-start.59
  139.7 3.0 %collective-permute-done.59 = f32[12,768]{1,0:T(8,128)S(1)} collective-permute-done((f32[12,768]{1,0:T(8,128)S(1)}, f32[12,768]{1,0:T(8,128)S(1)}, u32[]{:S(2)}, u32[]{:S(2)}) %collective-permute-start.59) | collective-permute-done | bytes 36896 | tf_op jit(solution)/shard_map/ppermute | solution.py:26
  142.7 2.5 %collective-permute-start.60 = (f32[12,768]{1,0:T(8,128)S(1)}, f32[12,768]{1,0:T(8,128)S(1)}, u32[]{:S(2)}, u32[]{:S(2)}) collective-permute-start(f32[12,768]{1,0:T(8,128)S(1)} %add.139), channel_id=1, source_target_pairs={{0,2},{1,3},{2,0},{3,1},{4,6},{5,7},{6,4},{7,5},{8,10},{9,11},{10,... | collective-permute-start | bytes 110600 | tf_op jit(solution)/shard_map/ppermute | solution.py:26
  145.2 0.8 collective-permute-start.42
  146.0 2.0 collective-permute-done.60
  148.1 1.1 collective-permute-start.61
  149.2 0.8 add_add_fusion
  150.0 2.3 %collective-permute-done.61 = f32[12,768]{1,0:T(8,128)S(1)} collective-permute-done((f32[12,768]{1,0:T(8,128)S(1)}, f32[12,768]{1,0:T(8,128)S(1)}, u32[]{:S(2)}, u32[]{:S(2)}) %collective-permute-start.61) | collective-permute-done | bytes 36896 | tf_op jit(solution)/shard_map/ppermute | solution.py:26
  153.6 2.4 %norm_first_back.1 = f32[128,768]{1,0:T(8,128)} custom-call(f32[128,768]{1,0:T(8,128)} %x_ref.5, f32[128,768]{1,0:T(8,128)} %get-tuple-element.60.keep_ref, bf16[128,768]{1,0:T(8,128)(2,1)} %copy-done.28, f32[128,768]{1,0:T(8,128)} %get-tuple-element.62.grad1_ref, f32[12,768]{1,0:T(8,128)} %copy-done.3), custom_call_target="tpu_custom_call" | custom-call | tf_op jit(solution)/shard_map/norm_first_back/pallas_call | solution.py:65
  156.1 1.2 collective-permute-start.44
  157.5 1.5 collective-permute-start.47
  159.5 1.1 collective-permute-start.51
  161.1 1.5 collective-permute-start.54
  162.6 4.8 %collective-permute-done.47 = bf16[2,96,768]{2,1,0:T(8,128)(2,1)S(1)} collective-permute-done((bf16[2,96,768]{2,1,0:T(8,128)(2,1)S(1)}, bf16[2,96,768]{2,1,0:T(8,128)(2,1)S(1)}, u32[]{:S(2)}, u32[]{:S(2)}) %collective-permute-start.47) | collective-permute-done | bytes 294944 | tf_op jit(solution)/shard_map/ppermute | solution.py:26
  167.4 1.1 collective-permute-start.48
  168.6 1.5 collective-permute-start.45
  170.2 11.3 %collective-permute-done.48 = bf16[1,96,768]{2,1,0:T(8,128)(2,1)S(1)} collective-permute-done((bf16[1,96,768]{2,1,0:T(8,128)(2,1)S(1)}, bf16[1,96,768]{2,1,0:T(8,128)(2,1)S(1)}, u32[]{:S(2)}, u32[]{:S(2)}) %collective-permute-start.48) | collective-permute-done | bytes 147488 | tf_op jit(solution)/shard_map/ppermute | solution.py:26
  181.5 2.3 %collective-permute-start.49 = (bf16[96,768]{1,0:T(8,128)(2,1)S(1)}, bf16[96,768]{1,0:T(8,128)(2,1)S(1)}, u32[]{:S(2)}, u32[]{:S(2)}) collective-permute-start(bf16[96,768]{1,0:T(8,128)(2,1)S(1)} %fusion.7), channel_id=1, source_target_pairs={{0,2},{1,3},{2,0},{3,1},{4,6},{5,7},{6,4},{7,5},{8,10},{9,11},{10,... | collective-permute-start | bytes 442376 | tf_op jit(solution)/shard_map/ppermute | solution.py:26
  184.0 1.2 collective-permute-start.55
  186.1 6.3 %collective-permute-done.55 = bf16[1,96,1536]{2,1,0:T(8,128)(2,1)S(1)} collective-permute-done((bf16[1,96,1536]{2,1,0:T(8,128)(2,1)S(1)}, bf16[1,96,1536]{2,1,0:T(8,128)(2,1)S(1)}, u32[]{:S(2)}, u32[]{:S(2)}) %collective-permute-start.55) | collective-permute-done | bytes 294944 | tf_op jit(solution)/shard_map/ppermute | solution.py:26
  193.4 0.7 copy.23
  194.3 0.9 copy.22
  195.2 12.1 %collective-permute-done.56 = bf16[96,1536]{1,0:T(8,128)(2,1)S(1)} collective-permute-done((bf16[96,1536]{1,0:T(8,128)(2,1)S(1)}, bf16[96,1536]{1,0:T(8,128)(2,1)S(1)}, u32[]{:S(2)}, u32[]{:S(2)}) %collective-permute-start.56) | collective-permute-done | bytes 294944 | tf_op jit(solution)/shard_map/ppermute | solution.py:26
  207.3 0.9 slice_bitcast_fusion
  (217 shorter events, 21.9 us)
Async XLA Ops:
  1.6 6.4 %collective-permute-start.1 = (f32[12,768]{1,0:T(8,128)S(1)}, f32[12,768]{1,0:T(8,128)S(1)}, u32[]{:S(2)}, u32[]{:S(2)}) collective-permute-start(f32[12,768]{1,0:T(8,128)S(1)} %dynamic_update_slice.5), channel_id=1, source_target_pairs={{0,4},{4,0},{8,12},{12,8},{16,20},{20,16},{24,28},{28,24},{1,5},{5... | collective-permute-start | bytes 110600 | tf_op jit(solution)/shard_map/ppermute | solution.py:26
  4.4 60.5 %copy-start.8 = (bf16[1,96,768]{2,1,0:T(8,128)(2,1)}, bf16[1,96,768]{2,1,0:T(8,128)(2,1)S(1)}, u32[]{:S(2)}) copy-start(bf16[1,96,768]{2,1,0:T(8,128)(2,1)S(1)} %maximum_bitcast_fusion.1.refs_5_) | copy-start | bytes 442372
  4.4 24.3 %collective-permute-start.13 = (bf16[1,96,768]{2,1,0:T(8,128)(2,1)S(1)}, bf16[1,96,768]{2,1,0:T(8,128)(2,1)S(1)}, u32[]{:S(2)}, u32[]{:S(2)}) collective-permute-start(bf16[1,96,768]{2,1,0:T(8,128)(2,1)S(1)} %maximum_bitcast_fusion.1.refs_5_), channel_id=1, source_target_pairs={{0,2},{1,3},{2,0},{3,1},{4,6},{5,7},{6,4},{7,5},{8,10},{9,11},{10,... | collective-permute-start | bytes 442376 | tf_op jit(solution)/shard_map/ppermute | solution.py:26
  9.1 4.2 %collective-permute-start.2 = (f32[12,768]{1,0:T(8,128)S(1)}, f32[12,768]{1,0:T(8,128)S(1)}, u32[]{:S(2)}, u32[]{:S(2)}) collective-permute-start(f32[12,768]{1,0:T(8,128)S(1)} %add.111), channel_id=1, source_target_pairs={{0,16},{4,20},{8,24},{12,28},{16,0},{20,4},{24,8},{28,12},{1,17},{... | collective-permute-start | bytes 110600 | tf_op jit(solution)/shard_map/ppermute | solution.py:26
  13.2 5.7 %collective-permute-start.3 = (f32[12,768]{1,0:T(8,128)S(1)}, f32[12,768]{1,0:T(8,128)S(1)}, u32[]{:S(2)}, u32[]{:S(2)}) collective-permute-start(f32[12,768]{1,0:T(8,128)S(1)} %add.112), channel_id=1, source_target_pairs={{0,8},{4,12},{8,0},{12,4},{16,24},{20,28},{24,16},{28,20},{1,9},{5... | collective-permute-start | bytes 110600 | tf_op jit(solution)/shard_map/ppermute | solution.py:26
  16.9 18.2 %collective-permute-start.23 = (bf16[128,768]{1,0:T(8,128)(2,1)}, bf16[128,768]{1,0:T(8,128)(2,1)S(1)}, u32[]{:S(2)}, u32[]{:S(2)}) collective-permute-start(bf16[128,768]{1,0:T(8,128)(2,1)} %get-tuple-element.51.refs_3_), channel_id=1, source_target_pairs={{0,1},{1,0},{2,3},{3,2},{4,5},{5,4},{6,7},{7,6},{8,9},{9,8},{10,11... | collective-permute-start | bytes 589832 | tf_op jit(solution)/shard_map/ppermute | solution.py:26
  18.4 16.6 %collective-permute-start = (bf16[128,768]{1,0:T(8,128)(2,1)}, bf16[128,768]{1,0:T(8,128)(2,1)S(1)}, u32[]{:S(2)}, u32[]{:S(2)}) collective-permute-start(bf16[128,768]{1,0:T(8,128)(2,1)} %get-tuple-element.46.refs_1_.refs_3_), channel_id=1, source_target_pairs={{0,1},{1,0},{2,3},{3,2},{4,5},{5,4},{6,7},{7,6},{8,9},{9,8},{10,11... | collective-permute-start | bytes 589832 | tf_op jit(solution)/shard_map/ppermute | solution.py:26
  18.9 8.4 %collective-permute-start.4 = (f32[12,768]{1,0:T(8,128)S(1)}, f32[12,768]{1,0:T(8,128)S(1)}, u32[]{:S(2)}, u32[]{:S(2)}) collective-permute-start(f32[12,768]{1,0:T(8,128)S(1)} %add.113), channel_id=1, source_target_pairs={{0,2},{1,3},{2,0},{3,1},{4,6},{5,7},{6,4},{7,5},{8,10},{9,11},{10,... | collective-permute-start | bytes 110600 | tf_op jit(solution)/shard_map/ppermute | solution.py:26
  19.3 10.1 %collective-permute-start.9 = (bf16[1,96,768]{2,1,0:T(8,128)(2,1)S(1)}, bf16[1,96,768]{2,1,0:T(8,128)(2,1)S(1)}, u32[]{:S(2)}, u32[]{:S(2)}) collective-permute-start(bf16[1,96,768]{2,1,0:T(8,128)(2,1)S(1)} %maximum_bitcast_fusion.1.refs_5_), channel_id=1, source_target_pairs={{0,4},{4,0},{8,12},{12,8},{16,20},{20,16},{24,28},{28,24},{1,5},{5... | collective-permute-start | bytes 442376 | tf_op jit(solution)/shard_map/ppermute | solution.py:26
  27.3 5.1 %collective-permute-start.7 = (bf16[1,96,768]{2,1,0:T(8,128)(2,1)S(1)}, bf16[1,96,768]{2,1,0:T(8,128)(2,1)S(1)}, u32[]{:S(2)}, u32[]{:S(2)}) collective-permute-start(bf16[1,96,768]{2,1,0:T(8,128)(2,1)S(1)} %maximum_bitcast_fusion.1.refs_5_), channel_id=1, source_target_pairs={{0,16},{4,20},{8,24},{12,28},{16,0},{20,4},{24,8},{28,12},{1,17},{... | collective-permute-start | bytes 442376 | tf_op jit(solution)/shard_map/ppermute | solution.py:26
  28.7 5.1 %collective-permute-start.6 = (bf16[1,96,768]{2,1,0:T(8,128)(2,1)S(1)}, bf16[1,96,768]{2,1,0:T(8,128)(2,1)S(1)}, u32[]{:S(2)}, u32[]{:S(2)}) collective-permute-start(bf16[1,96,768]{2,1,0:T(8,128)(2,1)S(1)} %maximum_bitcast_fusion.1.refs_5_), channel_id=1, source_target_pairs={{0,8},{4,12},{8,0},{12,4},{16,24},{20,28},{24,16},{28,20},{1,9},{5... | collective-permute-start | bytes 442376 | tf_op jit(solution)/shard_map/ppermute | solution.py:26
  29.4 5.1 %collective-permute-start.5 = (f32[12,768]{1,0:T(8,128)S(1)}, f32[12,768]{1,0:T(8,128)S(1)}, u32[]{:S(2)}, u32[]{:S(2)}) collective-permute-start(f32[12,768]{1,0:T(8,128)S(1)} %add.114), channel_id=1, source_target_pairs={{0,1},{1,0},{2,3},{3,2},{4,5},{5,4},{6,7},{7,6},{8,9},{9,8},{10,11... | collective-permute-start | bytes 110600 | tf_op jit(solution)/shard_map/ppermute | solution.py:26
  32.5 3.1 %collective-permute-start.17 = (bf16[1,96,768]{2,1,0:T(8,128)(2,1)S(1)}, bf16[1,96,768]{2,1,0:T(8,128)(2,1)S(1)}, u32[]{:S(2)}, u32[]{:S(2)}) collective-permute-start(bf16[1,96,768]{2,1,0:T(8,128)(2,1)S(1)} %collective-permute-done.13.refs_13_), channel_id=1, source_target_pairs={{0,4},{4,0},{8,12},{12,8},{16,20},{20,16},{24,28},{28,24},{1,5},{5... | collective-permute-start | bytes 442376 | tf_op jit(solution)/shard_map/ppermute | solution.py:26
  33.8 5.2 %collective-permute-start.15 = (bf16[1,96,768]{2,1,0:T(8,128)(2,1)S(1)}, bf16[1,96,768]{2,1,0:T(8,128)(2,1)}, u32[]{:S(2)}, u32[]{:S(2)}) collective-permute-start(bf16[1,96,768]{2,1,0:T(8,128)(2,1)S(1)} %collective-permute-done.13.refs_13_), channel_id=1, source_target_pairs={{0,8},{4,12},{8,0},{12,4},{16,24},{20,28},{24,16},{28,20},{1,9},{5... | collective-permute-start | bytes 442376 | tf_op jit(solution)/shard_map/ppermute | solution.py:26
  34.5 5.2 %collective-permute-start.14 = (bf16[1,96,768]{2,1,0:T(8,128)(2,1)S(1)}, bf16[1,96,768]{2,1,0:T(8,128)(2,1)}, u32[]{:S(2)}, u32[]{:S(2)}) collective-permute-start(bf16[1,96,768]{2,1,0:T(8,128)(2,1)S(1)} %collective-permute-done.13.refs_13_), channel_id=1, source_target_pairs={{0,16},{4,20},{8,24},{12,28},{16,0},{20,4},{24,8},{28,12},{1,17},{... | collective-permute-start | bytes 442376 | tf_op jit(solution)/shard_map/ppermute | solution.py:26
  35.0 5.6 %collective-permute-start.11 = (bf16[1,96,768]{2,1,0:T(8,128)(2,1)S(1)}, bf16[1,96,768]{2,1,0:T(8,128)(2,1)}, u32[]{:S(2)}, u32[]{:S(2)}) collective-permute-start(bf16[1,96,768]{2,1,0:T(8,128)(2,1)S(1)} %collective-permute-done.7.refs_7_), channel_id=1, source_target_pairs={{0,4},{4,0},{8,12},{12,8},{16,20},{20,16},{24,28},{28,24},{1,5},{5... | collective-permute-start | bytes 442376 | tf_op jit(solution)/shard_map/ppermute | solution.py:26
  35.1 6.9 %collective-permute-start.10 = (bf16[1,96,768]{2,1,0:T(8,128)(2,1)S(1)}, bf16[1,96,768]{2,1,0:T(8,128)(2,1)S(1)}, u32[]{:S(2)}, u32[]{:S(2)}) collective-permute-start(bf16[1,96,768]{2,1,0:T(8,128)(2,1)S(1)} %collective-permute-done.6.refs_6_), channel_id=1, source_target_pairs={{0,4},{4,0},{8,12},{12,8},{16,20},{20,16},{24,28},{28,24},{1,5},{5... | collective-permute-start | bytes 442376 | tf_op jit(solution)/shard_map/ppermute | solution.py:26
  35.6 52.9 %copy-start.4 = (bf16[1,96,1536]{2,1,0:T(8,128)(2,1)}, bf16[1,96,1536]{2,1,0:T(8,128)(2,1)S(1)}, u32[]{:S(2)}) copy-start(bf16[1,96,1536]{2,1,0:T(8,128)(2,1)S(1)} %maximum_bitcast_fusion.refs_6_) | copy-start | bytes 884740
  35.6 17.0 %collective-permute-start.31 = (bf16[1,96,1536]{2,1,0:T(8,128)(2,1)S(1)}, bf16[1,96,1536]{2,1,0:T(8,128)(2,1)S(1)}, u32[]{:S(2)}, u32[]{:S(2)}) collective-permute-start(bf16[1,96,1536]{2,1,0:T(8,128)(2,1)S(1)} %maximum_bitcast_fusion.refs_6_), channel_id=1, source_target_pairs={{0,2},{1,3},{2,0},{3,1},{4,6},{5,7},{6,4},{7,5},{8,10},{9,11},{10,... | collective-permute-start | bytes 884744 | tf_op jit(solution)/shard_map/ppermute | solution.py:26
  39.1 15.0 %collective-permute-start.27 = (bf16[1,96,1536]{2,1,0:T(8,128)(2,1)S(1)}, bf16[1,96,1536]{2,1,0:T(8,128)(2,1)S(1)}, u32[]{:S(2)}, u32[]{:S(2)}) collective-permute-start(bf16[1,96,1536]{2,1,0:T(8,128)(2,1)S(1)} %maximum_bitcast_fusion.refs_6_), channel_id=1, source_target_pairs={{0,4},{4,0},{8,12},{12,8},{16,20},{20,16},{24,28},{28,24},{1,5},{5... | collective-permute-start | bytes 884744 | tf_op jit(solution)/shard_map/ppermute | solution.py:26
  39.8 14.3 %collective-permute-start.25 = (bf16[1,96,1536]{2,1,0:T(8,128)(2,1)S(1)}, bf16[1,96,1536]{2,1,0:T(8,128)(2,1)S(1)}, u32[]{:S(2)}, u32[]{:S(2)}) collective-permute-start(bf16[1,96,1536]{2,1,0:T(8,128)(2,1)S(1)} %maximum_bitcast_fusion.refs_6_), channel_id=1, source_target_pairs={{0,16},{4,20},{8,24},{12,28},{16,0},{20,4},{24,8},{28,12},{1,17},{... | collective-permute-start | bytes 884744 | tf_op jit(solution)/shard_map/ppermute | solution.py:26
  40.7 14.0 %collective-permute-start.24 = (bf16[1,96,1536]{2,1,0:T(8,128)(2,1)S(1)}, bf16[1,96,1536]{2,1,0:T(8,128)(2,1)S(1)}, u32[]{:S(2)}, u32[]{:S(2)}) collective-permute-start(bf16[1,96,1536]{2,1,0:T(8,128)(2,1)S(1)} %maximum_bitcast_fusion.refs_6_), channel_id=1, source_target_pairs={{0,8},{4,12},{8,0},{12,4},{16,24},{20,28},{24,16},{28,20},{1,9},{5... | collective-permute-start | bytes 884744 | tf_op jit(solution)/shard_map/ppermute | solution.py:26
  42.0 9.7 %collective-permute-start.8 = (bf16[1,96,768]{2,1,0:T(8,128)(2,1)S(1)}, bf16[1,96,768]{2,1,0:T(8,128)(2,1)S(1)}, u32[]{:S(2)}, u32[]{:S(2)}) collective-permute-start(bf16[1,96,768]{2,1,0:T(8,128)(2,1)S(1)} %collective-permute-done.6.refs_6_), channel_id=1, source_target_pairs={{0,16},{4,20},{8,24},{12,28},{16,0},{20,4},{24,8},{28,12},{1,17},{... | collective-permute-start | bytes 442376 | tf_op jit(solution)/shard_map/ppermute | solution.py:26
  51.7 5.2 %collective-permute-start.19 = (bf16[1,96,768]{2,1,0:T(8,128)(2,1)}, bf16[1,96,768]{2,1,0:T(8,128)(2,1)}, u32[]{:S(2)}, u32[]{:S(2)}) collective-permute-start(bf16[1,96,768]{2,1,0:T(8,128)(2,1)} %collective-permute-done.15.refs_15_), channel_id=1, source_target_pairs={{0,4},{4,0},{8,12},{12,8},{16,20},{20,16},{24,28},{28,24},{1,5},{5... | collective-permute-start | bytes 442376 | tf_op jit(solution)/shard_map/ppermute | solution.py:26
  52.6 6.0 %collective-permute-start.16 = (bf16[1,96,768]{2,1,0:T(8,128)(2,1)}, bf16[1,96,768]{2,1,0:T(8,128)(2,1)}, u32[]{:S(2)}, u32[]{:S(2)}) collective-permute-start(bf16[1,96,768]{2,1,0:T(8,128)(2,1)} %collective-permute-done.14.refs_14_), channel_id=1, source_target_pairs={{0,8},{4,12},{8,0},{12,4},{16,24},{20,28},{24,16},{28,20},{1,9},{5... | collective-permute-start | bytes 442376 | tf_op jit(solution)/shard_map/ppermute | solution.py:26
  54.1 4.8 %collective-permute-start.18 = (bf16[1,96,768]{2,1,0:T(8,128)(2,1)}, bf16[1,96,768]{2,1,0:T(8,128)(2,1)}, u32[]{:S(2)}, u32[]{:S(2)}) collective-permute-start(bf16[1,96,768]{2,1,0:T(8,128)(2,1)} %collective-permute-done.14.refs_14_), channel_id=1, source_target_pairs={{0,4},{4,0},{8,12},{12,8},{16,20},{20,16},{24,28},{28,24},{1,5},{5... | collective-permute-start | bytes 442376 | tf_op jit(solution)/shard_map/ppermute | solution.py:26
  54.1 8.0 %collective-permute-start.35 = (bf16[1,96,1536]{2,1,0:T(8,128)(2,1)S(1)}, bf16[1,96,1536]{2,1,0:T(8,128)(2,1)S(1)}, u32[]{:S(2)}, u32[]{:S(2)}) collective-permute-start(bf16[1,96,1536]{2,1,0:T(8,128)(2,1)S(1)} %collective-permute-done.31.refs_14_), channel_id=1, source_target_pairs={{0,4},{4,0},{8,12},{12,8},{16,20},{20,16},{24,28},{28,24},{1,5},{5... | collective-permute-start | bytes 884744 | tf_op jit(solution)/shard_map/ppermute | solution.py:26
  54.7 9.0 %collective-permute-start.32 = (bf16[1,96,1536]{2,1,0:T(8,128)(2,1)S(1)}, bf16[1,96,1536]{2,1,0:T(8,128)(2,1)S(1)}, u32[]{:S(2)}, u32[]{:S(2)}) collective-permute-start(bf16[1,96,1536]{2,1,0:T(8,128)(2,1)S(1)} %collective-permute-done.31.refs_14_), channel_id=1, source_target_pairs={{0,16},{4,20},{8,24},{12,28},{16,0},{20,4},{24,8},{28,12},{1,17},{... | collective-permute-start | bytes 884744 | tf_op jit(solution)/shard_map/ppermute | solution.py:26
  56.9 3.5 %collective-permute-start.12 = (bf16[1,96,768]{2,1,0:T(8,128)(2,1)}, bf16[1,96,768]{2,1,0:T(8,128)(2,1)}, u32[]{:S(2)}, u32[]{:S(2)}) collective-permute-start(bf16[1,96,768]{2,1,0:T(8,128)(2,1)} %copy-done.37), channel_id=1, source_target_pairs={{0,4},{4,0},{8,12},{12,8},{16,20},{20,16},{24,28},{28,24},{1,5},{5... | collective-permute-start | bytes 442376 | tf_op jit(solution)/shard_map/ppermute | solution.py:26
  58.7 2.0 collective-permute-start.20
  58.9 12.7 %collective-permute-start.33 = (bf16[1,96,1536]{2,1,0:T(8,128)(2,1)S(1)}, bf16[1,96,1536]{2,1,0:T(8,128)(2,1)S(1)}, u32[]{:S(2)}, u32[]{:S(2)}) collective-permute-start(bf16[1,96,1536]{2,1,0:T(8,128)(2,1)S(1)} %collective-permute-done.31.refs_14_), channel_id=1, source_target_pairs={{0,8},{4,12},{8,0},{12,4},{16,24},{20,28},{24,16},{28,20},{1,9},{5... | collective-permute-start | bytes 884744 | tf_op jit(solution)/shard_map/ppermute | solution.py:26
  60.4 20.9 %collective-permute-start.28 = (bf16[1,96,1536]{2,1,0:T(8,128)(2,1)S(1)}, bf16[1,96,1536]{2,1,0:T(8,128)(2,1)S(1)}, u32[]{:S(2)}, u32[]{:S(2)}) collective-permute-start(bf16[1,96,1536]{2,1,0:T(8,128)(2,1)S(1)} %collective-permute-done.24.refs_7_), channel_id=1, source_target_pairs={{0,4},{4,0},{8,12},{12,8},{16,20},{20,16},{24,28},{28,24},{1,5},{5... | collective-permute-start | bytes 884744 | tf_op jit(solution)/shard_map/ppermute | solution.py:26
  60.7 11.6 %collective-permute-start.26 = (bf16[1,96,1536]{2,1,0:T(8,128)(2,1)S(1)}, bf16[1,96,1536]{2,1,0:T(8,128)(2,1)S(1)}, u32[]{:S(2)}, u32[]{:S(2)}) collective-permute-start(bf16[1,96,1536]{2,1,0:T(8,128)(2,1)S(1)} %collective-permute-done.24.refs_7_), channel_id=1, source_target_pairs={{0,16},{4,20},{8,24},{12,28},{16,0},{20,4},{24,8},{28,12},{1,17},{... | collective-permute-start | bytes 884744 | tf_op jit(solution)/shard_map/ppermute | solution.py:26
  62.1 10.1 %collective-permute-start.29 = (bf16[1,96,1536]{2,1,0:T(8,128)(2,1)S(1)}, bf16[1,96,1536]{2,1,0:T(8,128)(2,1)S(1)}, u32[]{:S(2)}, u32[]{:S(2)}) collective-permute-start(bf16[1,96,1536]{2,1,0:T(8,128)(2,1)S(1)} %collective-permute-done.25.refs_8_), channel_id=1, source_target_pairs={{0,4},{4,0},{8,12},{12,8},{16,20},{20,16},{24,28},{28,24},{1,5},{5... | collective-permute-start | bytes 884744 | tf_op jit(solution)/shard_map/ppermute | solution.py:26
  63.7 14.3 %collective-permute-start.34 = (bf16[1,96,1536]{2,1,0:T(8,128)(2,1)S(1)}, bf16[1,96,1536]{2,1,0:T(8,128)(2,1)S(1)}, u32[]{:S(2)}, u32[]{:S(2)}) collective-permute-start(bf16[1,96,1536]{2,1,0:T(8,128)(2,1)S(1)} %collective-permute-done.32.refs_15_), channel_id=1, source_target_pairs={{0,8},{4,12},{8,0},{12,4},{16,24},{20,28},{24,16},{28,20},{1,9},{5... | collective-permute-start | bytes 884744 | tf_op jit(solution)/shard_map/ppermute | solution.py:26
  71.6 6.3 %collective-permute-start.21 = (bf16[128,768]{1,0:T(8,128)(2,1)}, bf16[128,768]{1,0:T(8,128)(2,1)S(1)}, u32[]{:S(2)}, u32[]{:S(2)}) collective-permute-start(bf16[128,768]{1,0:T(8,128)(2,1)} %get-tuple-element.48), channel_id=1, source_target_pairs={{0,1},{1,0},{2,3},{3,2},{4,5},{5,4},{6,7},{7,6},{8,9},{9,8},{10,11... | collective-permute-start | bytes 589832 | tf_op jit(solution)/shard_map/ppermute | solution.py:26
  72.3 10.1 %collective-permute-start.36 = (bf16[1,96,1536]{2,1,0:T(8,128)(2,1)S(1)}, bf16[1,96,1536]{2,1,0:T(8,128)(2,1)S(1)}, u32[]{:S(2)}, u32[]{:S(2)}) collective-permute-start(bf16[1,96,1536]{2,1,0:T(8,128)(2,1)S(1)} %collective-permute-done.32.refs_15_), channel_id=1, source_target_pairs={{0,4},{4,0},{8,12},{12,8},{16,20},{20,16},{24,28},{28,24},{1,5},{5... | collective-permute-start | bytes 884744 | tf_op jit(solution)/shard_map/ppermute | solution.py:26
  72.3 10.0 %collective-permute-start.37 = (bf16[1,96,1536]{2,1,0:T(8,128)(2,1)S(1)}, bf16[1,96,1536]{2,1,0:T(8,128)(2,1)S(1)}, u32[]{:S(2)}, u32[]{:S(2)}) collective-permute-start(bf16[1,96,1536]{2,1,0:T(8,128)(2,1)S(1)} %collective-permute-done.33.refs_16_), channel_id=1, source_target_pairs={{0,4},{4,0},{8,12},{12,8},{16,20},{20,16},{24,28},{28,24},{1,5},{5... | collective-permute-start | bytes 884744 | tf_op jit(solution)/shard_map/ppermute | solution.py:26
  78.0 4.4 %collective-permute-start.30 = (bf16[1,96,1536]{2,1,0:T(8,128)(2,1)S(1)}, bf16[1,96,1536]{2,1,0:T(8,128)(2,1)S(1)}, u32[]{:S(2)}, u32[]{:S(2)}) collective-permute-start(bf16[1,96,1536]{2,1,0:T(8,128)(2,1)S(1)} %collective-permute-done.26.refs_9_), channel_id=1, source_target_pairs={{0,4},{4,0},{8,12},{12,8},{16,20},{20,16},{24,28},{28,24},{1,5},{5... | collective-permute-start | bytes 884744 | tf_op jit(solution)/shard_map/ppermute | solution.py:26
  78.0 10.5 %collective-permute-start.38 = (bf16[1,96,1536]{2,1,0:T(8,128)(2,1)S(1)}, bf16[1,96,1536]{2,1,0:T(8,128)(2,1)S(1)}, u32[]{:S(2)}, u32[]{:S(2)}) collective-permute-start(bf16[1,96,1536]{2,1,0:T(8,128)(2,1)S(1)} %collective-permute-done.34.refs_17_), channel_id=1, source_target_pairs={{0,4},{4,0},{8,12},{12,8},{16,20},{20,16},{24,28},{28,24},{1,5},{5... | collective-permute-start | bytes 884744 | tf_op jit(solution)/shard_map/ppermute | solution.py:26
  81.3 7.2 %collective-permute-start.22 = (bf16[128,768]{1,0:T(8,128)(2,1)}, bf16[128,768]{1,0:T(8,128)(2,1)S(1)}, u32[]{:S(2)}, u32[]{:S(2)}) collective-permute-start(bf16[128,768]{1,0:T(8,128)(2,1)} %get-tuple-element.50.refs_1_), channel_id=1, source_target_pairs={{0,1},{1,0},{2,3},{3,2},{4,5},{5,4},{6,7},{7,6},{8,9},{9,8},{10,11... | collective-permute-start | bytes 589832 | tf_op jit(solution)/shard_map/ppermute | solution.py:26
  97.3 6.4 %collective-permute-start.40 = (bf16[128,768]{1,0:T(8,128)(2,1)}, bf16[128,768]{1,0:T(8,128)(2,1)S(1)}, u32[]{:S(2)}, u32[]{:S(2)}) collective-permute-start(bf16[128,768]{1,0:T(8,128)(2,1)} %get-tuple-element.55), channel_id=1, source_target_pairs={{0,1},{1,0},{2,3},{3,2},{4,5},{5,4},{6,7},{7,6},{8,9},{9,8},{10,11... | collective-permute-start | bytes 589832 | tf_op jit(solution)/shard_map/ppermute | solution.py:26
  106.8 5.9 %collective-permute-start.41 = (bf16[128,768]{1,0:T(8,128)(2,1)}, bf16[128,768]{1,0:T(8,128)(2,1)S(1)}, u32[]{:S(2)}, u32[]{:S(2)}) collective-permute-start(bf16[128,768]{1,0:T(8,128)(2,1)} %get-tuple-element.56.refs_1_), channel_id=1, source_target_pairs={{0,1},{1,0},{2,3},{3,2},{4,5},{5,4},{6,7},{7,6},{8,9},{9,8},{10,11... | collective-permute-start | bytes 589832 | tf_op jit(solution)/shard_map/ppermute | solution.py:26
  125.6 30.3 %collective-permute-start.43 = (bf16[4,96,768]{2,1,0:T(8,128)(2,1)}, bf16[4,96,768]{2,1,0:T(8,128)(2,1)S(1)}, u32[]{:S(2)}, u32[]{:S(2)}) collective-permute-start(bf16[4,96,768]{2,1,0:T(8,128)(2,1)} %get-tuple-element.73), channel_id=1, source_target_pairs={{0,4},{4,0},{8,12},{12,8},{16,20},{20,16},{24,28},{28,24},{1,5},{5... | collective-permute-start | bytes 1769480 | tf_op jit(solution)/shard_map/ppermute | solution.py:26
  131.4 27.6 %collective-permute-start.50 = (bf16[4,96,1536]{2,1,0:T(8,128)(2,1)}, bf16[4,96,1536]{2,1,0:T(8,128)(2,1)S(1)}, u32[]{:S(2)}, u32[]{:S(2)}) collective-permute-start(bf16[4,96,1536]{2,1,0:T(8,128)(2,1)} %get-tuple-element.81), channel_id=1, source_target_pairs={{0,4},{4,0},{8,12},{12,8},{16,20},{20,16},{24,28},{28,24},{1,5},{5... | collective-permute-start | bytes 3538952 | tf_op jit(solution)/shard_map/ppermute | solution.py:26
  131.9 16.1 %collective-permute-start.39 = (bf16[128,768]{1,0:T(8,128)(2,1)S(1)}, bf16[128,768]{1,0:T(8,128)(2,1)S(1)}, u32[]{:S(2)}, u32[]{:S(2)}) collective-permute-start(bf16[128,768]{1,0:T(8,128)(2,1)S(1)} %copy-done.43), channel_id=1, source_target_pairs={{0,1},{1,0},{2,3},{3,2},{4,5},{5,4},{6,7},{7,6},{8,9},{9,8},{10,11... | collective-permute-start | bytes 589832 | tf_op jit(solution)/shard_map/ppermute | solution.py:26
  132.3 2.2 %collective-permute-start.57 = (f32[12,768]{1,0:T(8,128)S(1)}, f32[12,768]{1,0:T(8,128)S(1)}, u32[]{:S(2)}, u32[]{:S(2)}) collective-permute-start(f32[12,768]{1,0:T(8,128)S(1)} %copy-done.40), channel_id=1, source_target_pairs={{0,4},{4,0},{8,12},{12,8},{16,20},{20,16},{24,28},{28,24},{1,5},{5... | collective-permute-start | bytes 110600 | tf_op jit(solution)/shard_map/ppermute | solution.py:26
  134.5 4.1 %collective-permute-start.58 = (f32[12,768]{1,0:T(8,128)S(1)}, f32[12,768]{1,0:T(8,128)S(1)}, u32[]{:S(2)}, u32[]{:S(2)}) collective-permute-start(f32[12,768]{1,0:T(8,128)S(1)} %add.137), channel_id=1, source_target_pairs={{0,16},{4,20},{8,24},{12,28},{16,0},{20,4},{24,8},{28,12},{1,17},{... | collective-permute-start | bytes 110600 | tf_op jit(solution)/shard_map/ppermute | solution.py:26
  138.6 4.2 %collective-permute-start.59 = (f32[12,768]{1,0:T(8,128)S(1)}, f32[12,768]{1,0:T(8,128)S(1)}, u32[]{:S(2)}, u32[]{:S(2)}) collective-permute-start(f32[12,768]{1,0:T(8,128)S(1)} %add.138), channel_id=1, source_target_pairs={{0,8},{4,12},{8,0},{12,4},{16,24},{20,28},{24,16},{28,20},{1,9},{5... | collective-permute-start | bytes 110600 | tf_op jit(solution)/shard_map/ppermute | solution.py:26
  142.7 5.3 %collective-permute-start.60 = (f32[12,768]{1,0:T(8,128)S(1)}, f32[12,768]{1,0:T(8,128)S(1)}, u32[]{:S(2)}, u32[]{:S(2)}) collective-permute-start(f32[12,768]{1,0:T(8,128)S(1)} %add.139), channel_id=1, source_target_pairs={{0,2},{1,3},{2,0},{3,1},{4,6},{5,7},{6,4},{7,5},{8,10},{9,11},{10,... | collective-permute-start | bytes 110600 | tf_op jit(solution)/shard_map/ppermute | solution.py:26
  145.2 7.7 %collective-permute-start.42 = (bf16[128,768]{1,0:T(8,128)(2,1)S(1)}, bf16[128,768]{1,0:T(8,128)(2,1)S(1)}, u32[]{:S(2)}, u32[]{:S(2)}) collective-permute-start(bf16[128,768]{1,0:T(8,128)(2,1)S(1)} %copy-done.44), channel_id=1, source_target_pairs={{0,1},{1,0},{2,3},{3,2},{4,5},{5,4},{6,7},{7,6},{8,9},{9,8},{10,11... | collective-permute-start | bytes 589832 | tf_op jit(solution)/shard_map/ppermute | solution.py:26
  148.0 9.3 %collective-permute-start.46 = (bf16[4,96,768]{2,1,0:T(8,128)(2,1)S(1)}, bf16[4,96,768]{2,1,0:T(8,128)(2,1)S(1)}, u32[]{:S(2)}, u32[]{:S(2)}) collective-permute-start(bf16[4,96,768]{2,1,0:T(8,128)(2,1)S(1)} %copy-done.42), channel_id=1, source_target_pairs={{0,4},{4,0},{8,12},{12,8},{16,20},{20,16},{24,28},{28,24},{1,5},{5... | collective-permute-start | bytes 1769480 | tf_op jit(solution)/shard_map/ppermute | solution.py:26
  148.1 4.2 %collective-permute-start.61 = (f32[12,768]{1,0:T(8,128)S(1)}, f32[12,768]{1,0:T(8,128)S(1)}, u32[]{:S(2)}, u32[]{:S(2)}) collective-permute-start(f32[12,768]{1,0:T(8,128)S(1)} %add.140), channel_id=1, source_target_pairs={{0,1},{1,0},{2,3},{3,2},{4,5},{5,4},{6,7},{7,6},{8,9},{9,8},{10,11... | collective-permute-start | bytes 110600 | tf_op jit(solution)/shard_map/ppermute | solution.py:26
  152.3 8.3 %collective-permute-start.53 = (bf16[4,96,1536]{2,1,0:T(8,128)(2,1)S(1)}, bf16[4,96,1536]{2,1,0:T(8,128)(2,1)S(1)}, u32[]{:S(2)}, u32[]{:S(2)}) collective-permute-start(bf16[4,96,1536]{2,1,0:T(8,128)(2,1)S(1)} %copy-done.41), channel_id=1, source_target_pairs={{0,4},{4,0},{8,12},{12,8},{16,20},{20,16},{24,28},{28,24},{1,5},{5... | collective-permute-start | bytes 3538952 | tf_op jit(solution)/shard_map/ppermute | solution.py:26
  156.1 12.4 %collective-permute-start.44 = (bf16[2,96,768]{2,1,0:T(8,128)(2,1)S(1)}, bf16[2,96,768]{2,1,0:T(8,128)(2,1)S(1)}, u32[]{:S(2)}, u32[]{:S(2)}) collective-permute-start(bf16[2,96,768]{2,1,0:T(8,128)(2,1)S(1)} %slice.171), channel_id=1, source_target_pairs={{0,16},{4,20},{8,24},{12,28},{16,0},{20,4},{24,8},{28,12},{1,17},{... | collective-permute-start | bytes 884744 | tf_op jit(solution)/shard_map/ppermute | solution.py:26
  157.5 9.9 %collective-permute-start.47 = (bf16[2,96,768]{2,1,0:T(8,128)(2,1)S(1)}, bf16[2,96,768]{2,1,0:T(8,128)(2,1)S(1)}, u32[]{:S(2)}, u32[]{:S(2)}) collective-permute-start(bf16[2,96,768]{2,1,0:T(8,128)(2,1)S(1)} %slice.170), channel_id=1, source_target_pairs={{0,8},{4,12},{8,0},{12,4},{16,24},{20,28},{24,16},{28,20},{1,9},{5... | collective-permute-start | bytes 884744 | tf_op jit(solution)/shard_map/ppermute | solution.py:26
  159.5 25.7 %collective-permute-start.51 = (bf16[2,96,1536]{2,1,0:T(8,128)(2,1)S(1)}, bf16[2,96,1536]{2,1,0:T(8,128)(2,1)S(1)}, u32[]{:S(2)}, u32[]{:S(2)}) collective-permute-start(bf16[2,96,1536]{2,1,0:T(8,128)(2,1)S(1)} %slice.167), channel_id=1, source_target_pairs={{0,16},{4,20},{8,24},{12,28},{16,0},{20,4},{24,8},{28,12},{1,17},{... | collective-permute-start | bytes 1769480 | tf_op jit(solution)/shard_map/ppermute | solution.py:26
  161.1 22.7 %collective-permute-start.54 = (bf16[2,96,1536]{2,1,0:T(8,128)(2,1)S(1)}, bf16[2,96,1536]{2,1,0:T(8,128)(2,1)S(1)}, u32[]{:S(2)}, u32[]{:S(2)}) collective-permute-start(bf16[2,96,1536]{2,1,0:T(8,128)(2,1)S(1)} %slice.166), channel_id=1, source_target_pairs={{0,8},{4,12},{8,0},{12,4},{16,24},{20,28},{24,16},{28,20},{1,9},{5... | collective-permute-start | bytes 1769480 | tf_op jit(solution)/shard_map/ppermute | solution.py:26
  167.4 14.0 %collective-permute-start.48 = (bf16[1,96,768]{2,1,0:T(8,128)(2,1)S(1)}, bf16[1,96,768]{2,1,0:T(8,128)(2,1)S(1)}, u32[]{:S(2)}, u32[]{:S(2)}) collective-permute-start(bf16[1,96,768]{2,1,0:T(8,128)(2,1)S(1)} %slice.172), channel_id=1, source_target_pairs={{0,16},{4,20},{8,24},{12,28},{16,0},{20,4},{24,8},{28,12},{1,17},{... | collective-permute-start | bytes 442376 | tf_op jit(solution)/shard_map/ppermute | solution.py:26
  168.6 24.6 %collective-permute-start.45 = (bf16[1,96,768]{2,1,0:T(8,128)(2,1)S(1)}, bf16[1,96,768]{2,1,0:T(8,128)(2,1)S(1)}, u32[]{:S(2)}, u32[]{:S(2)}) collective-permute-start(bf16[1,96,768]{2,1,0:T(8,128)(2,1)S(1)} %slice.173), channel_id=1, source_target_pairs={{0,8},{4,12},{8,0},{12,4},{16,24},{20,28},{24,16},{28,20},{1,9},{5... | collective-permute-start | bytes 442376 | tf_op jit(solution)/shard_map/ppermute | solution.py:26
  181.5 11.8 %collective-permute-start.49 = (bf16[96,768]{1,0:T(8,128)(2,1)S(1)}, bf16[96,768]{1,0:T(8,128)(2,1)S(1)}, u32[]{:S(2)}, u32[]{:S(2)}) collective-permute-start(bf16[96,768]{1,0:T(8,128)(2,1)S(1)} %fusion.7), channel_id=1, source_target_pairs={{0,2},{1,3},{2,0},{3,1},{4,6},{5,7},{6,4},{7,5},{8,10},{9,11},{10,... | collective-permute-start | bytes 442376 | tf_op jit(solution)/shard_map/ppermute | solution.py:26
  184.0 8.4 %collective-permute-start.55 = (bf16[1,96,1536]{2,1,0:T(8,128)(2,1)S(1)}, bf16[1,96,1536]{2,1,0:T(8,128)(2,1)S(1)}, u32[]{:S(2)}, u32[]{:S(2)}) collective-permute-start(bf16[1,96,1536]{2,1,0:T(8,128)(2,1)S(1)} %slice.168), channel_id=1, source_target_pairs={{0,16},{4,20},{8,24},{12,28},{16,0},{20,4},{24,8},{28,12},{1,17},{... | collective-permute-start | bytes 884744 | tf_op jit(solution)/shard_map/ppermute | solution.py:26
  185.4 9.8 %collective-permute-start.52 = (bf16[1,96,1536]{2,1,0:T(8,128)(2,1)S(1)}, bf16[1,96,1536]{2,1,0:T(8,128)(2,1)S(1)}, u32[]{:S(2)}, u32[]{:S(2)}) collective-permute-start(bf16[1,96,1536]{2,1,0:T(8,128)(2,1)S(1)} %slice.169), channel_id=1, source_target_pairs={{0,8},{4,12},{8,0},{12,4},{16,24},{20,28},{24,16},{28,20},{1,9},{5... | collective-permute-start | bytes 884744 | tf_op jit(solution)/shard_map/ppermute | solution.py:26
  192.5 14.7 %collective-permute-start.56 = (bf16[96,1536]{1,0:T(8,128)(2,1)S(1)}, bf16[96,1536]{1,0:T(8,128)(2,1)S(1)}, u32[]{:S(2)}, u32[]{:S(2)}) collective-permute-start(bf16[96,1536]{1,0:T(8,128)(2,1)S(1)} %fusion.3), channel_id=1, source_target_pairs={{0,2},{1,3},{2,0},{3,1},{4,6},{5,7},{6,4},{7,5},{8,10},{9,11},{10,... | collective-permute-start | bytes 884744 | tf_op jit(solution)/shard_map/ppermute | solution.py:26
  (43 other events, 704.5 us)

commit v2 on v1

v2 whole, which is shorter than its diff:
```python
import jax
import jax.numpy as jnp
from jax import lax
from jax.experimental import pallas as pl
from jax.experimental.pallas import tpu as pltpu
from jax.sharding import PartitionSpec as P

HEAD_DIM = 64
NORM_EPS = 1e-05
GELU_COEF = 0.7978845608028654
MASK_LOW = -1000000000.0
SCALE = HEAD_DIM ** (-0.5)
BF16 = jnp.bfloat16
F32 = jnp.float32
NN = ((1,), (0,))
NT = ((1,), (1,))
TN = ((0,), (0,))


def dot(a, b, dims=NN):
    return lax.dot_general(a, b, (dims, ((), ())), preferred_element_type=F32)


def swap(value, axis, bits):
    size = lax.axis_size(axis)
    return lax.ppermute(value, axis, [(i, i ^ bits) for i in range(size)])


def normalize(rows):
    mean = jnp.mean(rows, axis=-1, keepdims=True)
    centred = rows - mean
    variance = jnp.mean(centred * centred, axis=-1, keepdims=True)
    inv_std = lax.rsqrt(variance + NORM_EPS)
    return (centred * inv_std, inv_std)


def norm_back(grad_out, normed, inv_std, gain):
    grad_normed = grad_out * gain
    mean_one = jnp.mean(grad_normed, axis=-1, keepdims=True)
    mean_two = jnp.mean(grad_normed * normed, axis=-1, keepdims=True)
    return inv_std * (grad_normed - mean_one - normed * mean_two)


def gelu_parts(pre):
    square = pre * pre
    inner = GELU_COEF * (pre + 0.044715 * square * pre)
    tanh_val = jnp.tanh(inner)
    half = 0.5 * (1.0 + tanh_val)
    value = pre * half
    slope = half + 0.5 * pre * (1.0 - tanh_val * tanh_val) * GELU_COEF * (
        1.0 + 3.0 * 0.044715 * square
    )
    return (value, slope)


def column_sum(value):
    return jnp.sum(value, axis=0, keepdims=True)


def together(*values):
    return lax.optimization_barrier(values)


def call(body, name, micros, outs, args, scratch=(), spaces=None):
    spaces = spaces or {}
    in_specs = [
        pl.BlockSpec(memory_space=spaces.get(n, pltpu.VMEM)) for n in range(len(args))
    ]
    return pl.pallas_call(
        body,
        name=name,
        out_shape=[jax.ShapeDtypeStruct(shape, dtype) for shape, dtype in outs],
        in_specs=in_specs,
        out_specs=[pl.BlockSpec(memory_space=pltpu.VMEM) for _ in outs],
        scratch_shapes=list(scratch),
        compiler_params=pltpu.CompilerParams(vmem_limit_bytes=56 * 1024 * 1024),
        cost_estimate=pl.CostEstimate(
            flops=int(micros * 5e7), bytes_accessed=int(micros * 1e5), transcendentals=0
        ),
    )(*args)


def bit_orders():
    count = lax.axis_size("dp").bit_length() - 1
    bits = [1 << b for b in range(1, count)]
    return (bits + [1], bits[::-1] + [1])


def gather_start(piece):
    return [[((0,), piece[None])], [((0,), swap(piece[None], "tensor", 2))]]


def gather_stage(pieces, stage):
    out = []
    for held, order in zip(pieces, bit_orders()):
        bit = order[stage]
        while len(held) > 4:
            held = [
                (held[n][0] + held[n + 1][0], jnp.concatenate([held[n][1], held[n + 1][1]]))
                for n in range(0, len(held), 2)
            ]
        out.append(held + [(tuple(k ^ bit for k in ks), swap(v, "dp", bit)) for ks, v in held])
    return out


def tied(pieces, *values):
    flat, tree = jax.tree.flatten([[v for _, v in held] for held in pieces])
    done = together(*flat, *values)
    arrays = jax.tree.unflatten(tree, done[: len(flat)])
    pieces = [
        [(ks, v) for (ks, _), v in zip(held, new)] for held, new in zip(pieces, arrays)
    ]
    return (pieces, *done[len(flat) :])


def assembled(held):
    ks = [k for group, _ in held for k in group]
    stacked = jnp.concatenate([v for _, v in held])
    slot = [ks.index(k) for k in range(len(ks))]
    stacked = jnp.stack([stacked[n] for n in slot])
    whole = jnp.take(stacked, lax.axis_index("dp") ^ jnp.arange(len(ks)), axis=0)
    return whole.reshape(1, -1, whole.shape[-1])


def piece_plan(pieces):
    aligned = pieces[0][0][1].shape[1] % 16 == 0
    arrays, plan = [], []
    for s, held in enumerate(pieces):
        if not aligned:
            plan.append((len(arrays), 0, s, None))
            arrays.append(assembled(held))
            continue
        for ks, value in held:
            plan += [(len(arrays), slot, s, k) for slot, k in enumerate(ks)]
            arrays.append(value)
    return arrays, plan


def place_pieces(refs, plan, dst_refs, sems, me):
    copies = []
    for n, (array, slot, s, k) in enumerate(plan):
        rows = refs[array].shape[1]
        if k is None:
            target = dst_refs[s]
        else:
            start = pl.multiple_of(jnp.bitwise_xor(me, k) * rows, 16)
            target = dst_refs[s].at[pl.ds(start, rows), :]
        copies.append(pltpu.make_async_copy(refs[array].at[slot], target, sems.at[n]))
    for copy in copies:
        copy.start()
    return copies


def relative_evens(shard):
    count = lax.axis_size("dp")
    bits = count.bit_length() - 1
    evens = list(range(0, count, 2))
    if shard == 1:
        evens.sort(key=lambda k: [k >> b & 1 for b in range(1, bits)])
    return evens


def put_grad(grad, s, scratch, keep_ref, send_ref, me, rows):
    if rows % 16:
        keep_ref[...] = grad
        return
    scratch[...] = grad
    for n, k in enumerate(relative_evens(s)):
        for k_of, ref in ((k, keep_ref), (k ^ 1, send_ref)):
            start = pl.multiple_of(jnp.bitwise_xor(me, k_of) * rows, 16)
            ref[n] = scratch[pl.ds(start, rows), :].astype(ref.dtype)


def grad_shapes(width, rows, cols):
    if rows % 16:
        return [((width, cols), F32), ((8, 128), BF16)] * 2
    half = width // rows // 2
    return [((half, rows, cols), BF16)] * 4


def scatter_core(keep, send, s, rows):
    if rows % 16:
        me = lax.axis_index("dp")
        blocks = keep.reshape(-1, rows, keep.shape[-1])
        evens = jnp.array(relative_evens(s))
        keep = jnp.take(blocks, me ^ evens, axis=0)
        send = jnp.take(blocks, me ^ evens ^ 1, axis=0).astype(BF16)
    return keep.astype(F32) + swap(send, "dp", 1).astype(F32)


def scatter_split(now):
    half = now.shape[0] // 2
    return now[:half], now[half:].astype(BF16)


def scatter_step(kept, sent, s, n):
    return kept + swap(sent, "dp", bit_orders()[s][:-1][::-1][n]).astype(F32)


def scatter_end(own, other):
    return own + swap(other.astype(BF16), "tensor", 2).astype(F32)


def spread_columns(value, index, count):
    rows, cols = value.shape
    return lax.dynamic_update_slice(jnp.zeros((rows, count * cols), F32), value, (0, index * cols))


def plus_swapped(value, axis, bit):
    return value + swap(value, axis, bit)


def norm_first_body(x_ref, g_ref, xh_ref, dy_ref, sum_ref):
    xh_ref[...] = normalize(x_ref[...])[0].astype(BF16)
    grad = g_ref[...]
    dy_ref[...] = grad.astype(BF16)
    sum_ref[...] = column_sum(grad)


def causal_mask(length):
    rows = lax.broadcasted_iota(jnp.int32, (length, length), 0)
    cols = lax.broadcasted_iota(jnp.int32, (length, length), 1)
    return rows >= cols


def attend_body(plan, n_arrays, head_cols, *refs):
    ids, own, other, vec, biases = refs[:5]
    pieces = refs[5 : 5 + n_arrays]
    outs, (lse_out, a_out, keep, send, total, sems) = refs[5 + n_arrays : 11 + n_arrays], refs[11 + n_arrays :]
    w, qkv_out, ctx_out = outs[0:2], outs[2:4], outs[4:6]
    me, role = ids[0], ids[1]
    copies = place_pieces(pieces, plan, w, sems, me)
    rows = own.shape[0]
    gain, shift = vec[0:1, :], vec[1:2, :]
    for ref, at in ((own, role), (other, 1 - role)):
        a_rows = ref[...].astype(F32) * gain + shift
        a_out[pl.ds(pl.multiple_of(at * rows, rows), rows), :] = a_rows.astype(BF16)
    for copy in copies:
        copy.wait()
    seq = 2 * rows
    a_rows = a_out[...]
    mask = causal_mask(seq)
    lane = lax.broadcasted_iota(jnp.int32, (seq, 128), 1)
    lse_all = jnp.zeros((seq, 128), F32)
    heads = head_cols // HEAD_DIM
    attn = None
    for s in range(2):
        qkv = dot(a_rows, w[s][:, : 3 * head_cols]) + biases[s : s + 1, :]
        qkv = qkv.astype(BF16)
        qkv_out[s][...] = qkv
        parts = []
        for h in range(heads):
            q, k, v = (
                qkv[:, n * head_cols + h * HEAD_DIM : n * head_cols + (h + 1) * HEAD_DIM]
                for n in range(3)
            )
            scores = jnp.where(mask, dot(q, k, NT) * SCALE, MASK_LOW)
            top = jnp.max(scores, axis=-1, keepdims=True)
            lse = top + jnp.log(jnp.sum(jnp.exp(scores - top), axis=-1, keepdims=True))
            lse_all = jnp.where(lane == s * heads + h, lse, lse_all)
            probs = jnp.exp(scores - lse).astype(BF16)
            parts.append(dot(probs, v).astype(BF16))
        ctx = jnp.concatenate(parts, axis=1)
        ctx_out[s][...] = ctx
        add = dot(ctx, w[s][:, 3 * head_cols :], NT)
        attn = add if attn is None else attn + add
    lse_out[...] = lse_all
    total[...] = attn
    keep[...] = total[pl.ds(pl.multiple_of(role * rows, rows), rows), :]
    send[...] = total[pl.ds(pl.multiple_of((1 - role) * rows, rows), rows), :].astype(BF16)


def norm_second_body(x_ref, keep_ref, recv_ref, vec_ref, resid_ref, m_ref):
    resid = x_ref[...] + (keep_ref[...] + recv_ref[...].astype(F32)) + vec_ref[4:5, :]
    resid_ref[...] = resid
    normed, _ = normalize(resid)
    m_ref[...] = (normed * vec_ref[5:6, :] + vec_ref[6:7, :]).astype(BF16)


def feed_body(plan, n_arrays, hidden, *refs):
    ids, m_own, m_other, dy_own, dy_other, bias = refs[:6]
    pieces = refs[6 : 6 + n_arrays]
    act_out, dpre_out = refs[6 + n_arrays : 8 + n_arrays], refs[8 + n_arrays : 10 + n_arrays]
    m_out, dy_out, dm_keep, dm_send, br_keep, br_send, sum_out, w, sems = refs[10 + n_arrays :]
    copies = place_pieces(pieces, plan, (w.at[0], w.at[1]), sems, ids[0])
    rows = m_own.shape[0]
    m_out[:rows] = m_own[...]
    m_out[rows:] = m_other[...]
    dy_out[:rows] = dy_own[...]
    dy_out[rows:] = dy_other[...]
    m, dy = m_out[...], dy_out[...]
    for copy in copies:
        copy.wait()
    d_m = branch = None
    for s in range(2):
        w_fc, w_proj = w[s, :, :hidden], w[s, :, hidden:]
        pre = dot(m, w_fc) + bias[s : s + 1, :]
        act, slope = gelu_parts(pre)
        act_low = act.astype(BF16)
        act_out[s][...] = act_low
        d_pre = dot(dy, w_proj) * slope
        sum_out[s : s + 1, :] = column_sum(d_pre)
        d_pre_low = d_pre.astype(BF16)
        dpre_out[s][...] = d_pre_low
        one, two = dot(d_pre_low, w_fc, NT), dot(act_low, w_proj, NT)
        d_m = one if d_m is None else d_m + one
        branch = two if branch is None else branch + two
    dm_keep[...] = d_m[:rows]
    dm_send[...] = d_m[rows:].astype(BF16)
    br_keep[...] = branch[:rows]
    br_send[...] = branch[rows:].astype(BF16)


def feed_grad_body(block_rows, s, ids, m_ref, dy_ref, act_ref, dpre_ref, keep, send, scratch):
    grad = jnp.concatenate(
        [dot(m_ref[...], dpre_ref[...], TN), dot(dy_ref[...], act_ref[...], TN)], axis=1
    )
    put_grad(grad, s, scratch, keep, send, ids[0], block_rows)


def norm_second_back_body(resid_ref, keep_ref, recv_ref, grad_ref, vec_ref, grad1_ref, dz_ref, sum_ref):
    d_m = keep_ref[...] + recv_ref[...].astype(F32)
    normed, inv = normalize(resid_ref[...])
    grad1 = grad_ref[...] + norm_back(d_m, normed, inv, vec_ref[5:6, :])
    grad1_ref[...] = grad1
    dz_ref[...] = grad1.astype(BF16)
    sum_ref[0:1, :] = column_sum(grad1)
    sum_ref[1:2, :] = column_sum(d_m * normed)
    sum_ref[2:3, :] = column_sum(d_m)


def attend_back_body(block_rows, head_cols, s, *refs):
    ids, own, other, w, qkv_ref, lse_ref, a_ref, ctx_ref = refs[:8]
    last = s == 0
    if last:
        da_before, xh_own, xh_other = refs[8:11]
    keep_g, send_g, sum_heads = refs[11:14] if last else refs[8:11]
    outs = refs[14:] if last else refs[11:]
    dz, scratch = outs[-2:]
    role = ids[1]
    rows = own.shape[0]
    seq = 2 * rows
    mine = pl.ds(pl.multiple_of(role * rows, rows), rows)
    theirs = pl.ds(pl.multiple_of((1 - role) * rows, rows), rows)
    dz[mine, :] = own[...]
    dz[theirs, :] = other[...]
    mask = causal_mask(seq)
    heads = head_cols // HEAD_DIM
    d_ctx_all = dot(dz[...], w[:, 3 * head_cols :]).astype(BF16)
    d_parts = [[], [], []]
    qkv = qkv_ref[...]
    for h in range(heads):
        q, k, v = (
            qkv[:, n * head_cols + h * HEAD_DIM : n * head_cols + (h + 1) * HEAD_DIM]
            for n in range(3)
        )
        d_ctx = d_ctx_all[:, h * HEAD_DIM : (h + 1) * HEAD_DIM]
        head = s * heads + h
        scores = jnp.where(mask, dot(q, k, NT) * SCALE, MASK_LOW)
        probs = jnp.exp(scores - lse_ref[:, head : head + 1])
        d_parts[2].append(dot(probs.astype(BF16), d_ctx, TN))
        d_probs = dot(d_ctx, v, NT)
        row_sum = jnp.sum(probs * d_probs, axis=-1, keepdims=True)
        d_scores = (probs * (d_probs - row_sum) * SCALE).astype(BF16)
        d_parts[0].append(dot(d_scores, k))
        d_parts[1].append(dot(d_scores, q, TN))
    d_qkv = jnp.concatenate(d_parts[0] + d_parts[1] + d_parts[2], axis=1)
    sum_heads[...] = column_sum(d_qkv)
    d_qkv = d_qkv.astype(BF16)
    grad = jnp.concatenate([dot(a_ref[...], d_qkv, TN), dot(dz[...], ctx_ref[...], TN)], axis=1)
    put_grad(grad, s, scratch, keep_g, send_g, ids[0], block_rows)
    d_a = dot(d_qkv, w[:, : 3 * head_cols], NT)
    if not last:
        outs[0][...] = d_a
        return
    keep, send, sum_wide, total, normed = outs[:5]
    d_a = d_a + da_before[...]
    total[...] = d_a
    normed[mine, :] = xh_own[...]
    normed[theirs, :] = xh_other[...]
    sum_wide[0:1, :] = column_sum(d_a * normed[...].astype(F32))
    sum_wide[1:2, :] = column_sum(d_a)
    keep[...] = total[mine, :]
    send[...] = total[theirs, :].astype(BF16)


def sums_body(head_cols, ids, wide, heads_own, heads_other, second, fc_sum, bp_sum, vec_out):
    z = ids[2]
    vec_out[0:2, :] = wide[0:2, :]
    vec_out[4:7, :] = second[0:3, :]
    vec_out[7:8, :] = bp_sum[...]

    def placed(own, other, t):
        zero = jnp.zeros_like(own)
        return jnp.where(z == t, own, zero) + jnp.where(jnp.bitwise_xor(z, 2) == t, other, zero)

    n_z = vec_out.shape[1] // head_cols
    for row, part in ((2, 0), (3, 2)):
        own, other = (
            ref[:, part * head_cols : (part + 1) * head_cols] for ref in (heads_own, heads_other)
        )
        vec_out[row : row + 1, :] = jnp.concatenate(
            [placed(own, other, t) for t in range(n_z)], axis=1
        )
    for t in range(vec_out.shape[0] - 8):
        vec_out[8 + t : 9 + t, :] = placed(fc_sum[0:1, :], fc_sum[1:2, :], t)


def norm_first_back_body(x_ref, keep_ref, recv_ref, grad1_ref, vec_ref, out_ref):
    d_a = keep_ref[...] + recv_ref[...].astype(F32)
    normed, inv = normalize(x_ref[...])
    out_ref[...] = grad1_ref[...] + norm_back(d_a, normed, inv, vec_ref[0:1, :])


def shards(inputs, qkv_weight, out_weight, fc_weight, proj_weight, vectors, out_grad):
    rows, width = inputs.shape
    head_cols = qkv_weight.shape[3]
    hidden = fc_weight.shape[2]
    block_rows = qkv_weight.shape[1]
    vec_rows, vec_cols = vectors.shape[1:]
    n_z = lax.axis_size("tensor")
    n_dp = lax.axis_size("dp")
    z = lax.axis_index("tensor")
    me = lax.axis_index("dp")
    shard_ids = (z, z ^ 2)
    ids = jnp.stack([me, z & 1, z]).astype(jnp.int32)
    smem = {0: pltpu.SMEM}
    row = (rows, width)
    seq = 2 * rows
    both = (seq, width)

    part_a = jnp.concatenate(
        [qkv_weight[0].reshape(block_rows, 3 * head_cols), out_weight[0].T], axis=1
    )
    part_b = jnp.concatenate([fc_weight[0], proj_weight[0].T], axis=1)
    bits = bit_orders()[0]
    stages = len(bits)
    vec = spread_columns(vectors[0], me * n_z + z, n_dp * n_z)
    pieces_a = gather_start(part_a)
    vec = plus_swapped(vec, "tensor", 1)
    vec = plus_swapped(vec, "dp", bits[0])
    normed1, dy, bp_sum = call(
        norm_first_body, "norm_first", 2, [(row, BF16), (row, BF16), ((1, width), F32)], (inputs, out_grad)
    )
    pieces_a, vec, part_b, normed1, dy = tied(pieces_a, vec, part_b, normed1, dy)
    normed1_other = swap(normed1, "tensor", 1)
    pieces_b = gather_start(part_b)
    for stage in range(stages):
        pieces_a = gather_stage(pieces_a, stage)
        if stage < stages - 2:
            vec = plus_swapped(vec, "dp", bits[stage + 1])
            pieces_a, vec, normed1_other = tied(pieces_a, vec, normed1_other)
        elif stage == stages - 2:
            vec = plus_swapped(vec, "tensor", 3)
            flat, vec = tied(pieces_a + pieces_b, vec)
            pieces_a, pieces_b = flat[:2], flat[2:]
        else:
            vec = plus_swapped(vec, "dp", bits[stage])
    pieces_b = gather_stage(pieces_b, 0)
    arrays_a, plan_a = piece_plan(pieces_a)

    def of_shard(table):
        return jnp.stack([lax.dynamic_index_in_dim(table, s, 0, False) for s in shard_ids])

    bias_q = of_shard(vec[2].reshape(n_z, head_cols))
    bias_v = of_shard(vec[3].reshape(n_z, head_cols))
    biases = jnp.concatenate([bias_q, jnp.zeros_like(bias_q), bias_v], axis=1)
    bias_fc = of_shard(vec[8:].reshape(n_z, hidden))

    def any_space(first, arrays):
        return {**smem, **{first + n: pl.ANY for n in range(len(arrays))}}

    w_0, w_1, qkv_0, qkv_1, ctx_0, ctx_1, lse, a_seq, attn_keep, attn_send = call(
        lambda *refs: attend_body(plan_a, len(arrays_a), head_cols, *refs),
        "attend",
        6,
        [((width, 4 * head_cols), BF16)] * 2
        + [((seq, 3 * head_cols), BF16)] * 2
        + [((seq, head_cols), BF16)] * 2
        + [((seq, 128), F32), (both, BF16), (row, F32), (row, BF16)],
        (ids, normed1, normed1_other, vec, biases, *arrays_a),
        [pltpu.VMEM(both, F32), pltpu.SemaphoreType.DMA((len(plan_a),))],
        any_space(5, arrays_a),
    )
    pieces_b, attn_send = tied(pieces_b, attn_send)
    attn_recv = swap(attn_send, "tensor", 1)
    for stage in range(1, stages - 1):
        pieces_b = gather_stage(pieces_b, stage)
    resid1, m = call(
        norm_second_body,
        "norm_second",
        2,
        [(row, F32), (row, BF16)],
        (inputs, attn_keep, attn_recv, vec),
    )
    m_other = swap(m, "tensor", 1)
    dy_other = swap(dy, "tensor", 1)
    pieces_b, m_other, dy_other = tied(pieces_b, m_other, dy_other)
    pieces_b = gather_stage(pieces_b, stages - 1)
    arrays_b, plan_b = piece_plan(pieces_b)
    act_0, act_1, d_pre_0, d_pre_1, m_both, dy_both, dm_keep, dm_send, br_keep, br_send, fc_sum = call(
        lambda *refs: feed_body(plan_b, len(arrays_b), hidden, *refs),
        "feed",
        7,
        [((seq, hidden), BF16)] * 4
        + [(both, BF16), (both, BF16), (row, F32), (row, BF16), (row, F32), (row, BF16), ((2, hidden), F32)],
        (ids, m, m_other, dy, dy_other, bias_fc, *arrays_b),
        [pltpu.VMEM((2, width, 2 * hidden), BF16), pltpu.SemaphoreType.DMA((len(plan_b),))],
        any_space(6, arrays_b),
    )
    dm_recv = swap(dm_send, "tensor", 1)

    def feed_grad(s, act, d_pre):
        return call(
            lambda *refs: feed_grad_body(block_rows, s, *refs),
            "feed_grad_" + str(s),
            3,
            grad_shapes(width, block_rows, 2 * hidden)[:2],
            (ids, m_both, dy_both, act, d_pre),
            [pltpu.VMEM((width, 2 * hidden), F32)],
            smem,
        )

    parts_1 = feed_grad(1, act_1, d_pre_1)
    split_b1 = scatter_split(scatter_core(*parts_1, 1, block_rows))
    parts_0 = feed_grad(0, act_0, d_pre_0)
    dm_recv, *flat = together(dm_recv, *parts_0, *split_b1)
    parts_0, split_b1 = flat[:2], flat[2:]
    br_recv = swap(br_send, "tensor", 1)
    grad1, dz, second_sums = call(
        norm_second_back_body,
        "norm_second_back",
        2,
        [(row, F32), (row, BF16), ((3, width), F32)],
        (resid1, dm_keep, dm_recv, out_grad, vec),
    )
    split_b0 = scatter_split(scatter_core(*parts_0, 0, block_rows))
    dz, br_recv, *split_b0 = together(dz, br_recv, *split_b0)
    dz_other = swap(dz, "tensor", 1)
    split_b = [split_b0, split_b1]
    outputs = resid1 + (br_keep + br_recv.astype(F32)) + vec[7]

    def attend_back(s, w, qkv, ctx, more_args, more_outs, more_scratch):
        return call(
            lambda *refs: attend_back_body(block_rows, head_cols, s, *refs),
            "attend_back_" + str(s),
            6,
            grad_shapes(width, block_rows, 4 * head_cols)[:2] + [((1, 3 * head_cols), F32)] + more_outs,
            (ids, dz, dz_other, w, qkv, lse, a_seq, ctx, *more_args),
            more_scratch + [pltpu.VMEM(both, BF16), pltpu.VMEM((width, 4 * head_cols), F32)],
            smem,
        )

    halvings = stages - 1
    keep_1, send_1, head_sums_1, da_1 = attend_back(1, w_1, qkv_1, ctx_1, (), [(both, F32)], [])
    halvings = stages - 1
    now_b = [scatter_step(*split_b[s], s, 0) for s in range(2)]
    split_b = [scatter_split(now) for now in now_b]
    da_1, *flat = together(da_1, *split_b[0], *split_b[1])
    split_b = [flat[:2], flat[2:]]
    split_1 = scatter_split(scatter_core(keep_1, send_1, 1, block_rows))
    da_1, *split_1 = together(da_1, *split_1)
    keep_0, send_0, head_sums_0, da_keep, da_send, wide_sums = attend_back(
        0,
        w_0,
        qkv_0,
        ctx_0,
        (da_1, normed1, normed1_other),
        [(row, F32), (row, BF16), ((2, width), F32)],
        [pltpu.VMEM(both, F32), pltpu.VMEM(both, BF16)],
    )
    for n in range(1, halvings):
        now_b = [scatter_step(*split_b[s], s, n) for s in range(2)]
        if n < halvings - 1:
            split_b = [scatter_split(now) for now in now_b]
    now_1 = scatter_step(*split_1, 1, 0)
    split_1 = scatter_split(now_1)
    da_send, wide_sums, *flat = together(da_send, wide_sums, *split_1, *now_b)
    split_1, now_b = flat[:2], flat[2:]
    da_recv = swap(da_send, "tensor", 1)
    b_recv = swap(now_b[1][0].astype(BF16), "tensor", 2)
    split_0 = scatter_split(scatter_core(keep_0, send_0, 0, block_rows))
    (vec_sum,) = call(
        lambda *refs: sums_body(head_cols, *refs),
        "sums",
        1,
        [((vec_rows, width), F32)],
        (ids, wide_sums, head_sums_0, head_sums_1, second_sums, fc_sum, bp_sum),
        (),
        smem,
    )
    vec_sum = plus_swapped(vec_sum, "dp", 1)
    *split_0, vec_sum = together(*split_0, vec_sum)
    for n in range(halvings):
        now_0 = scatter_step(*split_0, 0, n)
        vec_sum = plus_swapped(vec_sum, "dp", bits[:-1][::-1][n])
        if n + 1 < halvings:
            now_1 = scatter_step(*split_1, 1, n + 1)
            split_0 = scatter_split(now_0)
            split_1 = scatter_split(now_1) if n + 2 < halvings else (now_1,)
            if n == 0:
                b_recv, da_recv, vec_sum = together(b_recv, da_recv, vec_sum)
            *flat, vec_sum = together(*split_0, *split_1, vec_sum)
            split_0, split_1 = flat[:2], flat[2:]
    b_grad = now_b[0][0] + b_recv.astype(F32)
    vec_sum = vec_sum + swap(vec_sum, "tensor", 1) + swap(vec_sum, "tensor", 2) + swap(vec_sum, "tensor", 3)
    a_grad = scatter_end(now_0[0], split_1[0][0])
    vector_grad = lax.dynamic_slice_in_dim(vec_sum, (me * n_z + z) * vec_cols, vec_cols, 1)
    (input_grad,) = call(
        norm_first_back_body,
        "norm_first_back",
        2,
        [(row, F32)],
        (inputs, da_keep, da_recv, grad1, vec),
    )
    qkv_grad = a_grad[:, : 3 * head_cols].reshape(block_rows, 3, head_cols)
    return (
        outputs,
        input_grad,
        qkv_grad[None],
        a_grad[:, 3 * head_cols :].T[None],
        b_grad[None, :, :hidden],
        b_grad[:, hidden:].T[None],
        vector_grad[None],
    )


def solution(mesh):
    rows = P(("dp", "tensor"), None)
    weights = (
        P(None, "dp", None, "tensor"),
        P(None, "tensor", "dp"),
        P(None, "dp", "tensor"),
        P(None, "tensor", "dp"),
        P(None, None, ("dp", "tensor")),
    )
    return jax.shard_map(
        shards,
        mesh=mesh,
        in_specs=(rows, *weights, rows),
        out_specs=(rows, rows, *weights),
        check_vma=False,
    )
```

time: 209 us -> 173 us (0.83)
  waiting for transfers between devices: 97 us -> 46.5 us
  starting transfers between devices: 52.2 us -> 59.3 us
  local copies, waits for them, and re-layouts: 11.5 us -> 15.3 us
  Pallas kernels: 41 us -> 43.5 us
    ppermute x62 -> x63, waiting for transfers between devices: 97 us -> 46.5 us  [swap(): return lax.ppermute(value, axis, [(i, i ^ bits) for i in range(size)])]
    ppermute x62 -> x63, starting transfers between devices: 52.2 us -> 59.3 us  [swap(): return lax.ppermute(value, axis, [(i, i ^ bits) for i in range(size)])]
    unnamed x95 -> x127, local copies, waits for them, and re-layouts: 7.88 us -> 10.8 us
    pallas_call x9 -> x11, Pallas kernels: 41 us -> 43.5 us  [call(): pl.pallas_call(body, name=name, out_shape=[jax.ShapeDtypeStruct(shape, dt...]
  transfers between devices with their start and end apart: 62 -> 63, of which waited for: 22 -> 26; matrix products, arithmetic and copies ran while one was open for 5% -> 6% of each run, Pallas kernels for 9% -> 19%
where the time goes in v2:
time: 173 us; the launch traced here: 172 us
  starting transfers between devices  59.3 us (34%)
  waiting for transfers between devices  46.5 us (27%)
  Pallas kernels  43.5 us (25%)
  local copies, waits for them, and re-layouts  15.3 us (9%)
  other arithmetic  6.02 us (3%)
    ppermute x63, starting transfers between devices, swap(): return lax.ppermute(value, axis, [(i, i ^ bits) for i in range(size)])  59.3 us
    ppermute x63, waiting for transfers between devices, swap(): return lax.ppermute(value, axis, [(i, i ^ bits) for i in range(size)])  46.5 us
    pallas_call x11, Pallas kernels, call(): pl.pallas_call(body, name=name, out_shape=[jax.ShapeDtypeStruct(shape, dt...  43.5 us
    unnamed x127, local copies, waits for them, and re-layouts  10.8 us
  transfers between devices with their start and end apart: 63, of which 26 were waited for; matrix products, arithmetic and copies ran while one was open for 6% of the time, Pallas kernels for 19%

profile of v2, /device:TPU:0, one launch (start us, length us, event | category | flops | bytes accessed | tf_op | source)
XLA Modules:
  0.0 172.3 jit_solution(4432975450636845918)
XLA Ops:
  1.6 3.1 %collective-permute-start.1 = (f32[12,768]{1,0:T(8,128)S(1)}, f32[12,768]{1,0:T(8,128)S(1)}, u32[]{:S(2)}, u32[]{:S(2)}) collective-permute-start(f32[12,768]{1,0:T(8,128)S(1)} %dynamic_update_slice.5), channel_id=1, source_target_pairs={{0,1},{1,0},{2,3},{3,2},{4,5},{5,4},{6,7},{7,6},{8,9},{9,8},{10,11... | collective-permute-start | bytes 110600 | tf_op jit(solution)/shard_map/ppermute | solution.py:26
  4.8 0.9 copy.19
  5.6 1.1 copy.18
  7.0 2.7 %collective-permute-start = (bf16[1,96,768]{2,1,0:T(8,128)(2,1)S(1)}, bf16[1,96,768]{2,1,0:T(8,128)(2,1)S(1)}, u32[]{:S(2)}, u32[]{:S(2)}) collective-permute-start(bf16[1,96,768]{2,1,0:T(8,128)(2,1)S(1)} %maximum_bitcast_fusion.refs_5_), channel_id=1, source_target_pairs={{0,2},{1,3},{2,0},{3,1},{4,6},{5,7},{6,4},{7,5},{8,10},{9,11},{10,... | collective-permute-start | bytes 442376 | tf_op jit(solution)/shard_map/ppermute | solution.py:26
  10.6 1.6 collective-permute-start.2
  12.2 2.2 %norm_first.1 = (bf16[128,768]{1,0:T(8,128)(2,1)}, bf16[128,768]{1,0:T(8,128)(2,1)}, f32[1,768]{1,0:T(1,128)}) custom-call(f32[128,768]{1,0:T(8,128)} %x_ref.5, f32[128,768]{1,0:T(8,128)} %grad_ref.1), custom_call_target="tpu_custom_call" | custom-call | flops 100000000 | bytes 200000 | tf_op jit(solution)/shard_map/norm_first/pallas_call | solution.py:69
  14.8 1.5 collective-permute-done.refs_13_
  16.3 1.5 collective-permute-start.3
  17.8 1.4 collective-permute-start.4
  19.2 3.1 %collective-permute-start.11 = (bf16[1,96,1536]{2,1,0:T(8,128)(2,1)S(1)}, bf16[1,96,1536]{2,1,0:T(8,128)(2,1)S(1)}, u32[]{:S(2)}, u32[]{:S(2)}) collective-permute-start(bf16[1,96,1536]{2,1,0:T(8,128)(2,1)S(1)} %bitcast.40), channel_id=1, source_target_pairs={{0,2},{1,3},{2,0},{3,1},{4,6},{5,7},{6,4},{7,5},{8,10},{9,11},{10,... | collective-permute-start | bytes 884744 | tf_op jit(solution)/shard_map/ppermute | solution.py:26
  23.0 3.5 %collective-permute-done.5 = f32[12,768]{1,0:T(8,128)S(1)} collective-permute-done((f32[12,768]{1,0:T(8,128)S(1)}, f32[12,768]{1,0:T(8,128)S(1)}, u32[]{:S(2)}, u32[]{:S(2)}) %collective-permute-start.5) | collective-permute-done | bytes 36896 | tf_op jit(solution)/shard_map/ppermute | solution.py:26
  26.6 1.3 collective-permute-start.12
  27.9 1.2 collective-permute-start.7
  29.9 1.5 collective-permute-start.9
  31.4 1.2 collective-permute-done.12
  33.2 3.2 %collective-permute-done.11.refs_14_ = bf16[1,96,1536]{2,1,0:T(8,128)(2,1)S(1)} collective-permute-done((bf16[1,96,1536]{2,1,0:T(8,128)(2,1)S(1)}, bf16[1,96,1536]{2,1,0:T(8,128)(2,1)S(1)}, u32[]{:S(2)}, u32[]{:S(2)}) %collective-permute-start.11) | collective-permute-done | bytes 294944 | tf_op jit(solution)/shard_map/ppermute | solution.py:26
  36.5 1.2 collective-permute-done.10.refs_16_
  40.3 0.9 collective-permute-start.22
  41.1 1.7 collective-permute-start.23
  45.8 6.1 %attend.1 = (bf16[768,768]{1,0:T(8,128)(2,1)}, bf16[768,768]{1,0:T(8,128)(2,1)}, bf16[256,576]{1,0:T(8,128)(2,1)}, bf16[256,576]{1,0:T(8,128)(2,1)}, bf16[256,19...) custom-call(s32[3]{0:T(128)} %pad_add_fusion.refs_0_, ...), custom_call_target="tpu_custom_call" | custom-call | flops 300000000 | bytes 600000 | tf_op jit(solution)/shard_map/attend/pallas_call | solution.py:69
  51.9 3.6 %collective-permute-start.24 = (bf16[128,768]{1,0:T(8,128)(2,1)}, bf16[128,768]{1,0:T(8,128)(2,1)S(1)}, u32[]{:S(2)}, u32[]{:S(2)}) collective-permute-start(bf16[128,768]{1,0:T(8,128)(2,1)} %get-tuple-element.147), channel_id=1, source_target_pairs={{0,1},{1,0},{2,3},{3,2},{4,5},{5,4},{6,7},{7,6},{8,9},{9,8},{10,11... | collective-permute-start | bytes 589832 | tf_op jit(solution)/shard_map/ppermute | solution.py:26
  55.5 1.6 collective-permute-start.25
  57.6 1.5 collective-permute-start.27
  59.1 2.2 %collective-permute-done.24.recv_ref = bf16[128,768]{1,0:T(8,128)(2,1)S(1)} collective-permute-done((bf16[128,768]{1,0:T(8,128)(2,1)}, bf16[128,768]{1,0:T(8,128)(2,1)S(1)}, u32[]{:S(2)}, u32[]{:S(2)}) %collective-permute-start.24) | collective-permute-done | bytes 196640 | tf_op jit(solution)/shard_map/ppermute | solution.py:26
  61.3 1.5 collective-permute-start.28
  62.9 2.1 %norm_second.1 = (f32[128,768]{1,0:T(8,128)}, bf16[128,768]{1,0:T(8,128)(2,1)}) custom-call(f32[128,768]{1,0:T(8,128)} %x_ref.5, f32[128,768]{1,0:T(8,128)} %get-tuple-element.143.keep_ref, bf16[128,768]{1,0:T(8,128)(2,1)} %copy-done.39, f32[12,768]{1,0:T(8,128)} %copy-done.8), custom_call_target="tpu_custom_call" | custom-call | flops 100000000 | bytes 200000 | tf_op jit(solution)/shard_map/norm_second/pallas_call | solution.py:69
  65.3 1.9 %collective-permute-start.29 = (bf16[128,768]{1,0:T(8,128)(2,1)}, bf16[128,768]{1,0:T(8,128)(2,1)S(1)}, u32[]{:S(2)}, u32[]{:S(2)}) collective-permute-start(bf16[128,768]{1,0:T(8,128)(2,1)} %get-tuple-element.149.refs_1_), channel_id=1, source_target_pairs={{0,1},{1,0},{2,3},{3,2},{4,5},{5,4},{6,7},{7,6},{8,9},{9,8},{10,11... | collective-permute-start | bytes 589832 | tf_op jit(solution)/shard_map/ppermute | solution.py:26
  67.1 3.7 %collective-permute-done.26.refs_9_ = bf16[1,96,1536]{2,1,0:T(8,128)(2,1)S(1)} collective-permute-done((bf16[1,96,1536]{2,1,0:T(8,128)(2,1)S(1)}, bf16[1,96,1536]{2,1,0:T(8,128)(2,1)S(1)}, u32[]{:S(2)}, u32[]{:S(2)}) %collective-permute-start.26) | collective-permute-done | bytes 294944 | tf_op jit(solution)/shard_map/ppermute | solution.py:26
  70.8 1.5 collective-permute-done.28.refs_17_
  78.1 7.4 %feed.1 = (bf16[256,768]{1,0:T(8,128)(2,1)}, bf16[256,768]{1,0:T(8,128)(2,1)}, bf16[256,768]{1,0:T(8,128)(2,1)}, bf16[256,768]{1,0:T(8,128)(2,1)}, bf16[256,768]...) custom-call(s32[3]{0:T(128)} %pad_add_fusion.refs_0_, ...), custom_call_target="tpu_custom_call" | custom-call | flops 350000000 | bytes 700000 | tf_op jit(solution)/shard_map/feed/pallas_call | solution.py:69
  85.5 3.7 %feed_grad_1.1 = (bf16[4,96,1536]{2,1,0:T(8,128)(2,1)}, bf16[4,96,1536]{2,1,0:T(8,128)(2,1)}) custom-call(s32[3]{0:T(128)} %pad_add_fusion.refs_0_, bf16[256,768]{1,0:T(8,128)(2,1)} %get-tuple-element.168.refs_1_, bf16[256,768]{1,0:T(8,128)(2,1)} %get-tuple-element.169.refs_2_, bf16[256,768]{1,0:T(8,128)(2,1)} %get-tuple-element.174.refs_3_, ...), custom_call_target="tpu_custom_call" | custom-call | flops 150000000 | bytes 300000 | tf_op jit(solution)/shard_map/feed_grad_1/pallas_call | solution.py:69
  89.6 1.6 collective-permute-start.39
  91.2 3.7 %feed_grad_0.1 = (bf16[4,96,1536]{2,1,0:T(8,128)(2,1)}, bf16[4,96,1536]{2,1,0:T(8,128)(2,1)}) custom-call(s32[3]{0:T(128)} %pad_add_fusion.refs_0_, bf16[256,768]{1,0:T(8,128)(2,1)} %get-tuple-element.168.refs_1_, bf16[256,768]{1,0:T(8,128)(2,1)} %get-tuple-element.169.refs_2_, bf16[256,768]{1,0:T(8,128)(2,1)} %get-tuple-element.170.refs_3_, ...), custom_call_target="tpu_custom_call" | custom-call | flops 150000000 | bytes 300000 | tf_op jit(solution)/shard_map/feed_grad_0/pallas_call | solution.py:69
  95.3 1.3 copy-done
  97.4 0.9 collective-permute-start.41
  98.3 1.5 collective-permute-start.45
  99.8 2.6 %norm_second_back.1 = (f32[128,768]{1,0:T(8,128)}, bf16[128,768]{1,0:T(8,128)(2,1)}, f32[3,768]{1,0:T(4,128)}) custom-call(f32[128,768]{1,0:T(8,128)} %get-tuple-element.148.resid_ref, f32[128,768]{1,0:T(8,128)} %get-tuple-element.166.keep_ref, bf16[128,768]{1,0:T(8,128)(2,1)} %copy-done.38, f32[128,768]{1,0:T(8,128)} %grad_ref.1, f32[12,768]{1,0:T(8,128)} %copy-done.8), custom_call_target="tpu_custom_call" | custom-call | flops 100000000 | bytes 200000 | tf_op jit(solution)/shard_map/norm_second_back/pallas_call | solution.py:69
  102.9 1.4 copy-done.1
  105.5 1.6 collective-permute-start.44
  107.1 4.2 %collective-permute-done.43.refs_2_ = bf16[128,768]{1,0:T(8,128)(2,1)S(1)} collective-permute-done((bf16[128,768]{1,0:T(8,128)(2,1)S(1)}, bf16[128,768]{1,0:T(8,128)(2,1)S(1)}, u32[]{:S(2)}, u32[]{:S(2)}) %collective-permute-start.43) | collective-permute-done | bytes 196640 | tf_op jit(solution)/shard_map/ppermute | solution.py:26
  111.9 5.7 %attend_back_1.1 = (bf16[4,96,768]{2,1,0:T(8,128)(2,1)}, bf16[4,96,768]{2,1,0:T(8,128)(2,1)}, f32[1,576]{1,0:T(1,128)}, f32[256,768]{1,0:T(8,128)}) custom-call(s32[3]{0:T(128)} %pad_add_fusion.refs_0_, bf16[128,768]{1,0:T(8,128)(2,1)} %get-tuple-element.184.refs_1_, bf16[128,768]{1,0:T(8,128)(2,1)} %copy-done.14, ...), custom_call_target="tpu_custom_call" | custom-call | flops 300000000 | bytes 600000 | tf_op jit(solution)/shard_map/attend_back_1/pallas_call | solution.py:69
  117.9 2.4 %collective-permute-done.44 = bf16[2,96,1536]{2,1,0:T(8,128)(2,1)S(1)} collective-permute-done((bf16[2,96,1536]{2,1,0:T(8,128)(2,1)S(1)}, bf16[2,96,1536]{2,1,0:T(8,128)(2,1)S(1)}, u32[]{:S(2)}, u32[]{:S(2)}) %collective-permute-start.44) | collective-permute-done | bytes 589856 | tf_op jit(solution)/shard_map/ppermute | solution.py:26
  120.5 1.4 collective-permute-start.48
  121.9 1.4 collective-permute-start.49
  124.3 6.0 %attend_back_0.1 = (bf16[4,96,768]{2,1,0:T(8,128)(2,1)}, bf16[4,96,768]{2,1,0:T(8,128)(2,1)}, f32[1,576]{1,0:T(1,128)}, f32[128,768]{1,0:T(8,128)}, bf16[128,768]{1,0:T(8,128)(2,1)}, /*index=5*/f32[2,768]{1,0:T(2,128)}) custom-call(s32[3]{0:T(128)} %pad_add_fusion.refs_0_, bf16[128,768]{1,0:T(8,128)(2,1)} %get-tuple-element.184.refs_1_, ...), custom_call_target="tpu_custom_call" | custom-call | flops 300000000 | bytes 600000 | tf_op jit(solution)/shard_map/attend_back_0/pallas_call | solution.py:69
  130.6 0.9 slice-done.3
  131.5 4.0 %collective-permute-done.47 = bf16[2,96,768]{2,1,0:T(8,128)(2,1)S(1)} collective-permute-done((bf16[2,96,768]{2,1,0:T(8,128)(2,1)S(1)}, bf16[2,96,768]{2,1,0:T(8,128)(2,1)S(1)}, u32[]{:S(2)}, u32[]{:S(2)}) %collective-permute-start.47) | collective-permute-done | bytes 294944 | tf_op jit(solution)/shard_map/ppermute | solution.py:26
  135.6 1.6 sums.1
  137.2 1.6 collective-permute-start.56
  138.8 0.8 collective-permute-start.50
  139.6 0.8 add.135
  141.7 0.8 add_add_fusion
  142.5 1.2 collective-permute-start.51
  143.8 1.1 collective-permute-start.54
  144.9 5.9 %collective-permute-done.54 = f32[12,768]{1,0:T(8,128)S(1)} collective-permute-done((f32[12,768]{1,0:T(8,128)S(1)}, f32[12,768]{1,0:T(8,128)S(1)}, u32[]{:S(2)}, u32[]{:S(2)}) %collective-permute-start.54) | collective-permute-done | bytes 36896 | tf_op jit(solution)/shard_map/ppermute | solution.py:26
  150.9 4.4 %collective-permute-done.51.recv_ref = bf16[128,768]{1,0:T(8,128)(2,1)S(1)} collective-permute-done((bf16[128,768]{1,0:T(8,128)(2,1)S(1)}, bf16[128,768]{1,0:T(8,128)(2,1)S(1)}, u32[]{:S(2)}, u32[]{:S(2)}) %collective-permute-start.51) | collective-permute-done | bytes 196640 | tf_op jit(solution)/shard_map/ppermute | solution.py:26
  155.4 1.5 collective-permute-start.59
  158.0 2.0 %collective-permute-done.59 = f32[12,768]{1,0:T(8,128)S(1)} collective-permute-done((f32[12,768]{1,0:T(8,128)S(1)}, f32[12,768]{1,0:T(8,128)S(1)}, u32[]{:S(2)}, u32[]{:S(2)}) %collective-permute-start.59) | collective-permute-done | bytes 36896 | tf_op jit(solution)/shard_map/ppermute | solution.py:26
  160.0 2.4 %collective-permute-start.62 = (f32[12,768]{1,0:T(8,128)S(1)}, f32[12,768]{1,0:T(8,128)S(1)}, u32[]{:S(2)}, u32[]{:S(2)}) collective-permute-start(f32[12,768]{1,0:T(8,128)S(1)} %add.142), channel_id=1, source_target_pairs={{0,3},{1,2},{2,1},{3,0},{4,7},{5,6},{6,5},{7,4},{8,11},{9,10},{10,... | collective-permute-start | bytes 110600 | tf_op jit(solution)/shard_map/ppermute | solution.py:26
  162.4 2.0 %collective-permute-start.60 = (f32[12,768]{1,0:T(8,128)S(1)}, f32[12,768]{1,0:T(8,128)S(1)}, u32[]{:S(2)}, u32[]{:S(2)}) collective-permute-start(f32[12,768]{1,0:T(8,128)S(1)} %add.142), channel_id=1, source_target_pairs={{0,1},{1,0},{2,3},{3,2},{4,5},{5,4},{6,7},{7,6},{8,9},{9,8},{10,11... | collective-permute-start | bytes 110600 | tf_op jit(solution)/shard_map/ppermute | solution.py:26
  164.5 0.8 slice_bitcast_fusion
  165.3 2.4 %norm_first_back.1 = f32[128,768]{1,0:T(8,128)} custom-call(f32[128,768]{1,0:T(8,128)} %x_ref.5, f32[128,768]{1,0:T(8,128)} %get-tuple-element.202.keep_ref, bf16[128,768]{1,0:T(8,128)(2,1)} %copy-done.37, f32[128,768]{1,0:T(8,128)} %get-tuple-element.223.grad1_ref, f32[12,768]{1,0:T(8,128)} %copy-done.8), custom_call_target="tpu_custom_call" | custom-call | flops 100000000 | bytes 200000 | tf_op jit(solution)/shard_map/norm_first_back/pallas_call | solution.py:69
  167.7 1.9 %collective-permute-done.61 = f32[12,768]{1,0:T(8,128)S(1)} collective-permute-done((f32[12,768]{1,0:T(8,128)S(1)}, f32[12,768]{1,0:T(8,128)S(1)}, u32[]{:S(2)}, u32[]{:S(2)}) %collective-permute-start.61) | collective-permute-done | bytes 36896 | tf_op jit(solution)/shard_map/ppermute | solution.py:26
  171.4 0.9 copy.22
  (268 shorter events, 26.1 us)
Async XLA Ops:
  1.6 8.0 %collective-permute-start.1 = (f32[12,768]{1,0:T(8,128)S(1)}, f32[12,768]{1,0:T(8,128)S(1)}, u32[]{:S(2)}, u32[]{:S(2)}) collective-permute-start(f32[12,768]{1,0:T(8,128)S(1)} %dynamic_update_slice.5), channel_id=1, source_target_pairs={{0,1},{1,0},{2,3},{3,2},{4,5},{5,4},{6,7},{7,6},{8,9},{9,8},{10,11... | collective-permute-start | bytes 110600 | tf_op jit(solution)/shard_map/ppermute | solution.py:26
  7.0 9.3 %collective-permute-start = (bf16[1,96,768]{2,1,0:T(8,128)(2,1)S(1)}, bf16[1,96,768]{2,1,0:T(8,128)(2,1)S(1)}, u32[]{:S(2)}, u32[]{:S(2)}) collective-permute-start(bf16[1,96,768]{2,1,0:T(8,128)(2,1)S(1)} %maximum_bitcast_fusion.refs_5_), channel_id=1, source_target_pairs={{0,2},{1,3},{2,0},{3,1},{4,6},{5,7},{6,4},{7,5},{8,10},{9,11},{10,... | collective-permute-start | bytes 442376 | tf_op jit(solution)/shard_map/ppermute | solution.py:26
  10.6 4.2 %collective-permute-start.2 = (f32[12,768]{1,0:T(8,128)S(1)}, f32[12,768]{1,0:T(8,128)S(1)}, u32[]{:S(2)}, u32[]{:S(2)}) collective-permute-start(f32[12,768]{1,0:T(8,128)S(1)} %add.114), channel_id=1, source_target_pairs={{0,8},{4,12},{8,0},{12,4},{16,24},{20,28},{24,16},{28,20},{1,9},{5... | collective-permute-start | bytes 110600 | tf_op jit(solution)/shard_map/ppermute | solution.py:26
  12.2 60.1 %copy-start.9 = (bf16[96,1536]{1,0:T(8,128)(2,1)}, bf16[96,1536]{1,0:T(8,128)(2,1)S(1)}, u32[]{:S(2)}) copy-start(bf16[96,1536]{1,0:T(8,128)(2,1)S(1)} %pad_maximum_fusion) | copy-start | bytes 884740
  16.3 10.3 %collective-permute-start.6 = (bf16[128,768]{1,0:T(8,128)(2,1)}, bf16[128,768]{1,0:T(8,128)(2,1)S(1)}, u32[]{:S(2)}, u32[]{:S(2)}) collective-permute-start(bf16[128,768]{1,0:T(8,128)(2,1)} %get-tuple-element.123.refs_1_.refs_9_), channel_id=1, source_target_pairs={{0,1},{1,0},{2,3},{3,2},{4,5},{5,4},{6,7},{7,6},{8,9},{9,8},{10,11... | collective-permute-start | bytes 589832 | tf_op jit(solution)/shard_map/ppermute | solution.py:26
  16.3 10.2 %collective-permute-start.3 = (bf16[1,96,768]{2,1,0:T(8,128)(2,1)S(1)}, bf16[1,96,768]{2,1,0:T(8,128)(2,1)S(1)}, u32[]{:S(2)}, u32[]{:S(2)}) collective-permute-start(bf16[1,96,768]{2,1,0:T(8,128)(2,1)S(1)} %maximum_bitcast_fusion.refs_5_), channel_id=1, source_target_pairs={{0,8},{4,12},{8,0},{12,4},{16,24},{20,28},{24,16},{28,20},{1,9},{5... | collective-permute-start | bytes 442376 | tf_op jit(solution)/shard_map/ppermute | solution.py:26
  17.8 8.7 %collective-permute-start.4 = (bf16[1,96,768]{2,1,0:T(8,128)(2,1)S(1)}, bf16[1,96,768]{2,1,0:T(8,128)(2,1)S(1)}, u32[]{:S(2)}, u32[]{:S(2)}) collective-permute-start(bf16[1,96,768]{2,1,0:T(8,128)(2,1)S(1)} %collective-permute-done.refs_13_), channel_id=1, source_target_pairs={{0,16},{4,20},{8,24},{12,28},{16,0},{20,4},{24,8},{28,12},{1,17},{... | collective-permute-start | bytes 442376 | tf_op jit(solution)/shard_map/ppermute | solution.py:26
  19.2 17.2 %collective-permute-start.11 = (bf16[1,96,1536]{2,1,0:T(8,128)(2,1)S(1)}, bf16[1,96,1536]{2,1,0:T(8,128)(2,1)S(1)}, u32[]{:S(2)}, u32[]{:S(2)}) collective-permute-start(bf16[1,96,1536]{2,1,0:T(8,128)(2,1)S(1)} %bitcast.40), channel_id=1, source_target_pairs={{0,2},{1,3},{2,0},{3,1},{4,6},{5,7},{6,4},{7,5},{8,10},{9,11},{10,... | collective-permute-start | bytes 884744 | tf_op jit(solution)/shard_map/ppermute | solution.py:26
  22.4 4.1 %collective-permute-start.5 = (f32[12,768]{1,0:T(8,128)S(1)}, f32[12,768]{1,0:T(8,128)S(1)}, u32[]{:S(2)}, u32[]{:S(2)}) collective-permute-start(f32[12,768]{1,0:T(8,128)S(1)} %add.115), channel_id=1, source_target_pairs={{0,16},{4,20},{8,24},{12,28},{16,0},{20,4},{24,8},{28,12},{1,17},{... | collective-permute-start | bytes 110600 | tf_op jit(solution)/shard_map/ppermute | solution.py:26
  26.6 6.1 %collective-permute-start.12 = (f32[12,768]{1,0:T(8,128)S(1)}, f32[12,768]{1,0:T(8,128)S(1)}, u32[]{:S(2)}, u32[]{:S(2)}) collective-permute-start(f32[12,768]{1,0:T(8,128)S(1)} %add.116), channel_id=1, source_target_pairs={{0,3},{1,2},{2,1},{3,0},{4,7},{5,6},{6,5},{7,4},{8,11},{9,10},{10,... | collective-permute-start | bytes 110600 | tf_op jit(solution)/shard_map/ppermute | solution.py:26
  27.9 8.6 %collective-permute-start.7 = (bf16[1,96,768]{2,1,0:T(8,128)(2,1)S(1)}, bf16[1,96,768]{2,1,0:T(8,128)(2,1)S(1)}, u32[]{:S(2)}, u32[]{:S(2)}) collective-permute-start(bf16[1,96,768]{2,1,0:T(8,128)(2,1)S(1)} %maximum_bitcast_fusion.refs_5_), channel_id=1, source_target_pairs={{0,16},{4,20},{8,24},{12,28},{16,0},{20,4},{24,8},{28,12},{1,17},{... | collective-permute-start | bytes 442376 | tf_op jit(solution)/shard_map/ppermute | solution.py:26
  29.1 7.4 %collective-permute-start.8 = (bf16[1,96,768]{2,1,0:T(8,128)(2,1)S(1)}, bf16[1,96,768]{2,1,0:T(8,128)(2,1)S(1)}, u32[]{:S(2)}, u32[]{:S(2)}) collective-permute-start(bf16[1,96,768]{2,1,0:T(8,128)(2,1)S(1)} %collective-permute-done.3.refs_6_), channel_id=1, source_target_pairs={{0,16},{4,20},{8,24},{12,28},{16,0},{20,4},{24,8},{28,12},{1,17},{... | collective-permute-start | bytes 442376 | tf_op jit(solution)/shard_map/ppermute | solution.py:26
  29.9 6.6 %collective-permute-start.9 = (bf16[1,96,768]{2,1,0:T(8,128)(2,1)S(1)}, bf16[1,96,768]{2,1,0:T(8,128)(2,1)S(1)}, u32[]{:S(2)}, u32[]{:S(2)}) collective-permute-start(bf16[1,96,768]{2,1,0:T(8,128)(2,1)S(1)} %collective-permute-done.refs_13_), channel_id=1, source_target_pairs={{0,8},{4,12},{8,0},{12,4},{16,24},{20,28},{24,16},{28,20},{1,9},{5... | collective-permute-start | bytes 442376 | tf_op jit(solution)/shard_map/ppermute | solution.py:26
  32.6 5.1 %collective-permute-start.10 = (bf16[1,96,768]{2,1,0:T(8,128)(2,1)S(1)}, bf16[1,96,768]{2,1,0:T(8,128)(2,1)S(1)}, u32[]{:S(2)}, u32[]{:S(2)}) collective-permute-start(bf16[1,96,768]{2,1,0:T(8,128)(2,1)S(1)} %collective-permute-done.4.refs_14_), channel_id=1, source_target_pairs={{0,8},{4,12},{8,0},{12,4},{16,24},{20,28},{24,16},{28,20},{1,9},{5... | collective-permute-start | bytes 442376 | tf_op jit(solution)/shard_map/ppermute | solution.py:26
  37.8 1.8 %collective-permute-start.13 = (f32[12,768]{1,0:T(8,128)S(1)}, f32[12,768]{1,0:T(8,128)S(1)}, u32[]{:S(2)}, u32[]{:S(2)}) collective-permute-start(f32[12,768]{1,0:T(8,128)S(1)} %add.117), channel_id=1, source_target_pairs={{0,4},{4,0},{8,12},{12,8},{16,20},{20,16},{24,28},{28,24},{1,5},{5... | collective-permute-start | bytes 110600 | tf_op jit(solution)/shard_map/ppermute | solution.py:26
  37.8 2.5 %collective-permute-start.14 = (bf16[1,96,768]{2,1,0:T(8,128)(2,1)S(1)}, bf16[1,96,768]{2,1,0:T(8,128)(2,1)S(1)}, u32[]{:S(2)}, u32[]{:S(2)}) collective-permute-start(bf16[1,96,768]{2,1,0:T(8,128)(2,1)S(1)} %maximum_bitcast_fusion.refs_5_), channel_id=1, source_target_pairs={{0,4},{4,0},{8,12},{12,8},{16,20},{20,16},{24,28},{28,24},{1,5},{5... | collective-permute-start | bytes 442376 | tf_op jit(solution)/shard_map/ppermute | solution.py:26
  38.3 2.9 %collective-permute-start.15 = (bf16[1,96,768]{2,1,0:T(8,128)(2,1)S(1)}, bf16[1,96,768]{2,1,0:T(8,128)(2,1)S(1)}, u32[]{:S(2)}, u32[]{:S(2)}) collective-permute-start(bf16[1,96,768]{2,1,0:T(8,128)(2,1)S(1)} %collective-permute-done.3.refs_6_), channel_id=1, source_target_pairs={{0,4},{4,0},{8,12},{12,8},{16,20},{20,16},{24,28},{28,24},{1,5},{5... | collective-permute-start | bytes 442376 | tf_op jit(solution)/shard_map/ppermute | solution.py:26
  39.0 3.8 %collective-permute-start.16 = (bf16[1,96,768]{2,1,0:T(8,128)(2,1)S(1)}, bf16[1,96,768]{2,1,0:T(8,128)(2,1)S(1)}, u32[]{:S(2)}, u32[]{:S(2)}) collective-permute-start(bf16[1,96,768]{2,1,0:T(8,128)(2,1)S(1)} %collective-permute-done.7.refs_7_), channel_id=1, source_target_pairs={{0,4},{4,0},{8,12},{12,8},{16,20},{20,16},{24,28},{28,24},{1,5},{5... | collective-permute-start | bytes 442376 | tf_op jit(solution)/shard_map/ppermute | solution.py:26
  39.5 3.4 %collective-permute-start.17 = (bf16[1,96,768]{2,1,0:T(8,128)(2,1)S(1)}, bf16[1,96,768]{2,1,0:T(8,128)(2,1)S(1)}, u32[]{:S(2)}, u32[]{:S(2)}) collective-permute-start(bf16[1,96,768]{2,1,0:T(8,128)(2,1)S(1)} %collective-permute-done.8.refs_8_), channel_id=1, source_target_pairs={{0,4},{4,0},{8,12},{12,8},{16,20},{20,16},{24,28},{28,24},{1,5},{5... | collective-permute-start | bytes 442376 | tf_op jit(solution)/shard_map/ppermute | solution.py:26
  39.6 3.8 %collective-permute-start.18 = (bf16[1,96,768]{2,1,0:T(8,128)(2,1)S(1)}, bf16[1,96,768]{2,1,0:T(8,128)(2,1)S(1)}, u32[]{:S(2)}, u32[]{:S(2)}) collective-permute-start(bf16[1,96,768]{2,1,0:T(8,128)(2,1)S(1)} %collective-permute-done.refs_13_), channel_id=1, source_target_pairs={{0,4},{4,0},{8,12},{12,8},{16,20},{20,16},{24,28},{28,24},{1,5},{5... | collective-permute-start | bytes 442376 | tf_op jit(solution)/shard_map/ppermute | solution.py:26
  40.3 11.6 %collective-permute-start.22 = (bf16[1,96,1536]{2,1,0:T(8,128)(2,1)S(1)}, bf16[1,96,1536]{2,1,0:T(8,128)(2,1)S(1)}, u32[]{:S(2)}, u32[]{:S(2)}) collective-permute-start(bf16[1,96,1536]{2,1,0:T(8,128)(2,1)S(1)} %bitcast.41), channel_id=1, source_target_pairs={{0,8},{4,12},{8,0},{12,4},{16,24},{20,28},{24,16},{28,20},{1,9},{5... | collective-permute-start | bytes 884744 | tf_op jit(solution)/shard_map/ppermute | solution.py:26
  41.1 10.8 %collective-permute-start.23 = (bf16[1,96,1536]{2,1,0:T(8,128)(2,1)S(1)}, bf16[1,96,1536]{2,1,0:T(8,128)(2,1)S(1)}, u32[]{:S(2)}, u32[]{:S(2)}) collective-permute-start(bf16[1,96,1536]{2,1,0:T(8,128)(2,1)S(1)} %collective-permute-done.11.refs_14_), channel_id=1, source_target_pairs={{0,16},{4,20},{8,24},{12,28},{16,0},{20,4},{24,8},{28,12},{1,17},{... | collective-permute-start | bytes 884744 | tf_op jit(solution)/shard_map/ppermute | solution.py:26
  42.8 1.4 collective-permute-start.19
  42.9 1.5 collective-permute-start.20
  43.4 1.4 collective-permute-start.21
  51.9 9.4 %collective-permute-start.24 = (bf16[128,768]{1,0:T(8,128)(2,1)}, bf16[128,768]{1,0:T(8,128)(2,1)S(1)}, u32[]{:S(2)}, u32[]{:S(2)}) collective-permute-start(bf16[128,768]{1,0:T(8,128)(2,1)} %get-tuple-element.147), channel_id=1, source_target_pairs={{0,1},{1,0},{2,3},{3,2},{4,5},{5,4},{6,7},{7,6},{8,9},{9,8},{10,11... | collective-permute-start | bytes 589832 | tf_op jit(solution)/shard_map/ppermute | solution.py:26
  55.5 9.8 %collective-permute-start.30 = (bf16[128,768]{1,0:T(8,128)(2,1)S(1)}, bf16[128,768]{1,0:T(8,128)(2,1)S(1)}, u32[]{:S(2)}, u32[]{:S(2)}) collective-permute-start(bf16[128,768]{1,0:T(8,128)(2,1)S(1)} %copy-done.34), channel_id=1, source_target_pairs={{0,1},{1,0},{2,3},{3,2},{4,5},{5,4},{6,7},{7,6},{8,9},{9,8},{10,11... | collective-permute-start | bytes 589832 | tf_op jit(solution)/shard_map/ppermute | solution.py:26
  55.5 11.6 %collective-permute-start.25 = (bf16[1,96,1536]{2,1,0:T(8,128)(2,1)S(1)}, bf16[1,96,1536]{2,1,0:T(8,128)(2,1)S(1)}, u32[]{:S(2)}, u32[]{:S(2)}) collective-permute-start(bf16[1,96,1536]{2,1,0:T(8,128)(2,1)S(1)} %bitcast.42), channel_id=1, source_target_pairs={{0,16},{4,20},{8,24},{12,28},{16,0},{20,4},{24,8},{28,12},{1,17},{... | collective-permute-start | bytes 884744 | tf_op jit(solution)/shard_map/ppermute | solution.py:26
  57.1 13.7 %collective-permute-start.26 = (bf16[1,96,1536]{2,1,0:T(8,128)(2,1)S(1)}, bf16[1,96,1536]{2,1,0:T(8,128)(2,1)S(1)}, u32[]{:S(2)}, u32[]{:S(2)}) collective-permute-start(bf16[1,96,1536]{2,1,0:T(8,128)(2,1)S(1)} %collective-permute-done.22.refs_7_), channel_id=1, source_target_pairs={{0,16},{4,20},{8,24},{12,28},{16,0},{20,4},{24,8},{28,12},{1,17},{... | collective-permute-start | bytes 884744 | tf_op jit(solution)/shard_map/ppermute | solution.py:26
  57.6 13.3 %collective-permute-start.27 = (bf16[1,96,1536]{2,1,0:T(8,128)(2,1)S(1)}, bf16[1,96,1536]{2,1,0:T(8,128)(2,1)S(1)}, u32[]{:S(2)}, u32[]{:S(2)}) collective-permute-start(bf16[1,96,1536]{2,1,0:T(8,128)(2,1)S(1)} %collective-permute-done.11.refs_14_), channel_id=1, source_target_pairs={{0,8},{4,12},{8,0},{12,4},{16,24},{20,28},{24,16},{28,20},{1,9},{5... | collective-permute-start | bytes 884744 | tf_op jit(solution)/shard_map/ppermute | solution.py:26
  61.3 11.0 %collective-permute-start.28 = (bf16[1,96,1536]{2,1,0:T(8,128)(2,1)S(1)}, bf16[1,96,1536]{2,1,0:T(8,128)(2,1)S(1)}, u32[]{:S(2)}, u32[]{:S(2)}) collective-permute-start(bf16[1,96,1536]{2,1,0:T(8,128)(2,1)S(1)} %collective-permute-done.23.refs_15_), channel_id=1, source_target_pairs={{0,8},{4,12},{8,0},{12,4},{16,24},{20,28},{24,16},{28,20},{1,9},{5... | collective-permute-start | bytes 884744 | tf_op jit(solution)/shard_map/ppermute | solution.py:26
  65.3 7.1 %collective-permute-start.29 = (bf16[128,768]{1,0:T(8,128)(2,1)}, bf16[128,768]{1,0:T(8,128)(2,1)S(1)}, u32[]{:S(2)}, u32[]{:S(2)}) collective-permute-start(bf16[128,768]{1,0:T(8,128)(2,1)} %get-tuple-element.149.refs_1_), channel_id=1, source_target_pairs={{0,1},{1,0},{2,3},{3,2},{4,5},{5,4},{6,7},{7,6},{8,9},{9,8},{10,11... | collective-permute-start | bytes 589832 | tf_op jit(solution)/shard_map/ppermute | solution.py:26
  72.3 1.6 collective-permute-start.31
  72.4 2.0 %collective-permute-start.32 = (bf16[1,96,1536]{2,1,0:T(8,128)(2,1)S(1)}, bf16[1,96,1536]{2,1,0:T(8,128)(2,1)S(1)}, u32[]{:S(2)}, u32[]{:S(2)}) collective-permute-start(bf16[1,96,1536]{2,1,0:T(8,128)(2,1)S(1)} %collective-permute-done.22.refs_7_), channel_id=1, source_target_pairs={{0,4},{4,0},{8,12},{12,8},{16,20},{20,16},{24,28},{28,24},{1,5},{5... | collective-permute-start | bytes 884744 | tf_op jit(solution)/shard_map/ppermute | solution.py:26
  72.9 1.9 %collective-permute-start.33 = (bf16[1,96,1536]{2,1,0:T(8,128)(2,1)S(1)}, bf16[1,96,1536]{2,1,0:T(8,128)(2,1)S(1)}, u32[]{:S(2)}, u32[]{:S(2)}) collective-permute-start(bf16[1,96,1536]{2,1,0:T(8,128)(2,1)S(1)} %collective-permute-done.25.refs_8_), channel_id=1, source_target_pairs={{0,4},{4,0},{8,12},{12,8},{16,20},{20,16},{24,28},{28,24},{1,5},{5... | collective-permute-start | bytes 884744 | tf_op jit(solution)/shard_map/ppermute | solution.py:26
  73.0 3.3 %collective-permute-start.34 = (bf16[1,96,1536]{2,1,0:T(8,128)(2,1)S(1)}, bf16[1,96,1536]{2,1,0:T(8,128)(2,1)S(1)}, u32[]{:S(2)}, u32[]{:S(2)}) collective-permute-start(bf16[1,96,1536]{2,1,0:T(8,128)(2,1)S(1)} %collective-permute-done.26.refs_9_), channel_id=1, source_target_pairs={{0,4},{4,0},{8,12},{12,8},{16,20},{20,16},{24,28},{28,24},{1,5},{5... | collective-permute-start | bytes 884744 | tf_op jit(solution)/shard_map/ppermute | solution.py:26
  73.4 2.9 %collective-permute-start.35 = (bf16[1,96,1536]{2,1,0:T(8,128)(2,1)S(1)}, bf16[1,96,1536]{2,1,0:T(8,128)(2,1)S(1)}, u32[]{:S(2)}, u32[]{:S(2)}) collective-permute-start(bf16[1,96,1536]{2,1,0:T(8,128)(2,1)S(1)} %collective-permute-done.11.refs_14_), channel_id=1, source_target_pairs={{0,4},{4,0},{8,12},{12,8},{16,20},{20,16},{24,28},{28,24},{1,5},{5... | collective-permute-start | bytes 884744 | tf_op jit(solution)/shard_map/ppermute | solution.py:26
  74.0 2.4 %collective-permute-start.36 = (bf16[1,96,1536]{2,1,0:T(8,128)(2,1)S(1)}, bf16[1,96,1536]{2,1,0:T(8,128)(2,1)S(1)}, u32[]{:S(2)}, u32[]{:S(2)}) collective-permute-start(bf16[1,96,1536]{2,1,0:T(8,128)(2,1)S(1)} %collective-permute-done.23.refs_15_), channel_id=1, source_target_pairs={{0,4},{4,0},{8,12},{12,8},{16,20},{20,16},{24,28},{28,24},{1,5},{5... | collective-permute-start | bytes 884744 | tf_op jit(solution)/shard_map/ppermute | solution.py:26
  74.4 2.1 %collective-permute-start.37 = (bf16[1,96,1536]{2,1,0:T(8,128)(2,1)S(1)}, bf16[1,96,1536]{2,1,0:T(8,128)(2,1)S(1)}, u32[]{:S(2)}, u32[]{:S(2)}) collective-permute-start(bf16[1,96,1536]{2,1,0:T(8,128)(2,1)S(1)} %collective-permute-done.27.refs_16_), channel_id=1, source_target_pairs={{0,4},{4,0},{8,12},{12,8},{16,20},{20,16},{24,28},{28,24},{1,5},{5... | collective-permute-start | bytes 884744 | tf_op jit(solution)/shard_map/ppermute | solution.py:26
  74.8 2.1 %collective-permute-start.38 = (bf16[1,96,1536]{2,1,0:T(8,128)(2,1)S(1)}, bf16[1,96,1536]{2,1,0:T(8,128)(2,1)S(1)}, u32[]{:S(2)}, u32[]{:S(2)}) collective-permute-start(bf16[1,96,1536]{2,1,0:T(8,128)(2,1)S(1)} %collective-permute-done.28.refs_17_), channel_id=1, source_target_pairs={{0,4},{4,0},{8,12},{12,8},{16,20},{20,16},{24,28},{28,24},{1,5},{5... | collective-permute-start | bytes 884744 | tf_op jit(solution)/shard_map/ppermute | solution.py:26
  89.2 5.7 %collective-permute-start.40 = (bf16[4,96,1536]{2,1,0:T(8,128)(2,1)}, bf16[4,96,1536]{2,1,0:T(8,128)(2,1)S(1)}, u32[]{:S(2)}, u32[]{:S(2)}) collective-permute-start(bf16[4,96,1536]{2,1,0:T(8,128)(2,1)} %get-tuple-element.177), channel_id=1, source_target_pairs={{0,4},{4,0},{8,12},{12,8},{16,20},{20,16},{24,28},{28,24},{1,5},{5... | collective-permute-start | bytes 3538952 | tf_op jit(solution)/shard_map/ppermute | solution.py:26
  89.6 7.0 %collective-permute-start.39 = (bf16[128,768]{1,0:T(8,128)(2,1)S(1)}, bf16[128,768]{1,0:T(8,128)(2,1)S(1)}, u32[]{:S(2)}, u32[]{:S(2)}) collective-permute-start(bf16[128,768]{1,0:T(8,128)(2,1)S(1)} %copy-done.60), channel_id=1, source_target_pairs={{0,1},{1,0},{2,3},{3,2},{4,5},{5,4},{6,7},{7,6},{8,9},{9,8},{10,11... | collective-permute-start | bytes 589832 | tf_op jit(solution)/shard_map/ppermute | solution.py:26
  97.4 5.0 %collective-permute-start.42 = (bf16[4,96,1536]{2,1,0:T(8,128)(2,1)S(1)}, bf16[4,96,1536]{2,1,0:T(8,128)(2,1)S(1)}, u32[]{:S(2)}, u32[]{:S(2)}) collective-permute-start(bf16[4,96,1536]{2,1,0:T(8,128)(2,1)S(1)} %copy-done.57), channel_id=1, source_target_pairs={{0,4},{4,0},{8,12},{12,8},{16,20},{20,16},{24,28},{28,24},{1,5},{5... | collective-permute-start | bytes 3538952 | tf_op jit(solution)/shard_map/ppermute | solution.py:26
  97.4 7.3 %collective-permute-start.41 = (bf16[128,768]{1,0:T(8,128)(2,1)S(1)}, bf16[128,768]{1,0:T(8,128)(2,1)S(1)}, u32[]{:S(2)}, u32[]{:S(2)}) collective-permute-start(bf16[128,768]{1,0:T(8,128)(2,1)S(1)} %copy-done.59), channel_id=1, source_target_pairs={{0,1},{1,0},{2,3},{3,2},{4,5},{5,4},{6,7},{7,6},{8,9},{9,8},{10,11... | collective-permute-start | bytes 589832 | tf_op jit(solution)/shard_map/ppermute | solution.py:26
  98.3 19.4 %collective-permute-start.45 = (bf16[2,96,1536]{2,1,0:T(8,128)(2,1)S(1)}, bf16[2,96,1536]{2,1,0:T(8,128)(2,1)S(1)}, u32[]{:S(2)}, u32[]{:S(2)}) collective-permute-start(bf16[2,96,1536]{2,1,0:T(8,128)(2,1)S(1)} %slice.143), channel_id=1, source_target_pairs={{0,8},{4,12},{8,0},{12,4},{16,24},{20,28},{24,16},{28,20},{1,9},{5... | collective-permute-start | bytes 1769480 | tf_op jit(solution)/shard_map/ppermute | solution.py:26
  104.7 6.5 %collective-permute-start.43 = (bf16[128,768]{1,0:T(8,128)(2,1)S(1)}, bf16[128,768]{1,0:T(8,128)(2,1)S(1)}, u32[]{:S(2)}, u32[]{:S(2)}) collective-permute-start(bf16[128,768]{1,0:T(8,128)(2,1)S(1)} %copy-done.13), channel_id=1, source_target_pairs={{0,1},{1,0},{2,3},{3,2},{4,5},{5,4},{6,7},{7,6},{8,9},{9,8},{10,11... | collective-permute-start | bytes 589832 | tf_op jit(solution)/shard_map/ppermute | solution.py:26
  105.5 14.8 %collective-permute-start.44 = (bf16[2,96,1536]{2,1,0:T(8,128)(2,1)S(1)}, bf16[2,96,1536]{2,1,0:T(8,128)(2,1)S(1)}, u32[]{:S(2)}, u32[]{:S(2)}) collective-permute-start(bf16[2,96,1536]{2,1,0:T(8,128)(2,1)S(1)} %slice.142), channel_id=1, source_target_pairs={{0,16},{4,20},{8,24},{12,28},{16,0},{20,4},{24,8},{28,12},{1,17},{... | collective-permute-start | bytes 1769480 | tf_op jit(solution)/shard_map/ppermute | solution.py:26
  117.7 5.7 %collective-permute-start.46 = (bf16[4,96,768]{2,1,0:T(8,128)(2,1)}, bf16[4,96,768]{2,1,0:T(8,128)(2,1)S(1)}, u32[]{:S(2)}, u32[]{:S(2)}) collective-permute-start(bf16[4,96,768]{2,1,0:T(8,128)(2,1)} %get-tuple-element.200), channel_id=1, source_target_pairs={{0,4},{4,0},{8,12},{12,8},{16,20},{20,16},{24,28},{28,24},{1,5},{5... | collective-permute-start | bytes 1769480 | tf_op jit(solution)/shard_map/ppermute | solution.py:26
  120.5 10.0 %collective-permute-start.48 = (bf16[1,96,1536]{2,1,0:T(8,128)(2,1)S(1)}, bf16[1,96,1536]{2,1,0:T(8,128)(2,1)S(1)}, u32[]{:S(2)}, u32[]{:S(2)}) collective-permute-start(bf16[1,96,1536]{2,1,0:T(8,128)(2,1)S(1)} %slice.147), channel_id=1, source_target_pairs={{0,8},{4,12},{8,0},{12,4},{16,24},{20,28},{24,16},{28,20},{1,9},{5... | collective-permute-start | bytes 884744 | tf_op jit(solution)/shard_map/ppermute | solution.py:26
  121.9 8.6 %collective-permute-start.49 = (bf16[1,96,1536]{2,1,0:T(8,128)(2,1)S(1)}, bf16[1,96,1536]{2,1,0:T(8,128)(2,1)S(1)}, u32[]{:S(2)}, u32[]{:S(2)}) collective-permute-start(bf16[1,96,1536]{2,1,0:T(8,128)(2,1)S(1)} %slice.146), channel_id=1, source_target_pairs={{0,16},{4,20},{8,24},{12,28},{16,0},{20,4},{24,8},{28,12},{1,17},{... | collective-permute-start | bytes 884744 | tf_op jit(solution)/shard_map/ppermute | solution.py:26
  123.6 11.9 %collective-permute-start.47 = (bf16[2,96,768]{2,1,0:T(8,128)(2,1)S(1)}, bf16[2,96,768]{2,1,0:T(8,128)(2,1)S(1)}, u32[]{:S(2)}, u32[]{:S(2)}) collective-permute-start(bf16[2,96,768]{2,1,0:T(8,128)(2,1)S(1)} %slice.145), channel_id=1, source_target_pairs={{0,8},{4,12},{8,0},{12,4},{16,24},{20,28},{24,16},{28,20},{1,9},{5... | collective-permute-start | bytes 884744 | tf_op jit(solution)/shard_map/ppermute | solution.py:26
  130.4 10.1 %collective-permute-start.52 = (bf16[4,96,768]{2,1,0:T(8,128)(2,1)}, bf16[4,96,768]{2,1,0:T(8,128)(2,1)S(1)}, u32[]{:S(2)}, u32[]{:S(2)}) collective-permute-start(bf16[4,96,768]{2,1,0:T(8,128)(2,1)} %get-tuple-element.214), channel_id=1, source_target_pairs={{0,4},{4,0},{8,12},{12,8},{16,20},{20,16},{24,28},{28,24},{1,5},{5... | collective-permute-start | bytes 1769480 | tf_op jit(solution)/shard_map/ppermute | solution.py:26
  137.2 2.4 %collective-permute-start.53 = (f32[12,768]{1,0:T(8,128)}, f32[12,768]{1,0:T(8,128)S(1)}, u32[]{:S(2)}, u32[]{:S(2)}) collective-permute-start(f32[12,768]{1,0:T(8,128)} %sums.1), channel_id=1, source_target_pairs={{0,4},{4,0},{8,12},{12,8},{16,20},{20,16},{24,28},{28,24},{1,5},{5... | collective-permute-start | bytes 110600 | tf_op jit(solution)/shard_map/ppermute | solution.py:26
  137.2 7.7 %collective-permute-start.56 = (bf16[1,96,768]{2,1,0:T(8,128)(2,1)S(1)}, bf16[1,96,768]{2,1,0:T(8,128)(2,1)S(1)}, u32[]{:S(2)}, u32[]{:S(2)}) collective-permute-start(bf16[1,96,768]{2,1,0:T(8,128)(2,1)S(1)} %slice.149), channel_id=1, source_target_pairs={{0,16},{4,20},{8,24},{12,28},{16,0},{20,4},{24,8},{28,12},{1,17},{... | collective-permute-start | bytes 442376 | tf_op jit(solution)/shard_map/ppermute | solution.py:26
  138.8 16.5 %collective-permute-start.50 = (bf16[96,1536]{1,0:T(8,128)(2,1)S(1)}, bf16[96,1536]{1,0:T(8,128)(2,1)S(1)}, u32[]{:S(2)}, u32[]{:S(2)}) collective-permute-start(bf16[96,1536]{1,0:T(8,128)(2,1)S(1)} %bitcast.47), channel_id=1, source_target_pairs={{0,2},{1,3},{2,0},{3,1},{4,6},{5,7},{6,4},{7,5},{8,10},{9,11},{10,... | collective-permute-start | bytes 884744 | tf_op jit(solution)/shard_map/ppermute | solution.py:26
  140.7 14.6 %collective-permute-start.55 = (bf16[2,96,768]{2,1,0:T(8,128)(2,1)S(1)}, bf16[2,96,768]{2,1,0:T(8,128)(2,1)S(1)}, u32[]{:S(2)}, u32[]{:S(2)}) collective-permute-start(bf16[2,96,768]{2,1,0:T(8,128)(2,1)S(1)} %slice.144), channel_id=1, source_target_pairs={{0,16},{4,20},{8,24},{12,28},{16,0},{20,4},{24,8},{28,12},{1,17},{... | collective-permute-start | bytes 884744 | tf_op jit(solution)/shard_map/ppermute | solution.py:26
  142.5 12.7 %collective-permute-start.51 = (bf16[128,768]{1,0:T(8,128)(2,1)S(1)}, bf16[128,768]{1,0:T(8,128)(2,1)S(1)}, u32[]{:S(2)}, u32[]{:S(2)}) collective-permute-start(bf16[128,768]{1,0:T(8,128)(2,1)S(1)} %copy-done.58), channel_id=1, source_target_pairs={{0,1},{1,0},{2,3},{3,2},{4,5},{5,4},{6,7},{7,6},{8,9},{9,8},{10,11... | collective-permute-start | bytes 589832 | tf_op jit(solution)/shard_map/ppermute | solution.py:26
  143.8 7.1 %collective-permute-start.54 = (f32[12,768]{1,0:T(8,128)S(1)}, f32[12,768]{1,0:T(8,128)S(1)}, u32[]{:S(2)}, u32[]{:S(2)}) collective-permute-start(f32[12,768]{1,0:T(8,128)S(1)} %add.135), channel_id=1, source_target_pairs={{0,16},{4,20},{8,24},{12,28},{16,0},{20,4},{24,8},{28,12},{1,17},{... | collective-permute-start | bytes 110600 | tf_op jit(solution)/shard_map/ppermute | solution.py:26
  155.4 4.6 %collective-permute-start.59 = (f32[12,768]{1,0:T(8,128)S(1)}, f32[12,768]{1,0:T(8,128)S(1)}, u32[]{:S(2)}, u32[]{:S(2)}) collective-permute-start(f32[12,768]{1,0:T(8,128)S(1)} %add.136), channel_id=1, source_target_pairs={{0,8},{4,12},{8,0},{12,4},{16,24},{20,28},{24,16},{28,20},{1,9},{5... | collective-permute-start | bytes 110600 | tf_op jit(solution)/shard_map/ppermute | solution.py:26
  156.9 13.4 %collective-permute-start.57 = (bf16[1,96,768]{2,1,0:T(8,128)(2,1)S(1)}, bf16[1,96,768]{2,1,0:T(8,128)(2,1)S(1)}, u32[]{:S(2)}, u32[]{:S(2)}) collective-permute-start(bf16[1,96,768]{2,1,0:T(8,128)(2,1)S(1)} %slice.148), channel_id=1, source_target_pairs={{0,8},{4,12},{8,0},{12,4},{16,24},{20,28},{24,16},{28,20},{1,9},{5... | collective-permute-start | bytes 442376 | tf_op jit(solution)/shard_map/ppermute | solution.py:26
  157.6 12.7 %collective-permute-start.58 = (bf16[96,768]{1,0:T(8,128)(2,1)S(1)}, bf16[96,768]{1,0:T(8,128)(2,1)S(1)}, u32[]{:S(2)}, u32[]{:S(2)}) collective-permute-start(bf16[96,768]{1,0:T(8,128)(2,1)S(1)} %bitcast.51), channel_id=1, source_target_pairs={{0,2},{1,3},{2,0},{3,1},{4,6},{5,7},{6,4},{7,5},{8,10},{9,11},{10,... | collective-permute-start | bytes 442376 | tf_op jit(solution)/shard_map/ppermute | solution.py:26
  160.0 7.7 %collective-permute-start.62 = (f32[12,768]{1,0:T(8,128)S(1)}, f32[12,768]{1,0:T(8,128)S(1)}, u32[]{:S(2)}, u32[]{:S(2)}) collective-permute-start(f32[12,768]{1,0:T(8,128)S(1)} %add.142), channel_id=1, source_target_pairs={{0,3},{1,2},{2,1},{3,0},{4,7},{5,6},{6,5},{7,4},{8,11},{9,10},{10,... | collective-permute-start | bytes 110600 | tf_op jit(solution)/shard_map/ppermute | solution.py:26
  162.4 7.2 %collective-permute-start.61 = (f32[12,768]{1,0:T(8,128)S(1)}, f32[12,768]{1,0:T(8,128)S(1)}, u32[]{:S(2)}, u32[]{:S(2)}) collective-permute-start(f32[12,768]{1,0:T(8,128)S(1)} %add.142), channel_id=1, source_target_pairs={{0,2},{1,3},{2,0},{3,1},{4,6},{5,7},{6,4},{7,5},{8,10},{9,11},{10,... | collective-permute-start | bytes 110600 | tf_op jit(solution)/shard_map/ppermute | solution.py:26
  162.4 7.2 %collective-permute-start.60 = (f32[12,768]{1,0:T(8,128)S(1)}, f32[12,768]{1,0:T(8,128)S(1)}, u32[]{:S(2)}, u32[]{:S(2)}) collective-permute-start(f32[12,768]{1,0:T(8,128)S(1)} %add.142), channel_id=1, source_target_pairs={{0,1},{1,0},{2,3},{3,2},{4,5},{5,4},{6,7},{7,6},{8,9},{9,8},{10,11... | collective-permute-start | bytes 110600 | tf_op jit(solution)/shard_map/ppermute | solution.py:26
  (67 other events, 451.1 us)

commit v3 on v2

--- a/solution.py
+++ b/solution.py
@@ -90,6 +90,11 @@
     return [[((0,), piece[None])], [((0,), swap(piece[None], "tensor", 2))]]
 
 
+def with_columns(held, columns):
+    (ks, value), = held
+    return [(ks, jnp.concatenate([value, columns[None]], axis=2))]
+
+
 def gather_stage(pieces, stage):
     out = []
     for held, order in zip(pieces, bit_orders()):
@@ -193,21 +198,28 @@
     return now[:half], now[half:].astype(BF16)
 
 
+def scatter_send(sent, s, n):
+    return swap(sent, "dp", bit_orders()[s][:-1][::-1][n]).astype(F32)
+
+
 def scatter_step(kept, sent, s, n):
-    return kept + swap(sent, "dp", bit_orders()[s][:-1][::-1][n]).astype(F32)
+    return kept + scatter_send(sent, s, n)
+
+
+def scatter_on(kept, sent, s, first, halvings):
+    for n in range(first, halvings):
+        now = scatter_step(kept, sent, s, n)
+        if n < halvings - 1:
+            kept, sent = scatter_split(now)
+    return now[0]
 
 
 def scatter_end(own, other):
     return own + swap(other.astype(BF16), "tensor", 2).astype(F32)
 
 
-def spread_columns(value, index, count):
-    rows, cols = value.shape
-    return lax.dynamic_update_slice(jnp.zeros((rows, count * cols), F32), value, (0, index * cols))
-
-
-def plus_swapped(value, axis, bit):
-    return value + swap(value, axis, bit)
+def from_tensor(value):
+    return [value] + [swap(value, "tensor", k) for k in (1, 2, 3)]
 
 
 def norm_first_body(x_ref, g_ref, xh_ref, dy_ref, sum_ref):
@@ -217,6 +229,23 @@
     sum_ref[...] = column_sum(grad)
 
 
+def table_body(ids, own, one, two, three, out, wide):
+    cols, table = own.shape
+    wide[...] = jnp.zeros_like(wide)
+    for k, ref in enumerate((own, one, two, three)):
+        for r in range(4):
+            @pl.when(jnp.bitwise_xor(ids[2], k) == r)
+            def _(ref=ref, r=r):
+                wide[r * cols : (r + 1) * cols, 0:table] = ref[...]
+    rest = wide[...]
+    terms = []
+    for _ in range(3):
+        term = rest.astype(BF16)
+        rest = rest - term.astype(F32)
+        terms.append(term)
+    out[...] = jnp.concatenate([t[:, :16] for t in terms] + [jnp.zeros_like(terms[0][:, :80])], axis=1)
+
+
 def causal_mask(length):
     rows = lax.broadcasted_iota(jnp.int32, (length, length), 0)
     cols = lax.broadcasted_iota(jnp.int32, (length, length), 1)
@@ -224,19 +253,30 @@
 
 
 def attend_body(plan, n_arrays, head_cols, *refs):
-    ids, own, other, vec, biases = refs[:5]
-    pieces = refs[5 : 5 + n_arrays]
-    outs, (lse_out, a_out, keep, send, total, sems) = refs[5 + n_arrays : 11 + n_arrays], refs[11 + n_arrays :]
+    ids, own, other = refs[:3]
+    pieces = refs[3 : 3 + n_arrays]
+    outs, (lse_out, a_out, keep, send, vec, total, sems) = refs[3 + n_arrays : 9 + n_arrays], refs[9 + n_arrays :]
     w, qkv_out, ctx_out = outs[0:2], outs[2:4], outs[4:6]
     me, role = ids[0], ids[1]
     copies = place_pieces(pieces, plan, w, sems, me)
     rows = own.shape[0]
+    for copy in copies:
+        copy.wait()
+    terms = w[0][:, 4 * head_cols :].astype(F32).T
+    vec[...] = terms[0:16] + terms[16:32] + terms[32:48]
     gain, shift = vec[0:1, :], vec[1:2, :]
     for ref, at in ((own, role), (other, 1 - role)):
         a_rows = ref[...].astype(F32) * gain + shift
         a_out[pl.ds(pl.multiple_of(at * rows, rows), rows), :] = a_rows.astype(BF16)
-    for copy in copies:
-        copy.wait()
+
+    def of_shard(row, s):
+        shard = jnp.bitwise_xor(ids[2], 2 * s)
+        value = jnp.zeros((1, head_cols), F32)
+        for t in range(vec.shape[1] // head_cols):
+            part = vec[row : row + 1, t * head_cols : (t + 1) * head_cols]
+            value = jnp.where(shard == t, part, value)
+        return value
+
     seq = 2 * rows
     a_rows = a_out[...]
     mask = causal_mask(seq)
@@ -245,7 +285,8 @@
     heads = head_cols // HEAD_DIM
     attn = None
     for s in range(2):
-        qkv = dot(a_rows, w[s][:, : 3 * head_cols]) + biases[s : s + 1, :]
+        bias = [of_shard(2, s), jnp.zeros((1, head_cols), F32), of_shard(3, s)]
+        qkv = dot(a_rows, w[s][:, : 3 * head_cols]) + jnp.concatenate(bias, axis=1)
         qkv = qkv.astype(BF16)
         qkv_out[s][...] = qkv
         parts = []
@@ -262,7 +303,7 @@
             parts.append(dot(probs, v).astype(BF16))
         ctx = jnp.concatenate(parts, axis=1)
         ctx_out[s][...] = ctx
-        add = dot(ctx, w[s][:, 3 * head_cols :], NT)
+        add = dot(ctx, w[s][:, 3 * head_cols : 4 * head_cols], NT)
         attn = add if attn is None else attn + add
     lse_out[...] = lse_all
     total[...] = attn
@@ -278,7 +319,7 @@
 
 
 def feed_body(plan, n_arrays, hidden, *refs):
-    ids, m_own, m_other, dy_own, dy_other, bias = refs[:6]
+    ids, m_own, m_other, dy_own, dy_other, vec = refs[:6]
     pieces = refs[6 : 6 + n_arrays]
     act_out, dpre_out = refs[6 + n_arrays : 8 + n_arrays], refs[8 + n_arrays : 10 + n_arrays]
     m_out, dy_out, dm_keep, dm_send, br_keep, br_send, sum_out, w, sems = refs[10 + n_arrays :]
@@ -289,12 +330,14 @@
     dy_out[:rows] = dy_own[...]
     dy_out[rows:] = dy_other[...]
     m, dy = m_out[...], dy_out[...]
-    for copy in copies:
-        copy.wait()
     d_m = branch = None
     for s in range(2):
+        for entry, copy in zip(plan, copies):
+            if entry[2] == s:
+                copy.wait()
         w_fc, w_proj = w[s, :, :hidden], w[s, :, hidden:]
-        pre = dot(m, w_fc) + bias[s : s + 1, :]
+        bias = vec[pl.ds(8 + jnp.bitwise_xor(ids[2], 2 * s), 1), :]
+        pre = dot(m, w_fc) + bias
         act, slope = gelu_parts(pre)
         act_low = act.astype(BF16)
         act_out[s][...] = act_low
@@ -333,10 +376,10 @@
     ids, own, other, w, qkv_ref, lse_ref, a_ref, ctx_ref = refs[:8]
     last = s == 0
     if last:
-        da_before, xh_own, xh_other = refs[8:11]
-    keep_g, send_g, sum_heads = refs[11:14] if last else refs[8:11]
-    outs = refs[14:] if last else refs[11:]
-    dz, scratch = outs[-2:]
+        da_before, xh_own, xh_other, heads_other, second, fc_sum, bp_sum = refs[8:15]
+        keep_g, send_g, keep, send, total, normed, table, dz, scratch = refs[15:]
+    else:
+        keep_g, send_g, heads_out, da_out, dz, scratch = refs[8:]
     role = ids[1]
     rows = own.shape[0]
     seq = 2 * rows
@@ -346,7 +389,7 @@
     dz[theirs, :] = other[...]
     mask = causal_mask(seq)
     heads = head_cols // HEAD_DIM
-    d_ctx_all = dot(dz[...], w[:, 3 * head_cols :]).astype(BF16)
+    d_ctx_all = dot(dz[...], w[:, 3 * head_cols : 4 * head_cols]).astype(BF16)
     d_parts = [[], [], []]
     qkv = qkv_ref[...]
     for h in range(heads):
@@ -365,45 +408,44 @@
         d_parts[0].append(dot(d_scores, k))
         d_parts[1].append(dot(d_scores, q, TN))
     d_qkv = jnp.concatenate(d_parts[0] + d_parts[1] + d_parts[2], axis=1)
-    sum_heads[...] = column_sum(d_qkv)
+    heads_own = column_sum(d_qkv)
     d_qkv = d_qkv.astype(BF16)
-    grad = jnp.concatenate([dot(a_ref[...], d_qkv, TN), dot(dz[...], ctx_ref[...], TN)], axis=1)
-    put_grad(grad, s, scratch, keep_g, send_g, ids[0], block_rows)
+    grads = [dot(a_ref[...], d_qkv, TN), dot(dz[...], ctx_ref[...], TN)]
     d_a = dot(d_qkv, w[:, : 3 * head_cols], NT)
     if not last:
-        outs[0][...] = d_a
+        heads_out[...] = heads_own
+        da_out[...] = d_a
+        put_grad(jnp.concatenate(grads, axis=1), s, scratch, keep_g, send_g, ids[0], block_rows)
         return
-    keep, send, sum_wide, total, normed = outs[:5]
     d_a = d_a + da_before[...]
     total[...] = d_a
+    keep[...] = total[mine, :]
+    send[...] = total[theirs, :].astype(BF16)
     normed[mine, :] = xh_own[...]
     normed[theirs, :] = xh_other[...]
-    sum_wide[0:1, :] = column_sum(d_a * normed[...].astype(F32))
-    sum_wide[1:2, :] = column_sum(d_a)
-    keep[...] = total[mine, :]
-    send[...] = total[theirs, :].astype(BF16)
-
-
-def sums_body(head_cols, ids, wide, heads_own, heads_other, second, fc_sum, bp_sum, vec_out):
     z = ids[2]
-    vec_out[0:2, :] = wide[0:2, :]
-    vec_out[4:7, :] = second[0:3, :]
-    vec_out[7:8, :] = bp_sum[...]
-
-    def placed(own, other, t):
-        zero = jnp.zeros_like(own)
-        return jnp.where(z == t, own, zero) + jnp.where(jnp.bitwise_xor(z, 2) == t, other, zero)
-
-    n_z = vec_out.shape[1] // head_cols
+
+    def placed(own_value, other_value, t):
+        zero = jnp.zeros_like(own_value)
+        return jnp.where(z == t, own_value, zero) + jnp.where(
+            jnp.bitwise_xor(z, 2) == t, other_value, zero
+        )
+
+    table[...] = jnp.zeros_like(table)
+    table[0:1, :] = column_sum(d_a * normed[...].astype(F32))
+    table[1:2, :] = column_sum(d_a)
+    n_z = table.shape[1] // head_cols
     for row, part in ((2, 0), (3, 2)):
-        own, other = (
-            ref[:, part * head_cols : (part + 1) * head_cols] for ref in (heads_own, heads_other)
+        cols = slice(part * head_cols, (part + 1) * head_cols)
+        table[row : row + 1, :] = jnp.concatenate(
+            [placed(heads_own[:, cols], heads_other[:, cols], t) for t in range(n_z)], axis=1
         )
-        vec_out[row : row + 1, :] = jnp.concatenate(
-            [placed(own, other, t) for t in range(n_z)], axis=1
-        )
-    for t in range(vec_out.shape[0] - 8):
-        vec_out[8 + t : 9 + t, :] = placed(fc_sum[0:1, :], fc_sum[1:2, :], t)
+    table[4:7, :] = second[0:3, :]
+    table[7:8, :] = bp_sum[...]
+    for t in range(n_z):
+        table[8 + t : 9 + t, :] = placed(fc_sum[0:1, :], fc_sum[1:2, :], t)
+    grads.append(table[...].T)
+    put_grad(jnp.concatenate(grads, axis=1), s, scratch, keep_g, send_g, ids[0], block_rows)
 
 
 def norm_first_back_body(x_ref, keep_ref, recv_ref, grad1_ref, vec_ref, out_ref):
@@ -435,52 +477,48 @@
     part_b = jnp.concatenate([fc_weight[0], proj_weight[0].T], axis=1)
     bits = bit_orders()[0]
     stages = len(bits)
-    vec = spread_columns(vectors[0], me * n_z + z, n_dp * n_z)
+    parts_v = from_tensor(vectors[0].T)
     pieces_a = gather_start(part_a)
-    vec = plus_swapped(vec, "tensor", 1)
-    vec = plus_swapped(vec, "dp", bits[0])
     normed1, dy, bp_sum = call(
         norm_first_body, "norm_first", 2, [(row, BF16), (row, BF16), ((1, width), F32)], (inputs, out_grad)
     )
-    pieces_a, vec, part_b, normed1, dy = tied(pieces_a, vec, part_b, normed1, dy)
+    (table,) = call(
+        table_body,
+        "table",
+        1,
+        [((n_z * vec_cols, 128), BF16)],
+        (ids, *parts_v),
+        [pltpu.VMEM((n_z * vec_cols, 128), F32)],
+        smem,
+    )
+    pieces_a, part_b, normed1, table = tied(pieces_a, part_b, normed1, table)
+    pieces_a[0] = with_columns(pieces_a[0], table)
     normed1_other = swap(normed1, "tensor", 1)
     pieces_b = gather_start(part_b)
     for stage in range(stages):
         pieces_a = gather_stage(pieces_a, stage)
         if stage < stages - 2:
-            vec = plus_swapped(vec, "dp", bits[stage + 1])
-            pieces_a, vec, normed1_other = tied(pieces_a, vec, normed1_other)
+            pieces_a, normed1_other = tied(pieces_a, normed1_other)
         elif stage == stages - 2:
-            vec = plus_swapped(vec, "tensor", 3)
-            flat, vec = tied(pieces_a + pieces_b, vec)
+            (flat,) = tied(pieces_a + pieces_b)
             pieces_a, pieces_b = flat[:2], flat[2:]
-        else:
-            vec = plus_swapped(vec, "dp", bits[stage])
     pieces_b = gather_stage(pieces_b, 0)
     arrays_a, plan_a = piece_plan(pieces_a)
 
-    def of_shard(table):
-        return jnp.stack([lax.dynamic_index_in_dim(table, s, 0, False) for s in shard_ids])
-
-    bias_q = of_shard(vec[2].reshape(n_z, head_cols))
-    bias_v = of_shard(vec[3].reshape(n_z, head_cols))
-    biases = jnp.concatenate([bias_q, jnp.zeros_like(bias_q), bias_v], axis=1)
-    bias_fc = of_shard(vec[8:].reshape(n_z, hidden))
-
     def any_space(first, arrays):
         return {**smem, **{first + n: pl.ANY for n in range(len(arrays))}}
 
-    w_0, w_1, qkv_0, qkv_1, ctx_0, ctx_1, lse, a_seq, attn_keep, attn_send = call(
+    w_0, w_1, qkv_0, qkv_1, ctx_0, ctx_1, lse, a_seq, attn_keep, attn_send, vec = call(
         lambda *refs: attend_body(plan_a, len(arrays_a), head_cols, *refs),
         "attend",
         6,
-        [((width, 4 * head_cols), BF16)] * 2
+        [((width, 4 * head_cols + 128), BF16), ((width, 4 * head_cols), BF16)]
         + [((seq, 3 * head_cols), BF16)] * 2
         + [((seq, head_cols), BF16)] * 2
-        + [((seq, 128), F32), (both, BF16), (row, F32), (row, BF16)],
-        (ids, normed1, normed1_other, vec, biases, *arrays_a),
+        + [((seq, 128), F32), (both, BF16), (row, F32), (row, BF16), ((16, width), F32)],
+        (ids, normed1, normed1_other, *arrays_a),
         [pltpu.VMEM(both, F32), pltpu.SemaphoreType.DMA((len(plan_a),))],
-        any_space(5, arrays_a),
+        any_space(3, arrays_a),
     )
     pieces_b, attn_send = tied(pieces_b, attn_send)
     attn_recv = swap(attn_send, "tensor", 1)
@@ -504,7 +542,7 @@
         7,
         [((seq, hidden), BF16)] * 4
         + [(both, BF16), (both, BF16), (row, F32), (row, BF16), (row, F32), (row, BF16), ((2, hidden), F32)],
-        (ids, m, m_other, dy, dy_other, bias_fc, *arrays_b),
+        (ids, m, m_other, dy, dy_other, vec, *arrays_b),
         [pltpu.VMEM((2, width, 2 * hidden), BF16), pltpu.SemaphoreType.DMA((len(plan_b),))],
         any_space(6, arrays_b),
     )
@@ -541,71 +579,59 @@
     outputs = resid1 + (br_keep + br_recv.astype(F32)) + vec[7]
 
     def attend_back(s, w, qkv, ctx, more_args, more_outs, more_scratch):
+        cols = 4 * head_cols + 128 * (1 - s)
         return call(
             lambda *refs: attend_back_body(block_rows, head_cols, s, *refs),
             "attend_back_" + str(s),
             6,
-            grad_shapes(width, block_rows, 4 * head_cols)[:2] + [((1, 3 * head_cols), F32)] + more_outs,
+            grad_shapes(width, block_rows, cols)[:2] + more_outs,
             (ids, dz, dz_other, w, qkv, lse, a_seq, ctx, *more_args),
-            more_scratch + [pltpu.VMEM(both, BF16), pltpu.VMEM((width, 4 * head_cols), F32)],
+            more_scratch + [pltpu.VMEM(both, BF16), pltpu.VMEM((width, cols), F32)],
             smem,
         )
 
     halvings = stages - 1
-    keep_1, send_1, head_sums_1, da_1 = attend_back(1, w_1, qkv_1, ctx_1, (), [(both, F32)], [])
+    keep_1, send_1, head_sums_1, da_1 = attend_back(
+        1, w_1, qkv_1, ctx_1, (), [((1, 3 * head_cols), F32), (both, F32)], []
+    )
     halvings = stages - 1
-    now_b = [scatter_step(*split_b[s], s, 0) for s in range(2)]
-    split_b = [scatter_split(now) for now in now_b]
+    split_b = [scatter_split(scatter_step(*split_b[s], s, 0)) for s in range(2)]
     da_1, *flat = together(da_1, *split_b[0], *split_b[1])
     split_b = [flat[:2], flat[2:]]
     split_1 = scatter_split(scatter_core(keep_1, send_1, 1, block_rows))
     da_1, *split_1 = together(da_1, *split_1)
-    keep_0, send_0, head_sums_0, da_keep, da_send, wide_sums = attend_back(
+    keep_0, send_0, da_keep, da_send = attend_back(
         0,
         w_0,
         qkv_0,
         ctx_0,
-        (da_1, normed1, normed1_other),
-        [(row, F32), (row, BF16), ((2, width), F32)],
-        [pltpu.VMEM(both, F32), pltpu.VMEM(both, BF16)],
-    )
-    for n in range(1, halvings):
-        now_b = [scatter_step(*split_b[s], s, n) for s in range(2)]
-        if n < halvings - 1:
-            split_b = [scatter_split(now) for now in now_b]
+        (da_1, normed1, normed1_other, head_sums_1, second_sums, fc_sum, bp_sum),
+        [(row, F32), (row, BF16)],
+        [pltpu.VMEM(both, F32), pltpu.VMEM(both, BF16), pltpu.VMEM((128, width), F32)],
+    )
+    b_own, b_other = split_b
+    b_other = scatter_on(*b_other, 1, 1, halvings)
     now_1 = scatter_step(*split_1, 1, 0)
     split_1 = scatter_split(now_1)
-    da_send, wide_sums, *flat = together(da_send, wide_sums, *split_1, *now_b)
-    split_1, now_b = flat[:2], flat[2:]
+    split_0 = scatter_split(scatter_core(keep_0, send_0, 0, block_rows))
+    da_send, b_other, *flat = together(da_send, b_other, *split_1, *b_own)
+    split_1, b_own = flat[:2], flat[2:]
     da_recv = swap(da_send, "tensor", 1)
-    b_recv = swap(now_b[1][0].astype(BF16), "tensor", 2)
-    split_0 = scatter_split(scatter_core(keep_0, send_0, 0, block_rows))
-    (vec_sum,) = call(
-        lambda *refs: sums_body(head_cols, *refs),
-        "sums",
-        1,
-        [((vec_rows, width), F32)],
-        (ids, wide_sums, head_sums_0, head_sums_1, second_sums, fc_sum, bp_sum),
-        (),
-        smem,
-    )
-    vec_sum = plus_swapped(vec_sum, "dp", 1)
-    *split_0, vec_sum = together(*split_0, vec_sum)
+    b_recv = swap(b_other.astype(BF16), "tensor", 2)
+    b_own = scatter_on(*b_own, 0, 1, halvings)
     for n in range(halvings):
         now_0 = scatter_step(*split_0, 0, n)
-        vec_sum = plus_swapped(vec_sum, "dp", bits[:-1][::-1][n])
         if n + 1 < halvings:
             now_1 = scatter_step(*split_1, 1, n + 1)
             split_0 = scatter_split(now_0)
             split_1 = scatter_split(now_1) if n + 2 < halvings else (now_1,)
-            if n == 0:
-                b_recv, da_recv, vec_sum = together(b_recv, da_recv, vec_sum)
-            *flat, vec_sum = together(*split_0, *split_1, vec_sum)
+            b_recv, b_own, da_recv, *flat = together(b_recv, b_own, da_recv, *split_0, *split_1)
             split_0, split_1 = flat[:2], flat[2:]
-    b_grad = now_b[0][0] + b_recv.astype(F32)
-    vec_sum = vec_sum + swap(vec_sum, "tensor", 1) + swap(vec_sum, "tensor", 2) + swap(vec_sum, "tensor", 3)
-    a_grad = scatter_end(now_0[0], split_1[0][0])
-    vector_grad = lax.dynamic_slice_in_dim(vec_sum, (me * n_z + z) * vec_cols, vec_cols, 1)
+    b_grad = b_own + b_recv.astype(F32)
+    table_sum = now_0[0][:, 4 * head_cols :]
+    table_sum = sum(from_tensor(table_sum[:, :16]))
+    a_grad = scatter_end(now_0[0][:, : 4 * head_cols], split_1[0][0])
+    vector_grad = lax.dynamic_slice_in_dim(table_sum[:, :vec_rows], z * vec_cols, vec_cols, 0).T
     (input_grad,) = call(
         norm_first_back_body,
         "norm_first_back",

time: 173 us -> 161 us (0.931)
  starting transfers between devices: 59.3 us -> 48.8 us
  waiting for transfers between devices: 46.5 us -> 44.5 us
    ppermute x63 -> x58, starting transfers between devices: 59.3 us -> 48.8 us  [swap(): return lax.ppermute(value, axis, [(i, i ^ bits) for i in range(size)])]
    ppermute x63 -> x58, waiting for transfers between devices: 46.5 us -> 44.5 us  [swap(): return lax.ppermute(value, axis, [(i, i ^ bits) for i in range(size)])]
    unnamed x127 -> x128, local copies, waits for them, and re-layouts: 10.8 us -> 11.8 us
  transfers between devices with their start and end apart: 63 -> 58, of which waited for: 26 -> 29; matrix products, arithmetic and copies ran while one was open for 6% -> 8% of each run, Pallas kernels for 19% -> 21%
where the time goes in v3:
time: 161 us; the launch traced here: 160 us
  starting transfers between devices  48.8 us (30%)
  waiting for transfers between devices  44.5 us (28%)
  Pallas kernels  44.1 us (27%)
  local copies, waits for them, and re-layouts  15 us (9%)
  other arithmetic  6.07 us (4%)
    ppermute x58, starting transfers between devices, swap(): return lax.ppermute(value, axis, [(i, i ^ bits) for i in range(size)])  48.8 us
    ppermute x58, waiting for transfers between devices, swap(): return lax.ppermute(value, axis, [(i, i ^ bits) for i in range(size)])  44.5 us
    pallas_call x11, Pallas kernels, call(): pl.pallas_call(body, name=name, out_shape=[jax.ShapeDtypeStruct(shape, dt...  44.1 us
    unnamed x128, local copies, waits for them, and re-layouts  11.8 us
  transfers between devices with their start and end apart: 58, of which 29 were waited for; matrix products, arithmetic and copies ran while one was open for 8% of the time, Pallas kernels for 21%

profile of v3, /device:TPU:0, one launch (start us, length us, event | category | flops | bytes accessed | tf_op | source)
XLA Modules:
  0.0 160.1 jit_solution(16896046994743100900)
XLA Ops:
  0.6 0.8 copy.23
  1.4 3.0 %collective-permute-start.1 = (f32[24,12]{1,0:T(8,128)S(1)}, f32[24,12]{1,0:T(8,128)S(1)}, u32[]{:S(2)}, u32[]{:S(2)}) collective-permute-start(f32[24,12]{1,0:T(8,128)S(1)} %bitcast.57), channel_id=1, source_target_pairs={{0,1},{1,0},{2,3},{3,2},{4,5},{5,4},{6,7},{7,6},{8,9},{9,8},{10,11... | collective-permute-start | bytes 3464 | tf_op jit(solution)/shard_map/ppermute | solution.py:26
  4.4 2.6 %collective-permute-start.2 = (f32[24,12]{1,0:T(8,128)S(1)}, f32[24,12]{1,0:T(8,128)S(1)}, u32[]{:S(2)}, u32[]{:S(2)}) collective-permute-start(f32[24,12]{1,0:T(8,128)S(1)} %bitcast.58), channel_id=1, source_target_pairs={{0,2},{1,3},{2,0},{3,1},{4,6},{5,7},{6,4},{7,5},{8,10},{9,11},{10,... | collective-permute-start | bytes 3464 | tf_op jit(solution)/shard_map/ppermute | solution.py:26
  7.0 0.9 copy.21
  7.9 1.1 copy.20
  9.2 2.0 %collective-permute-start = (bf16[1,96,768]{2,1,0:T(8,128)(2,1)S(1)}, bf16[1,96,768]{2,1,0:T(8,128)(2,1)S(1)}, u32[]{:S(2)}, u32[]{:S(2)}) collective-permute-start(bf16[1,96,768]{2,1,0:T(8,128)(2,1)S(1)} %maximum_bitcast_fusion), channel_id=1, source_target_pairs={{0,2},{1,3},{2,0},{3,1},{4,6},{5,7},{6,4},{7,5},{8,10},{9,11},{10,... | collective-permute-start | bytes 442376 | tf_op jit(solution)/shard_map/ppermute | solution.py:26
  11.2 1.0 pad_maximum_fusion
  12.9 2.0 %norm_first.1 = (bf16[128,768]{1,0:T(8,128)(2,1)}, bf16[128,768]{1,0:T(8,128)(2,1)}, f32[1,768]{1,0:T(1,128)}) custom-call(f32[128,768]{1,0:T(8,128)} %x_ref.5, f32[128,768]{1,0:T(8,128)} %grad_ref.1), custom_call_target="tpu_custom_call" | custom-call | flops 100000000 | bytes 200000 | tf_op jit(solution)/shard_map/norm_first/pallas_call | solution.py:69
  16.1 1.6 %table.1 = bf16[96,128]{1,0:T(8,128)(2,1)} custom-call(s32[3]{0:T(128)} %pad_add_fusion.ids.refs_0_, f32[24,12]{1,0:T(8,128)} %bitcast.60, f32[24,12]{1,0:T(8,128)} %copy-done.58, f32[24,12]{1,0:T(8,128)} %copy-done.59, f32[24,12]{1,0:T(8,128)} %copy-done.60), custom_call_target="tpu_custom_call" | custom-call | flops 50000000 | bytes 100000 | tf_op jit(solution)/shard_map/table/pallas_call | solution.py:69
  17.7 0.8 collective-permute-done.refs_11_
  18.5 1.7 %collective-permute-start.6 = (bf16[128,768]{1,0:T(8,128)(2,1)}, bf16[128,768]{1,0:T(8,128)(2,1)S(1)}, u32[]{:S(2)}, u32[]{:S(2)}) collective-permute-start(bf16[128,768]{1,0:T(8,128)(2,1)} %get-tuple-element.114.refs_1_.refs_9_), channel_id=1, source_target_pairs={{0,1},{1,0},{2,3},{3,2},{4,5},{5,4},{6,7},{7,6},{8,9},{9,8},{10,11... | collective-permute-start | bytes 589832 | tf_op jit(solution)/shard_map/ppermute | solution.py:26
  20.2 0.8 pad_maximum_fusion.1.refs_3_
  21.0 1.6 collective-permute-start.4
  22.5 1.5 collective-permute-start.5
  24.1 1.3 collective-permute-start.11
  25.3 2.4 %collective-permute-done.5.refs_12_ = bf16[1,96,768]{2,1,0:T(8,128)(2,1)S(1)} collective-permute-done((bf16[1,96,768]{2,1,0:T(8,128)(2,1)S(1)}, bf16[1,96,768]{2,1,0:T(8,128)(2,1)S(1)}, u32[]{:S(2)}, u32[]{:S(2)}) %collective-permute-start.5) | collective-permute-done | bytes 147488 | tf_op jit(solution)/shard_map/ppermute | solution.py:26
  27.7 1.6 collective-permute-start.7
  30.3 1.5 collective-permute-start.10
  31.8 6.2 %collective-permute-done.11.refs_14_ = bf16[1,96,1536]{2,1,0:T(8,128)(2,1)S(1)} collective-permute-done((bf16[1,96,1536]{2,1,0:T(8,128)(2,1)S(1)}, bf16[1,96,1536]{2,1,0:T(8,128)(2,1)S(1)}, u32[]{:S(2)}, u32[]{:S(2)}) %collective-permute-start.11) | collective-permute-done | bytes 294944 | tf_op jit(solution)/shard_map/ppermute | solution.py:26
  41.3 0.8 collective-permute-done.13.refs_8_
  43.7 6.8 %attend.1 = (bf16[768,896]{1,0:T(8,128)(2,1)}, bf16[768,768]{1,0:T(8,128)(2,1)}, bf16[256,576]{1,0:T(8,128)(2,1)}, bf16[256,576]{1,0:T(8,128)(2,1)}, bf16[256,19...) custom-call(s32[3]{0:T(128)} %pad_add_fusion.ids.refs_0_, ...), custom_call_target="tpu_custom_call" | custom-call | flops 300000000 | bytes 600000 | tf_op jit(solution)/shard_map/attend/pallas_call | solution.py:69
  50.6 2.0 %collective-permute-start.28 = (bf16[128,768]{1,0:T(8,128)(2,1)S(1)}, bf16[128,768]{1,0:T(8,128)(2,1)S(1)}, u32[]{:S(2)}, u32[]{:S(2)}) collective-permute-start(bf16[128,768]{1,0:T(8,128)(2,1)S(1)} %copy-done.32), channel_id=1, source_target_pairs={{0,1},{1,0},{2,3},{3,2},{4,5},{5,4},{6,7},{7,6},{8,9},{9,8},{10,11... | collective-permute-start | bytes 589832 | tf_op jit(solution)/shard_map/ppermute | solution.py:26
  52.6 1.5 collective-permute-start.23
  54.7 1.4 collective-permute-start.25
  56.1 2.4 %collective-permute-done.22.recv_ref = bf16[128,768]{1,0:T(8,128)(2,1)S(1)} collective-permute-done((bf16[128,768]{1,0:T(8,128)(2,1)}, bf16[128,768]{1,0:T(8,128)(2,1)S(1)}, u32[]{:S(2)}, u32[]{:S(2)}) %collective-permute-start.22) | collective-permute-done | bytes 196640 | tf_op jit(solution)/shard_map/ppermute | solution.py:26
  58.6 1.4 collective-permute-start.26
  60.0 2.1 %norm_second.1 = (f32[128,768]{1,0:T(8,128)}, bf16[128,768]{1,0:T(8,128)(2,1)}) custom-call(f32[128,768]{1,0:T(8,128)} %x_ref.5, f32[128,768]{1,0:T(8,128)} %get-tuple-element.132.keep_ref, bf16[128,768]{1,0:T(8,128)(2,1)} %copy-done.37, f32[16,768]{1,0:T(8,128)} %get-tuple-element.137.vec_ref.refs_5_), custom_call_target="tpu_custom_call" | custom-call | flops 100000000 | bytes 200000 | tf_op jit(solution)/shard_map/norm_second/pallas_call | solution.py:69
  62.6 5.0 %collective-permute-done.24.refs_9_ = bf16[1,96,1536]{2,1,0:T(8,128)(2,1)S(1)} collective-permute-done((bf16[1,96,1536]{2,1,0:T(8,128)(2,1)S(1)}, bf16[1,96,1536]{2,1,0:T(8,128)(2,1)S(1)}, u32[]{:S(2)}, u32[]{:S(2)}) %collective-permute-start.24) | collective-permute-done | bytes 294944 | tf_op jit(solution)/shard_map/ppermute | solution.py:26
  67.6 1.5 collective-permute-done.26.refs_17_
  74.7 7.0 %feed.1 = (bf16[256,768]{1,0:T(8,128)(2,1)}, bf16[256,768]{1,0:T(8,128)(2,1)}, bf16[256,768]{1,0:T(8,128)(2,1)}, bf16[256,768]{1,0:T(8,128)(2,1)}, bf16[256,768]...) custom-call(s32[3]{0:T(128)} %pad_add_fusion.ids.refs_0_, ...), custom_call_target="tpu_custom_call" | custom-call | flops 350000000 | bytes 700000 | tf_op jit(solution)/shard_map/feed/pallas_call | solution.py:69
  81.7 3.7 %feed_grad_1.1 = (bf16[4,96,1536]{2,1,0:T(8,128)(2,1)}, bf16[4,96,1536]{2,1,0:T(8,128)(2,1)}) custom-call(s32[3]{0:T(128)} %pad_add_fusion.ids.refs_0_, bf16[256,768]{1,0:T(8,128)(2,1)} %get-tuple-element.158.refs_1_, bf16[256,768]{1,0:T(8,128)(2,1)} %get-tuple-element.159.refs_2_, bf16[256,768]{1,0:T(8,128)(2,1)} %get-tuple-element.164.refs_3_, ...), custom_call_target="tpu_custom_call" | custom-call | flops 150000000 | bytes 300000 | tf_op jit(solution)/shard_map/feed_grad_1/pallas_call | solution.py:69
  85.9 3.7 %feed_grad_0.1 = (bf16[4,96,1536]{2,1,0:T(8,128)(2,1)}, bf16[4,96,1536]{2,1,0:T(8,128)(2,1)}) custom-call(s32[3]{0:T(128)} %pad_add_fusion.ids.refs_0_, bf16[256,768]{1,0:T(8,128)(2,1)} %get-tuple-element.158.refs_1_, bf16[256,768]{1,0:T(8,128)(2,1)} %get-tuple-element.159.refs_2_, bf16[256,768]{1,0:T(8,128)(2,1)} %get-tuple-element.160.refs_3_, ...), custom_call_target="tpu_custom_call" | custom-call | flops 150000000 | bytes 300000 | tf_op jit(solution)/shard_map/feed_grad_0/pallas_call | solution.py:69
  90.1 1.4 copy-done
  91.5 1.3 collective-permute-done.37.recv_ref
  92.8 1.1 collective-permute-start.39
  93.9 1.4 collective-permute-start.43
  95.4 2.4 %norm_second_back.1 = (f32[128,768]{1,0:T(8,128)}, bf16[128,768]{1,0:T(8,128)(2,1)}, f32[3,768]{1,0:T(4,128)}) custom-call(f32[128,768]{1,0:T(8,128)} %get-tuple-element.138.resid_ref, f32[128,768]{1,0:T(8,128)} %get-tuple-element.156.keep_ref, bf16[128,768]{1,0:T(8,128)(2,1)} %copy-done.36, f32[128,768]{1,0:T(8,128)} %grad_ref.1, ...), custom_call_target="tpu_custom_call" | custom-call | flops 100000000 | bytes 200000 | tf_op jit(solution)/shard_map/norm_second_back/pallas_call | solution.py:69
  98.3 1.4 copy-done.1
  99.8 0.9 slice.147
  100.8 1.0 collective-permute-start.41
  101.7 1.5 collective-permute-start.42
  104.0 3.5 %collective-permute-done.41.refs_2_ = bf16[128,768]{1,0:T(8,128)(2,1)S(1)} collective-permute-done((bf16[128,768]{1,0:T(8,128)(2,1)S(1)}, bf16[128,768]{1,0:T(8,128)(2,1)S(1)}, u32[]{:S(2)}, u32[]{:S(2)}) %collective-permute-start.41) | collective-permute-done | bytes 196640 | tf_op jit(solution)/shard_map/ppermute | solution.py:26
  108.1 5.7 %attend_back_1.1 = (bf16[4,96,768]{2,1,0:T(8,128)(2,1)}, bf16[4,96,768]{2,1,0:T(8,128)(2,1)}, f32[1,576]{1,0:T(1,128)}, f32[256,768]{1,0:T(8,128)}) custom-call(s32[3]{0:T(128)} %pad_add_fusion.ids.refs_0_, bf16[128,768]{1,0:T(8,128)(2,1)} %get-tuple-element.174.refs_1_, bf16[128,768]{1,0:T(8,128)(2,1)} %copy-done.12, ...), custom_call_target="tpu_custom_call" | custom-call | flops 300000000 | bytes 600000 | tf_op jit(solution)/shard_map/attend_back_1/pallas_call | solution.py:69
  113.9 1.2 convert_add_fusion.4
  115.2 1.6 %collective-permute-done.42 = bf16[2,96,1536]{2,1,0:T(8,128)(2,1)S(1)} collective-permute-done((bf16[2,96,1536]{2,1,0:T(8,128)(2,1)}, bf16[2,96,1536]{2,1,0:T(8,128)(2,1)S(1)}, u32[]{:S(2)}, u32[]{:S(2)}) %collective-permute-start.42) | collective-permute-done | bytes 589856 | tf_op jit(solution)/shard_map/ppermute | solution.py:26
  117.0 1.6 collective-permute-start.45
  118.8 0.8 collective-permute-start.46
  119.6 6.4 %attend_back_0.1 = (bf16[4,96,896]{2,1,0:T(8,128)(2,1)}, bf16[4,96,896]{2,1,0:T(8,128)(2,1)}, f32[128,768]{1,0:T(8,128)}, bf16[128,768]{1,0:T(8,128)(2,1)}) custom-call(s32[3]{0:T(128)} %pad_add_fusion.ids.refs_0_, bf16[128,768]{1,0:T(8,128)(2,1)} %get-tuple-element.174.refs_1_, bf16[128,768]{1,0:T(8,128)(2,1)} %copy-done.12, ...), custom_call_target="tpu_custom_call" | custom-call | flops 300000000 | bytes 600000 | tf_op jit(solution)/shard_map/attend_back_0/pallas_call | solution.py:69
  126.6 1.5 collective-permute-done.46
  128.2 1.6 collective-permute-start.52
  129.8 0.8 add_add_fusion
  130.7 1.5 collective-permute-start.47
  132.9 1.0 collective-permute-start.49
  134.1 1.5 collective-permute-start.51
  135.6 4.5 %collective-permute-done.48 = bf16[1,96,1536]{2,1,0:T(8,128)(2,1)S(1)} collective-permute-done((bf16[1,96,1536]{2,1,0:T(8,128)(2,1)S(1)}, bf16[1,96,1536]{2,1,0:T(8,128)(2,1)S(1)}, u32[]{:S(2)}, u32[]{:S(2)}) %collective-permute-start.48) | collective-permute-done | bytes 294944 | tf_op jit(solution)/shard_map/ppermute | solution.py:26
  140.2 2.5 %collective-permute-done.51 = bf16[2,96,896]{2,1,0:T(8,128)(2,1)S(1)} collective-permute-done((bf16[2,96,896]{2,1,0:T(8,128)(2,1)S(1)}, bf16[2,96,896]{2,1,0:T(8,128)(2,1)S(1)}, u32[]{:S(2)}, u32[]{:S(2)}) %collective-permute-start.51) | collective-permute-done | bytes 344096 | tf_op jit(solution)/shard_map/ppermute | solution.py:26
  142.8 3.4 %collective-permute-done.47 = bf16[96,1536]{1,0:T(8,128)(2,1)S(1)} collective-permute-done((bf16[96,1536]{1,0:T(8,128)(2,1)S(1)}, bf16[96,1536]{1,0:T(8,128)(2,1)S(1)}, u32[]{:S(2)}, u32[]{:S(2)}) %collective-permute-start.47) | collective-permute-done | bytes 294944 | tf_op jit(solution)/shard_map/ppermute | solution.py:26
  147.0 2.4 %norm_first_back.1 = f32[128,768]{1,0:T(8,128)} custom-call(f32[128,768]{1,0:T(8,128)} %x_ref.5, f32[128,768]{1,0:T(8,128)} %get-tuple-element.196.keep_ref, bf16[128,768]{1,0:T(8,128)(2,1)} %copy-done.35, f32[128,768]{1,0:T(8,128)} %get-tuple-element.213.grad1_ref, f32[16,768]{1,0:T(8,128)} %get-tuple-element.137.vec_ref.refs_5_), custom_call_target="tpu_custom_call" | custom-call | flops 100000000 | bytes 200000 | tf_op jit(solution)/shard_map/norm_first_back/pallas_call | solution.py:69
  149.4 0.8 slice_bitcast_fusion
  150.2 1.9 %collective-permute-done.53 = bf16[1,96,896]{2,1,0:T(8,128)(2,1)S(1)} collective-permute-done((bf16[1,96,896]{2,1,0:T(8,128)(2,1)S(1)}, bf16[1,96,896]{2,1,0:T(8,128)(2,1)S(1)}, u32[]{:S(2)}, u32[]{:S(2)}) %collective-permute-start.53) | collective-permute-done | bytes 172064 | tf_op jit(solution)/shard_map/ppermute | solution.py:26
  152.2 2.0 %collective-permute-start.57 = (f32[96,16]{1,0:T(8,128)S(1)}, f32[96,16]{1,0:T(8,128)S(1)}, u32[]{:S(2)}, u32[]{:S(2)}) collective-permute-start(f32[96,16]{1,0:T(8,128)S(1)} %slice.127), channel_id=1, source_target_pairs={{0,3},{1,2},{2,1},{3,0},{4,7},{5,6},{6,5},{7,4},{8,11},{9,10},{10,... | collective-permute-start | bytes 18440 | tf_op jit(solution)/shard_map/ppermute | solution.py:26
  154.3 2.3 %collective-permute-start.55 = (f32[96,16]{1,0:T(8,128)S(1)}, f32[96,16]{1,0:T(8,128)S(1)}, u32[]{:S(2)}, u32[]{:S(2)}) collective-permute-start(f32[96,16]{1,0:T(8,128)S(1)} %slice.127), channel_id=1, source_target_pairs={{0,1},{1,0},{2,3},{3,2},{4,5},{5,4},{6,7},{7,6},{8,9},{9,8},{10,11... | collective-permute-start | bytes 18440 | tf_op jit(solution)/shard_map/ppermute | solution.py:26
  156.9 0.9 copy.25
  158.5 0.8 collective-permute-done.56
  (240 shorter events, 22.1 us)
Async XLA Ops:
  1.4 13.5 %collective-permute-start.1 = (f32[24,12]{1,0:T(8,128)S(1)}, f32[24,12]{1,0:T(8,128)S(1)}, u32[]{:S(2)}, u32[]{:S(2)}) collective-permute-start(f32[24,12]{1,0:T(8,128)S(1)} %bitcast.57), channel_id=1, source_target_pairs={{0,1},{1,0},{2,3},{3,2},{4,5},{5,4},{6,7},{7,6},{8,9},{9,8},{10,11... | collective-permute-start | bytes 3464 | tf_op jit(solution)/shard_map/ppermute | solution.py:26
  4.4 10.5 %collective-permute-start.2 = (f32[24,12]{1,0:T(8,128)S(1)}, f32[24,12]{1,0:T(8,128)S(1)}, u32[]{:S(2)}, u32[]{:S(2)}) collective-permute-start(f32[24,12]{1,0:T(8,128)S(1)} %bitcast.58), channel_id=1, source_target_pairs={{0,2},{1,3},{2,0},{3,1},{4,6},{5,7},{6,4},{7,5},{8,10},{9,11},{10,... | collective-permute-start | bytes 3464 | tf_op jit(solution)/shard_map/ppermute | solution.py:26
  7.0 7.9 %collective-permute-start.3 = (f32[24,12]{1,0:T(8,128)S(1)}, f32[24,12]{1,0:T(8,128)S(1)}, u32[]{:S(2)}, u32[]{:S(2)}) collective-permute-start(f32[24,12]{1,0:T(8,128)S(1)} %bitcast.59), channel_id=1, source_target_pairs={{0,3},{1,2},{2,1},{3,0},{4,7},{5,6},{6,5},{7,4},{8,11},{9,10},{10,... | collective-permute-start | bytes 3464 | tf_op jit(solution)/shard_map/ppermute | solution.py:26
  9.2 9.3 %collective-permute-start = (bf16[1,96,768]{2,1,0:T(8,128)(2,1)S(1)}, bf16[1,96,768]{2,1,0:T(8,128)(2,1)S(1)}, u32[]{:S(2)}, u32[]{:S(2)}) collective-permute-start(bf16[1,96,768]{2,1,0:T(8,128)(2,1)S(1)} %maximum_bitcast_fusion), channel_id=1, source_target_pairs={{0,2},{1,3},{2,0},{3,1},{4,6},{5,7},{6,4},{7,5},{8,10},{9,11},{10,... | collective-permute-start | bytes 442376 | tf_op jit(solution)/shard_map/ppermute | solution.py:26
  12.2 56.8 %copy-start.7 = (bf16[96,1536]{1,0:T(8,128)(2,1)}, bf16[96,1536]{1,0:T(8,128)(2,1)S(1)}, u32[]{:S(2)}) copy-start(bf16[96,1536]{1,0:T(8,128)(2,1)S(1)} %pad_maximum_fusion) | copy-start | bytes 884740
  18.5 24.1 %copy-start.45 = (bf16[1,96,768]{2,1,0:T(8,128)(2,1)}, bf16[1,96,768]{2,1,0:T(8,128)(2,1)S(1)}, u32[]{:S(2)}) copy-start(bf16[1,96,768]{2,1,0:T(8,128)(2,1)S(1)} %collective-permute-done.refs_11_) | copy-start | bytes 442372
  18.5 9.2 %collective-permute-start.6 = (bf16[128,768]{1,0:T(8,128)(2,1)}, bf16[128,768]{1,0:T(8,128)(2,1)S(1)}, u32[]{:S(2)}, u32[]{:S(2)}) collective-permute-start(bf16[128,768]{1,0:T(8,128)(2,1)} %get-tuple-element.114.refs_1_.refs_9_), channel_id=1, source_target_pairs={{0,1},{1,0},{2,3},{3,2},{4,5},{5,4},{6,7},{7,6},{8,9},{9,8},{10,11... | collective-permute-start | bytes 589832 | tf_op jit(solution)/shard_map/ppermute | solution.py:26
  21.0 6.7 %collective-permute-start.4 = (bf16[1,96,896]{2,1,0:T(8,128)(2,1)S(1)}, bf16[1,96,896]{2,1,0:T(8,128)(2,1)S(1)}, u32[]{:S(2)}, u32[]{:S(2)}) collective-permute-start(bf16[1,96,896]{2,1,0:T(8,128)(2,1)S(1)} %pad_maximum_fusion.1.refs_3_), channel_id=1, source_target_pairs={{0,8},{4,12},{8,0},{12,4},{16,24},{20,28},{24,16},{28,20},{1,9},{5... | collective-permute-start | bytes 516104 | tf_op jit(solution)/shard_map/ppermute | solution.py:26
  22.5 5.1 %collective-permute-start.5 = (bf16[1,96,768]{2,1,0:T(8,128)(2,1)S(1)}, bf16[1,96,768]{2,1,0:T(8,128)(2,1)S(1)}, u32[]{:S(2)}, u32[]{:S(2)}) collective-permute-start(bf16[1,96,768]{2,1,0:T(8,128)(2,1)S(1)} %collective-permute-done.refs_11_), channel_id=1, source_target_pairs={{0,16},{4,20},{8,24},{12,28},{16,0},{20,4},{24,8},{28,12},{1,17},{... | collective-permute-start | bytes 442376 | tf_op jit(solution)/shard_map/ppermute | solution.py:26
  24.1 26.6 %copy-start.32 = (bf16[128,768]{1,0:T(8,128)(2,1)S(1)}, bf16[128,768]{1,0:T(8,128)(2,1)}, u32[]{:S(2)}) copy-start(bf16[128,768]{1,0:T(8,128)(2,1)} %get-tuple-element.144.refs_3_) | copy-start | bytes 589828
  24.1 14.0 %collective-permute-start.11 = (bf16[1,96,1536]{2,1,0:T(8,128)(2,1)S(1)}, bf16[1,96,1536]{2,1,0:T(8,128)(2,1)S(1)}, u32[]{:S(2)}, u32[]{:S(2)}) collective-permute-start(bf16[1,96,1536]{2,1,0:T(8,128)(2,1)S(1)} %bitcast.45), channel_id=1, source_target_pairs={{0,2},{1,3},{2,0},{3,1},{4,6},{5,7},{6,4},{7,5},{8,10},{9,11},{10,... | collective-permute-start | bytes 884744 | tf_op jit(solution)/shard_map/ppermute | solution.py:26
  27.7 10.4 %collective-permute-start.7 = (bf16[1,96,896]{2,1,0:T(8,128)(2,1)S(1)}, bf16[1,96,896]{2,1,0:T(8,128)(2,1)S(1)}, u32[]{:S(2)}, u32[]{:S(2)}) collective-permute-start(bf16[1,96,896]{2,1,0:T(8,128)(2,1)S(1)} %pad_maximum_fusion.1.refs_3_), channel_id=1, source_target_pairs={{0,16},{4,20},{8,24},{12,28},{16,0},{20,4},{24,8},{28,12},{1,17},{... | collective-permute-start | bytes 516104 | tf_op jit(solution)/shard_map/ppermute | solution.py:26
  29.3 8.8 %collective-permute-start.8 = (bf16[1,96,896]{2,1,0:T(8,128)(2,1)S(1)}, bf16[1,96,896]{2,1,0:T(8,128)(2,1)S(1)}, u32[]{:S(2)}, u32[]{:S(2)}) collective-permute-start(bf16[1,96,896]{2,1,0:T(8,128)(2,1)S(1)} %collective-permute-done.4.refs_4_), channel_id=1, source_target_pairs={{0,16},{4,20},{8,24},{12,28},{16,0},{20,4},{24,8},{28,12},{1,17},{... | collective-permute-start | bytes 516104 | tf_op jit(solution)/shard_map/ppermute | solution.py:26
  29.8 8.3 %collective-permute-start.9 = (bf16[1,96,768]{2,1,0:T(8,128)(2,1)S(1)}, bf16[1,96,768]{2,1,0:T(8,128)(2,1)S(1)}, u32[]{:S(2)}, u32[]{:S(2)}) collective-permute-start(bf16[1,96,768]{2,1,0:T(8,128)(2,1)S(1)} %collective-permute-done.refs_11_), channel_id=1, source_target_pairs={{0,8},{4,12},{8,0},{12,4},{16,24},{20,28},{24,16},{28,20},{1,9},{5... | collective-permute-start | bytes 442376 | tf_op jit(solution)/shard_map/ppermute | solution.py:26
  30.3 7.7 %collective-permute-start.10 = (bf16[1,96,768]{2,1,0:T(8,128)(2,1)S(1)}, bf16[1,96,768]{2,1,0:T(8,128)(2,1)S(1)}, u32[]{:S(2)}, u32[]{:S(2)}) collective-permute-start(bf16[1,96,768]{2,1,0:T(8,128)(2,1)S(1)} %collective-permute-done.5.refs_12_), channel_id=1, source_target_pairs={{0,8},{4,12},{8,0},{12,4},{16,24},{20,28},{24,16},{28,20},{1,9},{5... | collective-permute-start | bytes 442376 | tf_op jit(solution)/shard_map/ppermute | solution.py:26
  38.1 32.1 %copy-start.17 = (bf16[1,96,1536]{2,1,0:T(8,128)(2,1)}, bf16[1,96,1536]{2,1,0:T(8,128)(2,1)S(1)}, u32[]{:S(2)}) copy-start(bf16[1,96,1536]{2,1,0:T(8,128)(2,1)S(1)} %collective-permute-done.11.refs_14_) | copy-start | bytes 884740
  38.1 1.4 collective-permute-start.16
  38.2 1.9 %collective-permute-start.17 = (bf16[1,96,768]{2,1,0:T(8,128)(2,1)S(1)}, bf16[1,96,768]{2,1,0:T(8,128)(2,1)S(1)}, u32[]{:S(2)}, u32[]{:S(2)}) collective-permute-start(bf16[1,96,768]{2,1,0:T(8,128)(2,1)S(1)} %collective-permute-done.5.refs_12_), channel_id=1, source_target_pairs={{0,4},{4,0},{8,12},{12,8},{16,20},{20,16},{24,28},{28,24},{1,5},{5... | collective-permute-start | bytes 442376 | tf_op jit(solution)/shard_map/ppermute | solution.py:26
  38.7 2.5 %collective-permute-start.12 = (bf16[1,96,896]{2,1,0:T(8,128)(2,1)S(1)}, bf16[1,96,896]{2,1,0:T(8,128)(2,1)S(1)}, u32[]{:S(2)}, u32[]{:S(2)}) collective-permute-start(bf16[1,96,896]{2,1,0:T(8,128)(2,1)S(1)} %pad_maximum_fusion.1.refs_3_), channel_id=1, source_target_pairs={{0,4},{4,0},{8,12},{12,8},{16,20},{20,16},{24,28},{28,24},{1,5},{5... | collective-permute-start | bytes 516104 | tf_op jit(solution)/shard_map/ppermute | solution.py:26
  38.8 1.9 %collective-permute-start.18 = (bf16[1,96,768]{2,1,0:T(8,128)(2,1)S(1)}, bf16[1,96,768]{2,1,0:T(8,128)(2,1)S(1)}, u32[]{:S(2)}, u32[]{:S(2)}) collective-permute-start(bf16[1,96,768]{2,1,0:T(8,128)(2,1)S(1)} %collective-permute-done.9.refs_13_), channel_id=1, source_target_pairs={{0,4},{4,0},{8,12},{12,8},{16,20},{20,16},{24,28},{28,24},{1,5},{5... | collective-permute-start | bytes 442376 | tf_op jit(solution)/shard_map/ppermute | solution.py:26
  39.2 1.5 collective-permute-start.19
  39.6 10.9 %collective-permute-start.20 = (bf16[1,96,1536]{2,1,0:T(8,128)(2,1)S(1)}, bf16[1,96,1536]{2,1,0:T(8,128)(2,1)S(1)}, u32[]{:S(2)}, u32[]{:S(2)}) collective-permute-start(bf16[1,96,1536]{2,1,0:T(8,128)(2,1)S(1)} %bitcast.46), channel_id=1, source_target_pairs={{0,8},{4,12},{8,0},{12,4},{16,24},{20,28},{24,16},{28,20},{1,9},{5... | collective-permute-start | bytes 884744 | tf_op jit(solution)/shard_map/ppermute | solution.py:26
  40.1 10.4 %collective-permute-start.21 = (bf16[1,96,1536]{2,1,0:T(8,128)(2,1)S(1)}, bf16[1,96,1536]{2,1,0:T(8,128)(2,1)S(1)}, u32[]{:S(2)}, u32[]{:S(2)}) collective-permute-start(bf16[1,96,1536]{2,1,0:T(8,128)(2,1)S(1)} %collective-permute-done.11.refs_14_), channel_id=1, source_target_pairs={{0,16},{4,20},{8,24},{12,28},{16,0},{20,4},{24,8},{28,12},{1,17},{... | collective-permute-start | bytes 884744 | tf_op jit(solution)/shard_map/ppermute | solution.py:26
  40.7 1.4 collective-permute-start.13
  40.7 1.6 %collective-permute-start.14 = (bf16[1,96,896]{2,1,0:T(8,128)(2,1)S(1)}, bf16[1,96,896]{2,1,0:T(8,128)(2,1)S(1)}, u32[]{:S(2)}, u32[]{:S(2)}) collective-permute-start(bf16[1,96,896]{2,1,0:T(8,128)(2,1)S(1)} %collective-permute-done.7.refs_5_), channel_id=1, source_target_pairs={{0,4},{4,0},{8,12},{12,8},{16,20},{20,16},{24,28},{28,24},{1,5},{5... | collective-permute-start | bytes 516104 | tf_op jit(solution)/shard_map/ppermute | solution.py:26
  41.2 1.4 collective-permute-start.15
  50.5 23.2 %copy-start.18 = (bf16[1,96,1536]{2,1,0:T(8,128)(2,1)}, bf16[1,96,1536]{2,1,0:T(8,128)(2,1)S(1)}, u32[]{:S(2)}) copy-start(bf16[1,96,1536]{2,1,0:T(8,128)(2,1)S(1)} %collective-permute-done.20.refs_7_) | copy-start | bytes 884740
  50.5 23.1 %copy-start.19 = (bf16[1,96,1536]{2,1,0:T(8,128)(2,1)}, bf16[1,96,1536]{2,1,0:T(8,128)(2,1)S(1)}, u32[]{:S(2)}) copy-start(bf16[1,96,1536]{2,1,0:T(8,128)(2,1)S(1)} %collective-permute-done.21.refs_15_) | copy-start | bytes 884740
  50.5 8.0 %collective-permute-start.22 = (bf16[128,768]{1,0:T(8,128)(2,1)}, bf16[128,768]{1,0:T(8,128)(2,1)S(1)}, u32[]{:S(2)}, u32[]{:S(2)}) collective-permute-start(bf16[128,768]{1,0:T(8,128)(2,1)} %get-tuple-element.136), channel_id=1, source_target_pairs={{0,1},{1,0},{2,3},{3,2},{4,5},{5,4},{6,7},{7,6},{8,9},{9,8},{10,11... | collective-permute-start | bytes 589832 | tf_op jit(solution)/shard_map/ppermute | solution.py:26
  50.6 11.5 %collective-permute-start.28 = (bf16[128,768]{1,0:T(8,128)(2,1)S(1)}, bf16[128,768]{1,0:T(8,128)(2,1)S(1)}, u32[]{:S(2)}, u32[]{:S(2)}) collective-permute-start(bf16[128,768]{1,0:T(8,128)(2,1)S(1)} %copy-done.32), channel_id=1, source_target_pairs={{0,1},{1,0},{2,3},{3,2},{4,5},{5,4},{6,7},{7,6},{8,9},{9,8},{10,11... | collective-permute-start | bytes 589832 | tf_op jit(solution)/shard_map/ppermute | solution.py:26
  52.6 9.9 %collective-permute-start.23 = (bf16[1,96,1536]{2,1,0:T(8,128)(2,1)S(1)}, bf16[1,96,1536]{2,1,0:T(8,128)(2,1)S(1)}, u32[]{:S(2)}, u32[]{:S(2)}) collective-permute-start(bf16[1,96,1536]{2,1,0:T(8,128)(2,1)S(1)} %bitcast.47), channel_id=1, source_target_pairs={{0,16},{4,20},{8,24},{12,28},{16,0},{20,4},{24,8},{28,12},{1,17},{... | collective-permute-start | bytes 884744 | tf_op jit(solution)/shard_map/ppermute | solution.py:26
  54.1 13.4 %collective-permute-start.24 = (bf16[1,96,1536]{2,1,0:T(8,128)(2,1)S(1)}, bf16[1,96,1536]{2,1,0:T(8,128)(2,1)S(1)}, u32[]{:S(2)}, u32[]{:S(2)}) collective-permute-start(bf16[1,96,1536]{2,1,0:T(8,128)(2,1)S(1)} %collective-permute-done.20.refs_7_), channel_id=1, source_target_pairs={{0,16},{4,20},{8,24},{12,28},{16,0},{20,4},{24,8},{28,12},{1,17},{... | collective-permute-start | bytes 884744 | tf_op jit(solution)/shard_map/ppermute | solution.py:26
  54.7 12.9 %collective-permute-start.25 = (bf16[1,96,1536]{2,1,0:T(8,128)(2,1)S(1)}, bf16[1,96,1536]{2,1,0:T(8,128)(2,1)S(1)}, u32[]{:S(2)}, u32[]{:S(2)}) collective-permute-start(bf16[1,96,1536]{2,1,0:T(8,128)(2,1)S(1)} %collective-permute-done.11.refs_14_), channel_id=1, source_target_pairs={{0,8},{4,12},{8,0},{12,4},{16,24},{20,28},{24,16},{28,20},{1,9},{5... | collective-permute-start | bytes 884744 | tf_op jit(solution)/shard_map/ppermute | solution.py:26
  58.6 10.5 %collective-permute-start.26 = (bf16[1,96,1536]{2,1,0:T(8,128)(2,1)S(1)}, bf16[1,96,1536]{2,1,0:T(8,128)(2,1)S(1)}, u32[]{:S(2)}, u32[]{:S(2)}) collective-permute-start(bf16[1,96,1536]{2,1,0:T(8,128)(2,1)S(1)} %collective-permute-done.21.refs_15_), channel_id=1, source_target_pairs={{0,8},{4,12},{8,0},{12,4},{16,24},{20,28},{24,16},{28,20},{1,9},{5... | collective-permute-start | bytes 884744 | tf_op jit(solution)/shard_map/ppermute | solution.py:26
  62.1 6.9 %collective-permute-start.27 = (bf16[128,768]{1,0:T(8,128)(2,1)}, bf16[128,768]{1,0:T(8,128)(2,1)S(1)}, u32[]{:S(2)}, u32[]{:S(2)}) collective-permute-start(bf16[128,768]{1,0:T(8,128)(2,1)} %get-tuple-element.139.refs_1_), channel_id=1, source_target_pairs={{0,1},{1,0},{2,3},{3,2},{4,5},{5,4},{6,7},{7,6},{8,9},{9,8},{10,11... | collective-permute-start | bytes 589832 | tf_op jit(solution)/shard_map/ppermute | solution.py:26
  69.1 1.6 %collective-permute-start.29 = (bf16[1,96,1536]{2,1,0:T(8,128)(2,1)S(1)}, bf16[1,96,1536]{2,1,0:T(8,128)(2,1)S(1)}, u32[]{:S(2)}, u32[]{:S(2)}) collective-permute-start(bf16[1,96,1536]{2,1,0:T(8,128)(2,1)S(1)} %bitcast.48), channel_id=1, source_target_pairs={{0,4},{4,0},{8,12},{12,8},{16,20},{20,16},{24,28},{28,24},{1,5},{5... | collective-permute-start | bytes 884744 | tf_op jit(solution)/shard_map/ppermute | solution.py:26
  69.1 2.0 %collective-permute-start.30 = (bf16[1,96,1536]{2,1,0:T(8,128)(2,1)S(1)}, bf16[1,96,1536]{2,1,0:T(8,128)(2,1)S(1)}, u32[]{:S(2)}, u32[]{:S(2)}) collective-permute-start(bf16[1,96,1536]{2,1,0:T(8,128)(2,1)S(1)} %collective-permute-done.20.refs_7_), channel_id=1, source_target_pairs={{0,4},{4,0},{8,12},{12,8},{16,20},{20,16},{24,28},{28,24},{1,5},{5... | collective-permute-start | bytes 884744 | tf_op jit(solution)/shard_map/ppermute | solution.py:26
  69.6 1.9 %collective-permute-start.31 = (bf16[1,96,1536]{2,1,0:T(8,128)(2,1)S(1)}, bf16[1,96,1536]{2,1,0:T(8,128)(2,1)S(1)}, u32[]{:S(2)}, u32[]{:S(2)}) collective-permute-start(bf16[1,96,1536]{2,1,0:T(8,128)(2,1)S(1)} %collective-permute-done.23.refs_8_), channel_id=1, source_target_pairs={{0,4},{4,0},{8,12},{12,8},{16,20},{20,16},{24,28},{28,24},{1,5},{5... | collective-permute-start | bytes 884744 | tf_op jit(solution)/shard_map/ppermute | solution.py:26
  69.7 2.3 %collective-permute-start.32 = (bf16[1,96,1536]{2,1,0:T(8,128)(2,1)S(1)}, bf16[1,96,1536]{2,1,0:T(8,128)(2,1)S(1)}, u32[]{:S(2)}, u32[]{:S(2)}) collective-permute-start(bf16[1,96,1536]{2,1,0:T(8,128)(2,1)S(1)} %collective-permute-done.24.refs_9_), channel_id=1, source_target_pairs={{0,4},{4,0},{8,12},{12,8},{16,20},{20,16},{24,28},{28,24},{1,5},{5... | collective-permute-start | bytes 884744 | tf_op jit(solution)/shard_map/ppermute | solution.py:26
  70.2 2.2 %collective-permute-start.33 = (bf16[1,96,1536]{2,1,0:T(8,128)(2,1)S(1)}, bf16[1,96,1536]{2,1,0:T(8,128)(2,1)S(1)}, u32[]{:S(2)}, u32[]{:S(2)}) collective-permute-start(bf16[1,96,1536]{2,1,0:T(8,128)(2,1)S(1)} %collective-permute-done.11.refs_14_), channel_id=1, source_target_pairs={{0,4},{4,0},{8,12},{12,8},{16,20},{20,16},{24,28},{28,24},{1,5},{5... | collective-permute-start | bytes 884744 | tf_op jit(solution)/shard_map/ppermute | solution.py:26
  70.7 2.1 %collective-permute-start.34 = (bf16[1,96,1536]{2,1,0:T(8,128)(2,1)S(1)}, bf16[1,96,1536]{2,1,0:T(8,128)(2,1)S(1)}, u32[]{:S(2)}, u32[]{:S(2)}) collective-permute-start(bf16[1,96,1536]{2,1,0:T(8,128)(2,1)S(1)} %collective-permute-done.21.refs_15_), channel_id=1, source_target_pairs={{0,4},{4,0},{8,12},{12,8},{16,20},{20,16},{24,28},{28,24},{1,5},{5... | collective-permute-start | bytes 884744 | tf_op jit(solution)/shard_map/ppermute | solution.py:26
  71.1 2.1 %collective-permute-start.35 = (bf16[1,96,1536]{2,1,0:T(8,128)(2,1)S(1)}, bf16[1,96,1536]{2,1,0:T(8,128)(2,1)S(1)}, u32[]{:S(2)}, u32[]{:S(2)}) collective-permute-start(bf16[1,96,1536]{2,1,0:T(8,128)(2,1)S(1)} %collective-permute-done.25.refs_16_), channel_id=1, source_target_pairs={{0,4},{4,0},{8,12},{12,8},{16,20},{20,16},{24,28},{28,24},{1,5},{5... | collective-permute-start | bytes 884744 | tf_op jit(solution)/shard_map/ppermute | solution.py:26
  71.6 2.1 %collective-permute-start.36 = (bf16[1,96,1536]{2,1,0:T(8,128)(2,1)S(1)}, bf16[1,96,1536]{2,1,0:T(8,128)(2,1)S(1)}, u32[]{:S(2)}, u32[]{:S(2)}) collective-permute-start(bf16[1,96,1536]{2,1,0:T(8,128)(2,1)S(1)} %collective-permute-done.26.refs_17_), channel_id=1, source_target_pairs={{0,4},{4,0},{8,12},{12,8},{16,20},{20,16},{24,28},{28,24},{1,5},{5... | collective-permute-start | bytes 884744 | tf_op jit(solution)/shard_map/ppermute | solution.py:26
  85.4 4.2 %collective-permute-start.38 = (bf16[4,96,1536]{2,1,0:T(8,128)(2,1)}, bf16[4,96,1536]{2,1,0:T(8,128)(2,1)S(1)}, u32[]{:S(2)}, u32[]{:S(2)}) collective-permute-start(bf16[4,96,1536]{2,1,0:T(8,128)(2,1)} %get-tuple-element.167), channel_id=1, source_target_pairs={{0,4},{4,0},{8,12},{12,8},{16,20},{20,16},{24,28},{28,24},{1,5},{5... | collective-permute-start | bytes 3538952 | tf_op jit(solution)/shard_map/ppermute | solution.py:26
  85.6 7.2 %collective-permute-start.37 = (bf16[128,768]{1,0:T(8,128)(2,1)S(1)}, bf16[128,768]{1,0:T(8,128)(2,1)S(1)}, u32[]{:S(2)}, u32[]{:S(2)}) collective-permute-start(bf16[128,768]{1,0:T(8,128)(2,1)S(1)} %copy-done.57), channel_id=1, source_target_pairs={{0,1},{1,0},{2,3},{3,2},{4,5},{5,4},{6,7},{7,6},{8,9},{9,8},{10,11... | collective-permute-start | bytes 589832 | tf_op jit(solution)/shard_map/ppermute | solution.py:26
  92.8 5.1 %collective-permute-start.40 = (bf16[4,96,1536]{2,1,0:T(8,128)(2,1)S(1)}, bf16[4,96,1536]{2,1,0:T(8,128)(2,1)S(1)}, u32[]{:S(2)}, u32[]{:S(2)}) collective-permute-start(bf16[4,96,1536]{2,1,0:T(8,128)(2,1)S(1)} %copy-done.54), channel_id=1, source_target_pairs={{0,4},{4,0},{8,12},{12,8},{16,20},{20,16},{24,28},{28,24},{1,5},{5... | collective-permute-start | bytes 3538952 | tf_op jit(solution)/shard_map/ppermute | solution.py:26
  92.8 7.9 %collective-permute-start.39 = (bf16[128,768]{1,0:T(8,128)(2,1)S(1)}, bf16[128,768]{1,0:T(8,128)(2,1)S(1)}, u32[]{:S(2)}, u32[]{:S(2)}) collective-permute-start(bf16[128,768]{1,0:T(8,128)(2,1)S(1)} %copy-done.56), channel_id=1, source_target_pairs={{0,1},{1,0},{2,3},{3,2},{4,5},{5,4},{6,7},{7,6},{8,9},{9,8},{10,11... | collective-permute-start | bytes 589832 | tf_op jit(solution)/shard_map/ppermute | solution.py:26
  93.9 20.0 %collective-permute-start.43 = (bf16[2,96,1536]{2,1,0:T(8,128)(2,1)S(1)}, bf16[2,96,1536]{2,1,0:T(8,128)(2,1)}, u32[]{:S(2)}, u32[]{:S(2)}) collective-permute-start(bf16[2,96,1536]{2,1,0:T(8,128)(2,1)S(1)} %slice.148), channel_id=1, source_target_pairs={{0,8},{4,12},{8,0},{12,4},{16,24},{20,28},{24,16},{28,20},{1,9},{5... | collective-permute-start | bytes 1769480 | tf_op jit(solution)/shard_map/ppermute | solution.py:26
  100.8 6.7 %collective-permute-start.41 = (bf16[128,768]{1,0:T(8,128)(2,1)S(1)}, bf16[128,768]{1,0:T(8,128)(2,1)S(1)}, u32[]{:S(2)}, u32[]{:S(2)}) collective-permute-start(bf16[128,768]{1,0:T(8,128)(2,1)S(1)} %copy-done.11), channel_id=1, source_target_pairs={{0,1},{1,0},{2,3},{3,2},{4,5},{5,4},{6,7},{7,6},{8,9},{9,8},{10,11... | collective-permute-start | bytes 589832 | tf_op jit(solution)/shard_map/ppermute | solution.py:26
  101.7 15.1 %collective-permute-start.42 = (bf16[2,96,1536]{2,1,0:T(8,128)(2,1)}, bf16[2,96,1536]{2,1,0:T(8,128)(2,1)S(1)}, u32[]{:S(2)}, u32[]{:S(2)}) collective-permute-start(bf16[2,96,1536]{2,1,0:T(8,128)(2,1)} %slice.147), channel_id=1, source_target_pairs={{0,16},{4,20},{8,24},{12,28},{16,0},{20,4},{24,8},{28,12},{1,17},{... | collective-permute-start | bytes 1769480 | tf_op jit(solution)/shard_map/ppermute | solution.py:26
  113.9 4.7 %collective-permute-start.44 = (bf16[4,96,768]{2,1,0:T(8,128)(2,1)}, bf16[4,96,768]{2,1,0:T(8,128)(2,1)S(1)}, u32[]{:S(2)}, u32[]{:S(2)}) collective-permute-start(bf16[4,96,768]{2,1,0:T(8,128)(2,1)} %get-tuple-element.190), channel_id=1, source_target_pairs={{0,4},{4,0},{8,12},{12,8},{16,20},{20,16},{24,28},{28,24},{1,5},{5... | collective-permute-start | bytes 1769480 | tf_op jit(solution)/shard_map/ppermute | solution.py:26
  117.0 9.5 %collective-permute-start.45 = (bf16[1,96,1536]{2,1,0:T(8,128)(2,1)S(1)}, bf16[1,96,1536]{2,1,0:T(8,128)(2,1)S(1)}, u32[]{:S(2)}, u32[]{:S(2)}) collective-permute-start(bf16[1,96,1536]{2,1,0:T(8,128)(2,1)S(1)} %slice.151), channel_id=1, source_target_pairs={{0,16},{4,20},{8,24},{12,28},{16,0},{20,4},{24,8},{28,12},{1,17},{... | collective-permute-start | bytes 884744 | tf_op jit(solution)/shard_map/ppermute | solution.py:26
  118.8 9.3 %collective-permute-start.46 = (bf16[2,96,768]{2,1,0:T(8,128)(2,1)S(1)}, bf16[2,96,768]{2,1,0:T(8,128)(2,1)S(1)}, u32[]{:S(2)}, u32[]{:S(2)}) collective-permute-start(bf16[2,96,768]{2,1,0:T(8,128)(2,1)S(1)} %slice.150), channel_id=1, source_target_pairs={{0,8},{4,12},{8,0},{12,4},{16,24},{20,28},{24,16},{28,20},{1,9},{5... | collective-permute-start | bytes 884744 | tf_op jit(solution)/shard_map/ppermute | solution.py:26
  126.0 7.9 %collective-permute-start.50 = (bf16[4,96,896]{2,1,0:T(8,128)(2,1)}, bf16[4,96,896]{2,1,0:T(8,128)(2,1)S(1)}, u32[]{:S(2)}, u32[]{:S(2)}) collective-permute-start(bf16[4,96,896]{2,1,0:T(8,128)(2,1)} %get-tuple-element.209), channel_id=1, source_target_pairs={{0,4},{4,0},{8,12},{12,8},{16,20},{20,16},{24,28},{28,24},{1,5},{5... | collective-permute-start | bytes 2064392 | tf_op jit(solution)/shard_map/ppermute | solution.py:26
  128.2 5.6 %collective-permute-start.52 = (bf16[1,96,768]{2,1,0:T(8,128)(2,1)S(1)}, bf16[1,96,768]{2,1,0:T(8,128)(2,1)S(1)}, u32[]{:S(2)}, u32[]{:S(2)}) collective-permute-start(bf16[1,96,768]{2,1,0:T(8,128)(2,1)S(1)} %slice.154), channel_id=1, source_target_pairs={{0,16},{4,20},{8,24},{12,28},{16,0},{20,4},{24,8},{28,12},{1,17},{... | collective-permute-start | bytes 442376 | tf_op jit(solution)/shard_map/ppermute | solution.py:26
  130.7 15.6 %collective-permute-start.47 = (bf16[96,1536]{1,0:T(8,128)(2,1)S(1)}, bf16[96,1536]{1,0:T(8,128)(2,1)S(1)}, u32[]{:S(2)}, u32[]{:S(2)}) collective-permute-start(bf16[96,1536]{1,0:T(8,128)(2,1)S(1)} %add_bitcast_fusion.1), channel_id=1, source_target_pairs={{0,2},{1,3},{2,0},{3,1},{4,6},{5,7},{6,4},{7,5},{8,10},{9,11},{10,... | collective-permute-start | bytes 884744 | tf_op jit(solution)/shard_map/ppermute | solution.py:26
  132.1 8.0 %collective-permute-start.48 = (bf16[1,96,1536]{2,1,0:T(8,128)(2,1)S(1)}, bf16[1,96,1536]{2,1,0:T(8,128)(2,1)S(1)}, u32[]{:S(2)}, u32[]{:S(2)}) collective-permute-start(bf16[1,96,1536]{2,1,0:T(8,128)(2,1)S(1)} %slice.152), channel_id=1, source_target_pairs={{0,8},{4,12},{8,0},{12,4},{16,24},{20,28},{24,16},{28,20},{1,9},{5... | collective-permute-start | bytes 884744 | tf_op jit(solution)/shard_map/ppermute | solution.py:26
  132.9 9.9 %collective-permute-start.49 = (bf16[128,768]{1,0:T(8,128)(2,1)S(1)}, bf16[128,768]{1,0:T(8,128)(2,1)S(1)}, u32[]{:S(2)}, u32[]{:S(2)}) collective-permute-start(bf16[128,768]{1,0:T(8,128)(2,1)S(1)} %copy-done.55), channel_id=1, source_target_pairs={{0,1},{1,0},{2,3},{3,2},{4,5},{5,4},{6,7},{7,6},{8,9},{9,8},{10,11... | collective-permute-start | bytes 589832 | tf_op jit(solution)/shard_map/ppermute | solution.py:26
  134.1 8.6 %collective-permute-start.51 = (bf16[2,96,896]{2,1,0:T(8,128)(2,1)S(1)}, bf16[2,96,896]{2,1,0:T(8,128)(2,1)S(1)}, u32[]{:S(2)}, u32[]{:S(2)}) collective-permute-start(bf16[2,96,896]{2,1,0:T(8,128)(2,1)S(1)} %slice.149), channel_id=1, source_target_pairs={{0,16},{4,20},{8,24},{12,28},{16,0},{20,4},{24,8},{28,12},{1,17},{... | collective-permute-start | bytes 1032200 | tf_op jit(solution)/shard_map/ppermute | solution.py:26
  146.2 5.9 %collective-permute-start.53 = (bf16[1,96,896]{2,1,0:T(8,128)(2,1)S(1)}, bf16[1,96,896]{2,1,0:T(8,128)(2,1)S(1)}, u32[]{:S(2)}, u32[]{:S(2)}) collective-permute-start(bf16[1,96,896]{2,1,0:T(8,128)(2,1)S(1)} %slice.153), channel_id=1, source_target_pairs={{0,8},{4,12},{8,0},{12,4},{16,24},{20,28},{24,16},{28,20},{1,9},{5... | collective-permute-start | bytes 516104 | tf_op jit(solution)/shard_map/ppermute | solution.py:26
  146.9 9.8 %collective-permute-start.54 = (bf16[96,768]{1,0:T(8,128)(2,1)S(1)}, bf16[96,768]{1,0:T(8,128)(2,1)S(1)}, u32[]{:S(2)}, u32[]{:S(2)}) collective-permute-start(bf16[96,768]{1,0:T(8,128)(2,1)S(1)} %bitcast.55), channel_id=1, source_target_pairs={{0,2},{1,3},{2,0},{3,1},{4,6},{5,7},{6,4},{7,5},{8,10},{9,11},{10,... | collective-permute-start | bytes 442376 | tf_op jit(solution)/shard_map/ppermute | solution.py:26
  152.2 6.4 %collective-permute-start.57 = (f32[96,16]{1,0:T(8,128)S(1)}, f32[96,16]{1,0:T(8,128)S(1)}, u32[]{:S(2)}, u32[]{:S(2)}) collective-permute-start(f32[96,16]{1,0:T(8,128)S(1)} %slice.127), channel_id=1, source_target_pairs={{0,3},{1,2},{2,1},{3,0},{4,7},{5,6},{6,5},{7,4},{8,11},{9,10},{10,... | collective-permute-start | bytes 18440 | tf_op jit(solution)/shard_map/ppermute | solution.py:26
  154.2 5.2 %collective-permute-start.56 = (f32[96,16]{1,0:T(8,128)S(1)}, f32[96,16]{1,0:T(8,128)S(1)}, u32[]{:S(2)}, u32[]{:S(2)}) collective-permute-start(f32[96,16]{1,0:T(8,128)S(1)} %slice.127), channel_id=1, source_target_pairs={{0,2},{1,3},{2,0},{3,1},{4,6},{5,7},{6,4},{7,5},{8,10},{9,11},{10,... | collective-permute-start | bytes 18440 | tf_op jit(solution)/shard_map/ppermute | solution.py:26
  154.3 5.1 %collective-permute-start.55 = (f32[96,16]{1,0:T(8,128)S(1)}, f32[96,16]{1,0:T(8,128)S(1)}, u32[]{:S(2)}, u32[]{:S(2)}) collective-permute-start(f32[96,16]{1,0:T(8,128)S(1)} %slice.127), channel_id=1, source_target_pairs={{0,1},{1,0},{2,3},{3,2},{4,5},{5,4},{6,7},{7,6},{8,9},{9,8},{10,11... | collective-permute-start | bytes 18440 | tf_op jit(solution)/shard_map/ppermute | solution.py:26
  (61 other events, 264.8 us)

commit v4 on v3

--- a/solution.py
+++ b/solution.py
@@ -165,32 +165,38 @@
     return evens
 
 
-def put_grad(grad, s, scratch, keep_ref, send_ref, me, rows):
+def put_grad(grad, s, scratch, low_ref, high_ref, send_ref, me, rows):
     if rows % 16:
-        keep_ref[...] = grad
+        low_ref[...] = grad
         return
     scratch[...] = grad
+    half = low_ref.shape[0]
     for n, k in enumerate(relative_evens(s)):
-        for k_of, ref in ((k, keep_ref), (k ^ 1, send_ref)):
+        keep_ref, at = (low_ref, n) if n < half else (high_ref, n - half)
+        for k_of, ref, slot in ((k, keep_ref, at), (k ^ 1, send_ref, n)):
             start = pl.multiple_of(jnp.bitwise_xor(me, k_of) * rows, 16)
-            ref[n] = scratch[pl.ds(start, rows), :].astype(ref.dtype)
+            ref[slot] = scratch[pl.ds(start, rows), :].astype(ref.dtype)
 
 
 def grad_shapes(width, rows, cols):
     if rows % 16:
-        return [((width, cols), F32), ((8, 128), BF16)] * 2
+        return [((width, cols), F32), ((8, 128), BF16), ((8, 128), BF16)]
     half = width // rows // 2
-    return [((half, rows, cols), BF16)] * 4
-
-
-def scatter_core(keep, send, s, rows):
+    return [((half // 2, rows, cols), BF16)] * 2 + [((half, rows, cols), BF16)]
+
+
+def scatter_core(low, high, send, s, rows):
     if rows % 16:
         me = lax.axis_index("dp")
-        blocks = keep.reshape(-1, rows, keep.shape[-1])
+        blocks = low.reshape(-1, rows, low.shape[-1])
         evens = jnp.array(relative_evens(s))
+        send = jnp.take(blocks, me ^ evens ^ 1, axis=0).astype(BF16)
         keep = jnp.take(blocks, me ^ evens, axis=0)
-        send = jnp.take(blocks, me ^ evens ^ 1, axis=0).astype(BF16)
-    return keep.astype(F32) + swap(send, "dp", 1).astype(F32)
+        low, high = keep[: len(evens) // 2], keep[len(evens) // 2 :]
+    half = low.shape[0]
+    came = swap(send, "dp", 1)
+    stays = low.astype(F32) + came[:half].astype(F32)
+    return stays, (high.astype(F32) + came[half:].astype(F32)).astype(BF16)
 
 
 def scatter_split(now):
@@ -318,11 +324,12 @@
     m_ref[...] = (normed * vec_ref[5:6, :] + vec_ref[6:7, :]).astype(BF16)
 
 
-def feed_body(plan, n_arrays, hidden, *refs):
+def feed_body(plan, n_arrays, hidden, block_rows, *refs):
     ids, m_own, m_other, dy_own, dy_other, vec = refs[:6]
     pieces = refs[6 : 6 + n_arrays]
-    act_out, dpre_out = refs[6 + n_arrays : 8 + n_arrays], refs[8 + n_arrays : 10 + n_arrays]
-    m_out, dy_out, dm_keep, dm_send, br_keep, br_send, sum_out, w, sems = refs[10 + n_arrays :]
+    outs = refs[6 + n_arrays :]
+    low_g, high_g, send_g, act_out, dpre_out = outs[:5]
+    m_out, dy_out, dm_keep, dm_send, br_keep, br_send, sum_out, w, scratch, sems = outs[5:]
     copies = place_pieces(pieces, plan, (w.at[0], w.at[1]), sems, ids[0])
     rows = m_own.shape[0]
     m_out[:rows] = m_own[...]
@@ -340,11 +347,13 @@
         pre = dot(m, w_fc) + bias
         act, slope = gelu_parts(pre)
         act_low = act.astype(BF16)
-        act_out[s][...] = act_low
+        if s == 0:
+            act_out[...] = act_low
         d_pre = dot(dy, w_proj) * slope
         sum_out[s : s + 1, :] = column_sum(d_pre)
         d_pre_low = d_pre.astype(BF16)
-        dpre_out[s][...] = d_pre_low
+        if s == 0:
+            dpre_out[...] = d_pre_low
         one, two = dot(d_pre_low, w_fc, NT), dot(act_low, w_proj, NT)
         d_m = one if d_m is None else d_m + one
         branch = two if branch is None else branch + two
@@ -352,13 +361,15 @@
     dm_send[...] = d_m[rows:].astype(BF16)
     br_keep[...] = branch[:rows]
     br_send[...] = branch[rows:].astype(BF16)
-
-
-def feed_grad_body(block_rows, s, ids, m_ref, dy_ref, act_ref, dpre_ref, keep, send, scratch):
+    grad = jnp.concatenate([dot(m, d_pre_low, TN), dot(dy, act_low, TN)], axis=1)
+    put_grad(grad, 1, scratch, low_g, high_g, send_g, ids[0], block_rows)
+
+
+def feed_grad_body(block_rows, s, ids, m_ref, dy_ref, act_ref, dpre_ref, low, high, send, scratch):
     grad = jnp.concatenate(
         [dot(m_ref[...], dpre_ref[...], TN), dot(dy_ref[...], act_ref[...], TN)], axis=1
     )
-    put_grad(grad, s, scratch, keep, send, ids[0], block_rows)
+    put_grad(grad, s, scratch, low, high, send, ids[0], block_rows)
 
 
 def norm_second_back_body(resid_ref, keep_ref, recv_ref, grad_ref, vec_ref, grad1_ref, dz_ref, sum_ref):
@@ -377,9 +388,9 @@
     last = s == 0
     if last:
         da_before, xh_own, xh_other, heads_other, second, fc_sum, bp_sum = refs[8:15]
-        keep_g, send_g, keep, send, total, normed, table, dz, scratch = refs[15:]
+        low_g, high_g, send_g, keep, send, total, normed, table, dz, scratch = refs[15:]
     else:
-        keep_g, send_g, heads_out, da_out, dz, scratch = refs[8:]
+        low_g, high_g, send_g, heads_out, da_out, dz, scratch = refs[8:]
     role = ids[1]
     rows = own.shape[0]
     seq = 2 * rows
@@ -415,7 +426,7 @@
     if not last:
         heads_out[...] = heads_own
         da_out[...] = d_a
-        put_grad(jnp.concatenate(grads, axis=1), s, scratch, keep_g, send_g, ids[0], block_rows)
+        put_grad(jnp.concatenate(grads, axis=1), s, scratch, low_g, high_g, send_g, ids[0], block_rows)
         return
     d_a = d_a + da_before[...]
     total[...] = d_a
@@ -445,7 +456,7 @@
     for t in range(n_z):
         table[8 + t : 9 + t, :] = placed(fc_sum[0:1, :], fc_sum[1:2, :], t)
     grads.append(table[...].T)
-    put_grad(jnp.concatenate(grads, axis=1), s, scratch, keep_g, send_g, ids[0], block_rows)
+    put_grad(jnp.concatenate(grads, axis=1), s, scratch, low_g, high_g, send_g, ids[0], block_rows)
 
 
 def norm_first_back_body(x_ref, keep_ref, recv_ref, grad1_ref, vec_ref, out_ref):
@@ -536,34 +547,38 @@
     pieces_b, m_other, dy_other = tied(pieces_b, m_other, dy_other)
     pieces_b = gather_stage(pieces_b, stages - 1)
     arrays_b, plan_b = piece_plan(pieces_b)
-    act_0, act_1, d_pre_0, d_pre_1, m_both, dy_both, dm_keep, dm_send, br_keep, br_send, fc_sum = call(
-        lambda *refs: feed_body(plan_b, len(arrays_b), hidden, *refs),
+    *parts_1, act_0, d_pre_0, m_both, dy_both, dm_keep, dm_send, br_keep, br_send, fc_sum = call(
+        lambda *refs: feed_body(plan_b, len(arrays_b), hidden, block_rows, *refs),
         "feed",
         7,
-        [((seq, hidden), BF16)] * 4
+        grad_shapes(width, block_rows, 2 * hidden)
+        + [((seq, hidden), BF16)] * 2
         + [(both, BF16), (both, BF16), (row, F32), (row, BF16), (row, F32), (row, BF16), ((2, hidden), F32)],
         (ids, m, m_other, dy, dy_other, vec, *arrays_b),
-        [pltpu.VMEM((2, width, 2 * hidden), BF16), pltpu.SemaphoreType.DMA((len(plan_b),))],
+        [
+            pltpu.VMEM((2, width, 2 * hidden), BF16),
+            pltpu.VMEM((width, 2 * hidden), F32),
+            pltpu.SemaphoreType.DMA((len(plan_b),)),
+        ],
         any_space(6, arrays_b),
     )
     dm_recv = swap(dm_send, "tensor", 1)
 
-    def feed_grad(s, act, d_pre):
-        return call(
-            lambda *refs: feed_grad_body(block_rows, s, *refs),
-            "feed_grad_" + str(s),
-            3,
-            grad_shapes(width, block_rows, 2 * hidden)[:2],
-            (ids, m_both, dy_both, act, d_pre),
-            [pltpu.VMEM((width, 2 * hidden), F32)],
-            smem,
-        )
-
-    parts_1 = feed_grad(1, act_1, d_pre_1)
-    split_b1 = scatter_split(scatter_core(*parts_1, 1, block_rows))
-    parts_0 = feed_grad(0, act_0, d_pre_0)
-    dm_recv, *flat = together(dm_recv, *parts_0, *split_b1)
-    parts_0, split_b1 = flat[:2], flat[2:]
+    split_b1 = scatter_core(*parts_1, 1, block_rows)
+    parts_0 = call(
+        lambda *refs: feed_grad_body(block_rows, 0, *refs),
+        "feed_grad",
+        3,
+        grad_shapes(width, block_rows, 2 * hidden),
+        (ids, m_both, dy_both, act_0, d_pre_0),
+        [pltpu.VMEM((width, 2 * hidden), F32)],
+        smem,
+    )
+    *parts_0, stays, goes = together(*parts_0, *split_b1)
+    split_b1 = [stays, goes]
+    br_recv = swap(br_send, "tensor", 1)
+    dm_recv, *parts_0 = together(dm_recv, *parts_0)
+    split_b0 = scatter_core(*parts_0, 0, block_rows)
     br_recv = swap(br_send, "tensor", 1)
     grad1, dz, second_sums = call(
         norm_second_back_body,
@@ -572,35 +587,33 @@
         [(row, F32), (row, BF16), ((3, width), F32)],
         (resid1, dm_keep, dm_recv, out_grad, vec),
     )
-    split_b0 = scatter_split(scatter_core(*parts_0, 0, block_rows))
-    dz, br_recv, *split_b0 = together(dz, br_recv, *split_b0)
+    dz, *split_b0 = together(dz, *split_b0)
     dz_other = swap(dz, "tensor", 1)
     split_b = [split_b0, split_b1]
-    outputs = resid1 + (br_keep + br_recv.astype(F32)) + vec[7]
-
     def attend_back(s, w, qkv, ctx, more_args, more_outs, more_scratch):
         cols = 4 * head_cols + 128 * (1 - s)
         return call(
             lambda *refs: attend_back_body(block_rows, head_cols, s, *refs),
             "attend_back_" + str(s),
             6,
-            grad_shapes(width, block_rows, cols)[:2] + more_outs,
+            grad_shapes(width, block_rows, cols) + more_outs,
             (ids, dz, dz_other, w, qkv, lse, a_seq, ctx, *more_args),
             more_scratch + [pltpu.VMEM(both, BF16), pltpu.VMEM((width, cols), F32)],
             smem,
         )
 
     halvings = stages - 1
-    keep_1, send_1, head_sums_1, da_1 = attend_back(
+    *parts_1, head_sums_1, da_1 = attend_back(
         1, w_1, qkv_1, ctx_1, (), [((1, 3 * head_cols), F32), (both, F32)], []
     )
     halvings = stages - 1
     split_b = [scatter_split(scatter_step(*split_b[s], s, 0)) for s in range(2)]
-    da_1, *flat = together(da_1, *split_b[0], *split_b[1])
+    da_1, br_recv, *flat = together(da_1, br_recv, *split_b[0], *split_b[1])
+    outputs = resid1 + (br_keep + br_recv.astype(F32)) + vec[7]
     split_b = [flat[:2], flat[2:]]
-    split_1 = scatter_split(scatter_core(keep_1, send_1, 1, block_rows))
+    split_1 = scatter_core(*parts_1, 1, block_rows)
     da_1, *split_1 = together(da_1, *split_1)
-    keep_0, send_0, da_keep, da_send = attend_back(
+    *parts_0, da_keep, da_send = attend_back(
         0,
         w_0,
         qkv_0,
@@ -613,7 +626,7 @@
     b_other = scatter_on(*b_other, 1, 1, halvings)
     now_1 = scatter_step(*split_1, 1, 0)
     split_1 = scatter_split(now_1)
-    split_0 = scatter_split(scatter_core(keep_0, send_0, 0, block_rows))
+    split_0 = scatter_core(*parts_0, 0, block_rows)
     da_send, b_other, *flat = together(da_send, b_other, *split_1, *b_own)
     split_1, b_own = flat[:2], flat[2:]
     da_recv = swap(da_send, "tensor", 1)

time: 161 us -> 156 us (0.969)
  local copies, waits for them, and re-layouts: 15 us -> 11.6 us
  Pallas kernels: 44.1 us -> 41.6 us
    pallas_call x11 -> x10, Pallas kernels: 44.1 us -> 41.6 us  [call(): pl.pallas_call(body, name=name, out_shape=[jax.ShapeDtypeStruct(shape, dt...]
    unnamed x128, local copies, waits for them, and re-layouts: 11.8 us -> 9.42 us
  transfers between devices with their start and end apart: 58 -> 58, of which waited for: 29 -> 30; matrix products, arithmetic and copies ran while one was open for 8% -> 8% of each run, Pallas kernels for 21% -> 21%
where the time goes in v4:
time: 156 us
  starting transfers between devices  49.2 us (32%)
  waiting for transfers between devices  45.2 us (29%)
  Pallas kernels  41.6 us (27%)
  local copies, waits for them, and re-layouts  11.6 us (7%)
  other arithmetic  6.55 us (4%)
    ppermute x58, starting transfers between devices, swap(): return lax.ppermute(value, axis, [(i, i ^ bits) for i in range(size)])  49.2 us
    ppermute x58, waiting for transfers between devices, swap(): return lax.ppermute(value, axis, [(i, i ^ bits) for i in range(size)])  45.2 us
    pallas_call x10, Pallas kernels, call(): pl.pallas_call(body, name=name, out_shape=[jax.ShapeDtypeStruct(shape, dt...  41.6 us
    unnamed x128, local copies, waits for them, and re-layouts  9.42 us
  transfers between devices with their start and end apart: 58, of which 30 were waited for; matrix products, arithmetic and copies ran while one was open for 8% of the time, Pallas kernels for 21%

profile of v4, /device:TPU:0, one launch (start us, length us, event | category | flops | bytes accessed | tf_op | source)
XLA Modules:
  0.0 155.6 jit_solution(10994756177850910785)
XLA Ops:
  0.6 0.8 copy.23
  1.4 3.0 %collective-permute-start.1 = (f32[24,12]{1,0:T(8,128)S(1)}, f32[24,12]{1,0:T(8,128)S(1)}, u32[]{:S(2)}, u32[]{:S(2)}) collective-permute-start(f32[24,12]{1,0:T(8,128)S(1)} %bitcast.57), channel_id=1, source_target_pairs={{0,1},{1,0},{2,3},{3,2},{4,5},{5,4},{6,7},{7,6},{8,9},{9,8},{10,11... | collective-permute-start | bytes 3464 | tf_op jit(solution)/shard_map/ppermute | solution.py:26
  4.4 2.6 %collective-permute-start.2 = (f32[24,12]{1,0:T(8,128)S(1)}, f32[24,12]{1,0:T(8,128)S(1)}, u32[]{:S(2)}, u32[]{:S(2)}) collective-permute-start(f32[24,12]{1,0:T(8,128)S(1)} %bitcast.58), channel_id=1, source_target_pairs={{0,2},{1,3},{2,0},{3,1},{4,6},{5,7},{6,4},{7,5},{8,10},{9,11},{10,... | collective-permute-start | bytes 3464 | tf_op jit(solution)/shard_map/ppermute | solution.py:26
  7.0 0.9 copy.21
  7.9 1.1 copy.20
  9.2 2.0 %collective-permute-start = (bf16[1,96,768]{2,1,0:T(8,128)(2,1)S(1)}, bf16[1,96,768]{2,1,0:T(8,128)(2,1)S(1)}, u32[]{:S(2)}, u32[]{:S(2)}) collective-permute-start(bf16[1,96,768]{2,1,0:T(8,128)(2,1)S(1)} %maximum_bitcast_fusion), channel_id=1, source_target_pairs={{0,2},{1,3},{2,0},{3,1},{4,6},{5,7},{6,4},{7,5},{8,10},{9,11},{10,... | collective-permute-start | bytes 442376 | tf_op jit(solution)/shard_map/ppermute | solution.py:26
  11.2 1.0 pad_maximum_fusion
  12.8 2.0 %norm_first.1 = (bf16[128,768]{1,0:T(8,128)(2,1)}, bf16[128,768]{1,0:T(8,128)(2,1)}, f32[1,768]{1,0:T(1,128)}) custom-call(f32[128,768]{1,0:T(8,128)} %x_ref.5, f32[128,768]{1,0:T(8,128)} %grad_ref.1), custom_call_target="tpu_custom_call" | custom-call | flops 100000000 | bytes 200000 | tf_op jit(solution)/shard_map/norm_first/pallas_call | solution.py:69
  16.1 1.6 %table.1 = bf16[96,128]{1,0:T(8,128)(2,1)} custom-call(s32[3]{0:T(128)} %pad_add_fusion.ids.refs_0_, f32[24,12]{1,0:T(8,128)} %bitcast.60, f32[24,12]{1,0:T(8,128)} %copy-done.58, f32[24,12]{1,0:T(8,128)} %copy-done.59, f32[24,12]{1,0:T(8,128)} %copy-done.60), custom_call_target="tpu_custom_call" | custom-call | flops 50000000 | bytes 100000 | tf_op jit(solution)/shard_map/table/pallas_call | solution.py:69
  17.7 0.8 collective-permute-done.refs_11_
  18.5 1.7 %collective-permute-start.6 = (bf16[128,768]{1,0:T(8,128)(2,1)}, bf16[128,768]{1,0:T(8,128)(2,1)S(1)}, u32[]{:S(2)}, u32[]{:S(2)}) collective-permute-start(bf16[128,768]{1,0:T(8,128)(2,1)} %get-tuple-element.120.refs_1_.refs_9_), channel_id=1, source_target_pairs={{0,1},{1,0},{2,3},{3,2},{4,5},{5,4},{6,7},{7,6},{8,9},{9,8},{10,11... | collective-permute-start | bytes 589832 | tf_op jit(solution)/shard_map/ppermute | solution.py:26
  20.2 0.8 pad_maximum_fusion.1.refs_3_
  21.0 1.6 collective-permute-start.4
  22.5 1.5 collective-permute-start.5
  24.0 1.3 collective-permute-start.11
  25.3 2.3 %collective-permute-done.5.refs_12_ = bf16[1,96,768]{2,1,0:T(8,128)(2,1)S(1)} collective-permute-done((bf16[1,96,768]{2,1,0:T(8,128)(2,1)S(1)}, bf16[1,96,768]{2,1,0:T(8,128)(2,1)S(1)}, u32[]{:S(2)}, u32[]{:S(2)}) %collective-permute-start.5) | collective-permute-done | bytes 147488 | tf_op jit(solution)/shard_map/ppermute | solution.py:26
  27.7 1.6 %collective-permute-start.7 = (bf16[1,96,896]{2,1,0:T(8,128)(2,1)S(1)}, bf16[1,96,896]{2,1,0:T(8,128)(2,1)S(1)}, u32[]{:S(2)}, u32[]{:S(2)}) collective-permute-start(bf16[1,96,896]{2,1,0:T(8,128)(2,1)S(1)} %pad_maximum_fusion.1.refs_3_), channel_id=1, source_target_pairs={{0,16},{4,20},{8,24},{12,28},{16,0},{20,4},{24,8},{28,12},{1,17},{... | collective-permute-start | bytes 516104 | tf_op jit(solution)/shard_map/ppermute | solution.py:26
  30.3 1.5 collective-permute-start.10
  31.8 6.2 %collective-permute-done.11.refs_14_ = bf16[1,96,1536]{2,1,0:T(8,128)(2,1)S(1)} collective-permute-done((bf16[1,96,1536]{2,1,0:T(8,128)(2,1)S(1)}, bf16[1,96,1536]{2,1,0:T(8,128)(2,1)S(1)}, u32[]{:S(2)}, u32[]{:S(2)}) %collective-permute-start.11) | collective-permute-done | bytes 294944 | tf_op jit(solution)/shard_map/ppermute | solution.py:26
  41.3 0.8 collective-permute-done.13.refs_8_
  43.6 6.8 %attend.1 = (bf16[768,896]{1,0:T(8,128)(2,1)}, bf16[768,768]{1,0:T(8,128)(2,1)}, bf16[256,576]{1,0:T(8,128)(2,1)}, bf16[256,576]{1,0:T(8,128)(2,1)}, bf16[256,19...) custom-call(s32[3]{0:T(128)} %pad_add_fusion.ids.refs_0_, ...), custom_call_target="tpu_custom_call" | custom-call | flops 300000000 | bytes 600000 | tf_op jit(solution)/shard_map/attend/pallas_call | solution.py:69
  50.6 2.0 %collective-permute-start.28 = (bf16[128,768]{1,0:T(8,128)(2,1)S(1)}, bf16[128,768]{1,0:T(8,128)(2,1)S(1)}, u32[]{:S(2)}, u32[]{:S(2)}) collective-permute-start(bf16[128,768]{1,0:T(8,128)(2,1)S(1)} %copy-done.33), channel_id=1, source_target_pairs={{0,1},{1,0},{2,3},{3,2},{4,5},{5,4},{6,7},{7,6},{8,9},{9,8},{10,11... | collective-permute-start | bytes 589832 | tf_op jit(solution)/shard_map/ppermute | solution.py:26
  52.6 1.5 collective-permute-start.23
  54.6 1.4 collective-permute-start.25
  56.1 2.4 %collective-permute-done.22.recv_ref = bf16[128,768]{1,0:T(8,128)(2,1)S(1)} collective-permute-done((bf16[128,768]{1,0:T(8,128)(2,1)}, bf16[128,768]{1,0:T(8,128)(2,1)S(1)}, u32[]{:S(2)}, u32[]{:S(2)}) %collective-permute-start.22) | collective-permute-done | bytes 196640 | tf_op jit(solution)/shard_map/ppermute | solution.py:26
  58.5 1.4 collective-permute-start.26
  60.0 2.1 %norm_second.1 = (f32[128,768]{1,0:T(8,128)}, bf16[128,768]{1,0:T(8,128)(2,1)}) custom-call(f32[128,768]{1,0:T(8,128)} %x_ref.5, f32[128,768]{1,0:T(8,128)} %get-tuple-element.138.keep_ref, bf16[128,768]{1,0:T(8,128)(2,1)} %copy-done.38, f32[16,768]{1,0:T(8,128)} %get-tuple-element.143.vec_ref.refs_5_), custom_call_target="tpu_custom_call" | custom-call | flops 100000000 | bytes 200000 | tf_op jit(solution)/shard_map/norm_second/pallas_call | solution.py:69
  62.5 5.0 %collective-permute-done.24.refs_9_ = bf16[1,96,1536]{2,1,0:T(8,128)(2,1)S(1)} collective-permute-done((bf16[1,96,1536]{2,1,0:T(8,128)(2,1)S(1)}, bf16[1,96,1536]{2,1,0:T(8,128)(2,1)S(1)}, u32[]{:S(2)}, u32[]{:S(2)}) %collective-permute-start.24) | collective-permute-done | bytes 294944 | tf_op jit(solution)/shard_map/ppermute | solution.py:26
  67.6 1.5 collective-permute-done.26.refs_17_
  73.9 0.7 copy-done.30
  74.6 8.5 %feed.1 = (bf16[2,96,1536]{2,1,0:T(8,128)(2,1)}, bf16[2,96,1536]{2,1,0:T(8,128)(2,1)}, bf16[4,96,1536]{2,1,0:T(8,128)(2,1)}, bf16[256,768]{1,0:T(8,128)(2,1)}, b...) custom-call(s32[3]{0:T(128)} %pad_add_fusion.ids.refs_0_, ...), custom_call_target="tpu_custom_call" | custom-call | flops 350000000 | bytes 700000 | tf_op jit(solution)/shard_map/feed/pallas_call | solution.py:69
  83.7 3.7 %feed_grad.1 = (bf16[2,96,1536]{2,1,0:T(8,128)(2,1)}, bf16[2,96,1536]{2,1,0:T(8,128)(2,1)}, bf16[4,96,1536]{2,1,0:T(8,128)(2,1)}) custom-call(s32[3]{0:T(128)} %pad_add_fusion.ids.refs_0_, bf16[256,768]{1,0:T(8,128)(2,1)} %get-tuple-element.164.refs_1_, bf16[256,768]{1,0:T(8,128)(2,1)} %get-tuple-element.165.refs_2_, ...), custom_call_target="tpu_custom_call" | custom-call | flops 150000000 | bytes 300000 | tf_op jit(solution)/shard_map/feed_grad/pallas_call | solution.py:69
  87.7 3.0 %collective-permute-done.37.recv_ref = bf16[128,768]{1,0:T(8,128)(2,1)S(1)} collective-permute-done((bf16[128,768]{1,0:T(8,128)(2,1)}, bf16[128,768]{1,0:T(8,128)(2,1)S(1)}, u32[]{:S(2)}, u32[]{:S(2)}) %collective-permute-start.37) | collective-permute-done | bytes 196640 | tf_op jit(solution)/shard_map/ppermute | solution.py:26
  90.8 1.5 collective-permute-start.43
  92.3 2.4 %norm_second_back.1 = (f32[128,768]{1,0:T(8,128)}, bf16[128,768]{1,0:T(8,128)(2,1)}, f32[3,768]{1,0:T(4,128)}) custom-call(f32[128,768]{1,0:T(8,128)} %get-tuple-element.144.resid_ref, f32[128,768]{1,0:T(8,128)} %get-tuple-element.162.keep_ref, bf16[128,768]{1,0:T(8,128)(2,1)} %copy-done.37, f32[128,768]{1,0:T(8,128)} %grad_ref.1, ...), custom_call_target="tpu_custom_call" | custom-call | flops 100000000 | bytes 200000 | tf_op jit(solution)/shard_map/norm_second_back/pallas_call | solution.py:69
  94.8 1.1 add_convert_fusion
  96.2 1.5 collective-permute-start.42
  97.7 0.8 slice_reduce_fusion
  98.5 1.7 %collective-permute-start.41 = (bf16[128,768]{1,0:T(8,128)(2,1)S(1)}, bf16[128,768]{1,0:T(8,128)(2,1)S(1)}, u32[]{:S(2)}, u32[]{:S(2)}) collective-permute-start(bf16[128,768]{1,0:T(8,128)(2,1)S(1)} %copy-done.56), channel_id=1, source_target_pairs={{0,1},{1,0},{2,3},{3,2},{4,5},{5,4},{6,7},{7,6},{8,9},{9,8},{10,11... | collective-permute-start | bytes 589832 | tf_op jit(solution)/shard_map/ppermute | solution.py:26
  100.2 3.4 %collective-permute-done.40.refs_2_ = bf16[128,768]{1,0:T(8,128)(2,1)S(1)} collective-permute-done((bf16[128,768]{1,0:T(8,128)(2,1)S(1)}, bf16[128,768]{1,0:T(8,128)(2,1)S(1)}, u32[]{:S(2)}, u32[]{:S(2)}) %collective-permute-start.40) | collective-permute-done | bytes 196640 | tf_op jit(solution)/shard_map/ppermute | solution.py:26
  103.6 0.7 copy-done.7
  104.3 5.7 %attend_back_1.1 = (bf16[2,96,768]{2,1,0:T(8,128)(2,1)}, bf16[2,96,768]{2,1,0:T(8,128)(2,1)}, bf16[4,96,768]{2,1,0:T(8,128)(2,1)}, f32[1,576]{1,0:T(1,128)}, f32[256,768]{1,0:T(8,128)}) custom-call(s32[3]{0:T(128)} %pad_add_fusion.ids.refs_0_, bf16[128,768]{1,0:T(8,128)(2,1)} %get-tuple-element.182.refs_1_, bf16[128,768]{1,0:T(8,128)(2,1)} %copy-done.7, ...), custom_call_target="tpu_custom_call" | custom-call | flops 300000000 | bytes 600000 | tf_op jit(solution)/shard_map/attend_back_1/pallas_call | solution.py:69
  109.9 1.2 convert_add_fusion
  112.3 1.6 %collective-permute-start.45 = (bf16[1,96,1536]{2,1,0:T(8,128)(2,1)S(1)}, bf16[1,96,1536]{2,1,0:T(8,128)(2,1)S(1)}, u32[]{:S(2)}, u32[]{:S(2)}) collective-permute-start(bf16[1,96,1536]{2,1,0:T(8,128)(2,1)S(1)} %slice.146), channel_id=1, source_target_pairs={{0,16},{4,20},{8,24},{12,28},{16,0},{20,4},{24,8},{28,12},{1,17},{... | collective-permute-start | bytes 884744 | tf_op jit(solution)/shard_map/ppermute | solution.py:26
  114.7 6.3 %attend_back_0.1 = (bf16[2,96,896]{2,1,0:T(8,128)(2,1)}, bf16[2,96,896]{2,1,0:T(8,128)(2,1)}, bf16[4,96,896]{2,1,0:T(8,128)(2,1)}, f32[128,768]{1,0:T(8,128)}, bf16[128,768]{1,0:T(8,128)(2,1)}) custom-call(s32[3]{0:T(128)} %pad_add_fusion.ids.refs_0_, bf16[128,768]{1,0:T(8,128)(2,1)} %get-tuple-element.182.refs_1_, bf16[128,768]{1,0:T(8,128)(2,1)} %copy-done.7, ...), custom_call_target="tpu_custom_call" | custom-call | flops 300000000 | bytes 600000 | tf_op jit(solution)/shard_map/attend_back_0/pallas_call | solution.py:69
  121.0 0.7 collective-permute-done.45
  121.8 1.5 collective-permute-done.46
  123.4 1.6 %collective-permute-start.52 = (bf16[1,96,768]{2,1,0:T(8,128)(2,1)S(1)}, bf16[1,96,768]{2,1,0:T(8,128)(2,1)S(1)}, u32[]{:S(2)}, u32[]{:S(2)}) collective-permute-start(bf16[1,96,768]{2,1,0:T(8,128)(2,1)S(1)} %slice.149), channel_id=1, source_target_pairs={{0,16},{4,20},{8,24},{12,28},{16,0},{20,4},{24,8},{28,12},{1,17},{... | collective-permute-start | bytes 442376 | tf_op jit(solution)/shard_map/ppermute | solution.py:26
  125.0 0.8 add_add_fusion
  125.8 0.9 collective-permute-start.47
  127.3 1.7 %collective-permute-start.49 = (bf16[128,768]{1,0:T(8,128)(2,1)S(1)}, bf16[128,768]{1,0:T(8,128)(2,1)S(1)}, u32[]{:S(2)}, u32[]{:S(2)}) collective-permute-start(bf16[128,768]{1,0:T(8,128)(2,1)S(1)} %copy-done.57), channel_id=1, source_target_pairs={{0,1},{1,0},{2,3},{3,2},{4,5},{5,4},{6,7},{7,6},{8,9},{9,8},{10,11... | collective-permute-start | bytes 589832 | tf_op jit(solution)/shard_map/ppermute | solution.py:26
  129.2 1.5 collective-permute-start.51
  130.7 3.6 %collective-permute-done.48 = bf16[1,96,1536]{2,1,0:T(8,128)(2,1)S(1)} collective-permute-done((bf16[1,96,1536]{2,1,0:T(8,128)(2,1)S(1)}, bf16[1,96,1536]{2,1,0:T(8,128)(2,1)S(1)}, u32[]{:S(2)}, u32[]{:S(2)}) %collective-permute-start.48) | collective-permute-done | bytes 294944 | tf_op jit(solution)/shard_map/ppermute | solution.py:26
  134.3 3.5 %collective-permute-done.51 = bf16[2,96,896]{2,1,0:T(8,128)(2,1)S(1)} collective-permute-done((bf16[2,96,896]{2,1,0:T(8,128)(2,1)S(1)}, bf16[2,96,896]{2,1,0:T(8,128)(2,1)S(1)}, u32[]{:S(2)}, u32[]{:S(2)}) %collective-permute-start.51) | collective-permute-done | bytes 344096 | tf_op jit(solution)/shard_map/ppermute | solution.py:26
  138.0 2.8 %collective-permute-done.47 = bf16[96,1536]{1,0:T(8,128)(2,1)S(1)} collective-permute-done((bf16[96,1536]{1,0:T(8,128)(2,1)S(1)}, bf16[96,1536]{1,0:T(8,128)(2,1)S(1)}, u32[]{:S(2)}, u32[]{:S(2)}) %collective-permute-start.47) | collective-permute-done | bytes 294944 | tf_op jit(solution)/shard_map/ppermute | solution.py:26
  140.7 1.1 collective-permute-start.53
  141.9 2.4 %norm_first_back.1 = f32[128,768]{1,0:T(8,128)} custom-call(f32[128,768]{1,0:T(8,128)} %x_ref.5, f32[128,768]{1,0:T(8,128)} %get-tuple-element.207.keep_ref, bf16[128,768]{1,0:T(8,128)(2,1)} %copy-done.36, f32[128,768]{1,0:T(8,128)} %get-tuple-element.225.grad1_ref, f32[16,768]{1,0:T(8,128)} %get-tuple-element.143.vec_ref.refs_5_), custom_call_target="tpu_custom_call" | custom-call | flops 100000000 | bytes 200000 | tf_op jit(solution)/shard_map/norm_first_back/pallas_call | solution.py:69
  144.3 0.8 slice_bitcast_fusion
  145.2 1.9 %collective-permute-done.53 = bf16[1,96,896]{2,1,0:T(8,128)(2,1)S(1)} collective-permute-done((bf16[1,96,896]{2,1,0:T(8,128)(2,1)S(1)}, bf16[1,96,896]{2,1,0:T(8,128)(2,1)S(1)}, u32[]{:S(2)}, u32[]{:S(2)}) %collective-permute-start.53) | collective-permute-done | bytes 172064 | tf_op jit(solution)/shard_map/ppermute | solution.py:26
  147.1 2.0 %collective-permute-start.57 = (f32[96,16]{1,0:T(8,128)S(1)}, f32[96,16]{1,0:T(8,128)S(1)}, u32[]{:S(2)}, u32[]{:S(2)}) collective-permute-start(f32[96,16]{1,0:T(8,128)S(1)} %slice.123), channel_id=1, source_target_pairs={{0,3},{1,2},{2,1},{3,0},{4,7},{5,6},{6,5},{7,4},{8,11},{9,10},{10,... | collective-permute-start | bytes 18440 | tf_op jit(solution)/shard_map/ppermute | solution.py:26
  149.3 2.2 %collective-permute-start.55 = (f32[96,16]{1,0:T(8,128)S(1)}, f32[96,16]{1,0:T(8,128)S(1)}, u32[]{:S(2)}, u32[]{:S(2)}) collective-permute-start(f32[96,16]{1,0:T(8,128)S(1)} %slice.123), channel_id=1, source_target_pairs={{0,1},{1,0},{2,3},{3,2},{4,5},{5,4},{6,7},{7,6},{8,9},{9,8},{10,11... | collective-permute-start | bytes 18440 | tf_op jit(solution)/shard_map/ppermute | solution.py:26
  152.2 0.9 copy.25
  153.1 0.7 copy.26
  153.8 1.1 collective-permute-done.56
  (229 shorter events, 19.6 us)
Async XLA Ops:
  1.4 13.5 %collective-permute-start.1 = (f32[24,12]{1,0:T(8,128)S(1)}, f32[24,12]{1,0:T(8,128)S(1)}, u32[]{:S(2)}, u32[]{:S(2)}) collective-permute-start(f32[24,12]{1,0:T(8,128)S(1)} %bitcast.57), channel_id=1, source_target_pairs={{0,1},{1,0},{2,3},{3,2},{4,5},{5,4},{6,7},{7,6},{8,9},{9,8},{10,11... | collective-permute-start | bytes 3464 | tf_op jit(solution)/shard_map/ppermute | solution.py:26
  4.4 10.5 %collective-permute-start.2 = (f32[24,12]{1,0:T(8,128)S(1)}, f32[24,12]{1,0:T(8,128)S(1)}, u32[]{:S(2)}, u32[]{:S(2)}) collective-permute-start(f32[24,12]{1,0:T(8,128)S(1)} %bitcast.58), channel_id=1, source_target_pairs={{0,2},{1,3},{2,0},{3,1},{4,6},{5,7},{6,4},{7,5},{8,10},{9,11},{10,... | collective-permute-start | bytes 3464 | tf_op jit(solution)/shard_map/ppermute | solution.py:26
  7.0 7.9 %collective-permute-start.3 = (f32[24,12]{1,0:T(8,128)S(1)}, f32[24,12]{1,0:T(8,128)S(1)}, u32[]{:S(2)}, u32[]{:S(2)}) collective-permute-start(f32[24,12]{1,0:T(8,128)S(1)} %bitcast.59), channel_id=1, source_target_pairs={{0,3},{1,2},{2,1},{3,0},{4,7},{5,6},{6,5},{7,4},{8,11},{9,10},{10,... | collective-permute-start | bytes 3464 | tf_op jit(solution)/shard_map/ppermute | solution.py:26
  9.2 9.3 %collective-permute-start = (bf16[1,96,768]{2,1,0:T(8,128)(2,1)S(1)}, bf16[1,96,768]{2,1,0:T(8,128)(2,1)S(1)}, u32[]{:S(2)}, u32[]{:S(2)}) collective-permute-start(bf16[1,96,768]{2,1,0:T(8,128)(2,1)S(1)} %maximum_bitcast_fusion), channel_id=1, source_target_pairs={{0,2},{1,3},{2,0},{3,1},{4,6},{5,7},{6,4},{7,5},{8,10},{9,11},{10,... | collective-permute-start | bytes 442376 | tf_op jit(solution)/shard_map/ppermute | solution.py:26
  12.2 56.8 %copy-start.4 = (bf16[96,1536]{1,0:T(8,128)(2,1)}, bf16[96,1536]{1,0:T(8,128)(2,1)S(1)}, u32[]{:S(2)}) copy-start(bf16[96,1536]{1,0:T(8,128)(2,1)S(1)} %pad_maximum_fusion) | copy-start | bytes 884740
  18.5 24.1 %copy-start.46 = (bf16[1,96,768]{2,1,0:T(8,128)(2,1)}, bf16[1,96,768]{2,1,0:T(8,128)(2,1)S(1)}, u32[]{:S(2)}) copy-start(bf16[1,96,768]{2,1,0:T(8,128)(2,1)S(1)} %collective-permute-done.refs_11_) | copy-start | bytes 442372
  18.5 9.1 %collective-permute-start.6 = (bf16[128,768]{1,0:T(8,128)(2,1)}, bf16[128,768]{1,0:T(8,128)(2,1)S(1)}, u32[]{:S(2)}, u32[]{:S(2)}) collective-permute-start(bf16[128,768]{1,0:T(8,128)(2,1)} %get-tuple-element.120.refs_1_.refs_9_), channel_id=1, source_target_pairs={{0,1},{1,0},{2,3},{3,2},{4,5},{5,4},{6,7},{7,6},{8,9},{9,8},{10,11... | collective-permute-start | bytes 589832 | tf_op jit(solution)/shard_map/ppermute | solution.py:26
  21.0 6.7 %collective-permute-start.4 = (bf16[1,96,896]{2,1,0:T(8,128)(2,1)S(1)}, bf16[1,96,896]{2,1,0:T(8,128)(2,1)S(1)}, u32[]{:S(2)}, u32[]{:S(2)}) collective-permute-start(bf16[1,96,896]{2,1,0:T(8,128)(2,1)S(1)} %pad_maximum_fusion.1.refs_3_), channel_id=1, source_target_pairs={{0,8},{4,12},{8,0},{12,4},{16,24},{20,28},{24,16},{28,20},{1,9},{5... | collective-permute-start | bytes 516104 | tf_op jit(solution)/shard_map/ppermute | solution.py:26
  22.5 5.1 %collective-permute-start.5 = (bf16[1,96,768]{2,1,0:T(8,128)(2,1)S(1)}, bf16[1,96,768]{2,1,0:T(8,128)(2,1)S(1)}, u32[]{:S(2)}, u32[]{:S(2)}) collective-permute-start(bf16[1,96,768]{2,1,0:T(8,128)(2,1)S(1)} %collective-permute-done.refs_11_), channel_id=1, source_target_pairs={{0,16},{4,20},{8,24},{12,28},{16,0},{20,4},{24,8},{28,12},{1,17},{... | collective-permute-start | bytes 442376 | tf_op jit(solution)/shard_map/ppermute | solution.py:26
  24.0 26.6 %copy-start.33 = (bf16[128,768]{1,0:T(8,128)(2,1)S(1)}, bf16[128,768]{1,0:T(8,128)(2,1)}, u32[]{:S(2)}) copy-start(bf16[128,768]{1,0:T(8,128)(2,1)} %get-tuple-element.150.refs_3_) | copy-start | bytes 589828
  24.0 14.0 %collective-permute-start.11 = (bf16[1,96,1536]{2,1,0:T(8,128)(2,1)S(1)}, bf16[1,96,1536]{2,1,0:T(8,128)(2,1)S(1)}, u32[]{:S(2)}, u32[]{:S(2)}) collective-permute-start(bf16[1,96,1536]{2,1,0:T(8,128)(2,1)S(1)} %bitcast.45), channel_id=1, source_target_pairs={{0,2},{1,3},{2,0},{3,1},{4,6},{5,7},{6,4},{7,5},{8,10},{9,11},{10,... | collective-permute-start | bytes 884744 | tf_op jit(solution)/shard_map/ppermute | solution.py:26
  27.7 10.4 %collective-permute-start.7 = (bf16[1,96,896]{2,1,0:T(8,128)(2,1)S(1)}, bf16[1,96,896]{2,1,0:T(8,128)(2,1)S(1)}, u32[]{:S(2)}, u32[]{:S(2)}) collective-permute-start(bf16[1,96,896]{2,1,0:T(8,128)(2,1)S(1)} %pad_maximum_fusion.1.refs_3_), channel_id=1, source_target_pairs={{0,16},{4,20},{8,24},{12,28},{16,0},{20,4},{24,8},{28,12},{1,17},{... | collective-permute-start | bytes 516104 | tf_op jit(solution)/shard_map/ppermute | solution.py:26
  29.3 8.8 %collective-permute-start.8 = (bf16[1,96,896]{2,1,0:T(8,128)(2,1)S(1)}, bf16[1,96,896]{2,1,0:T(8,128)(2,1)S(1)}, u32[]{:S(2)}, u32[]{:S(2)}) collective-permute-start(bf16[1,96,896]{2,1,0:T(8,128)(2,1)S(1)} %collective-permute-done.4.refs_4_), channel_id=1, source_target_pairs={{0,16},{4,20},{8,24},{12,28},{16,0},{20,4},{24,8},{28,12},{1,17},{... | collective-permute-start | bytes 516104 | tf_op jit(solution)/shard_map/ppermute | solution.py:26
  29.8 8.3 %collective-permute-start.9 = (bf16[1,96,768]{2,1,0:T(8,128)(2,1)S(1)}, bf16[1,96,768]{2,1,0:T(8,128)(2,1)S(1)}, u32[]{:S(2)}, u32[]{:S(2)}) collective-permute-start(bf16[1,96,768]{2,1,0:T(8,128)(2,1)S(1)} %collective-permute-done.refs_11_), channel_id=1, source_target_pairs={{0,8},{4,12},{8,0},{12,4},{16,24},{20,28},{24,16},{28,20},{1,9},{5... | collective-permute-start | bytes 442376 | tf_op jit(solution)/shard_map/ppermute | solution.py:26
  30.3 7.7 %collective-permute-start.10 = (bf16[1,96,768]{2,1,0:T(8,128)(2,1)S(1)}, bf16[1,96,768]{2,1,0:T(8,128)(2,1)S(1)}, u32[]{:S(2)}, u32[]{:S(2)}) collective-permute-start(bf16[1,96,768]{2,1,0:T(8,128)(2,1)S(1)} %collective-permute-done.5.refs_12_), channel_id=1, source_target_pairs={{0,8},{4,12},{8,0},{12,4},{16,24},{20,28},{24,16},{28,20},{1,9},{5... | collective-permute-start | bytes 442376 | tf_op jit(solution)/shard_map/ppermute | solution.py:26
  38.0 32.1 %copy-start.16 = (bf16[1,96,1536]{2,1,0:T(8,128)(2,1)}, bf16[1,96,1536]{2,1,0:T(8,128)(2,1)S(1)}, u32[]{:S(2)}) copy-start(bf16[1,96,1536]{2,1,0:T(8,128)(2,1)S(1)} %collective-permute-done.11.refs_14_) | copy-start | bytes 884740
  38.1 1.4 collective-permute-start.16
  38.2 1.9 %collective-permute-start.17 = (bf16[1,96,768]{2,1,0:T(8,128)(2,1)S(1)}, bf16[1,96,768]{2,1,0:T(8,128)(2,1)S(1)}, u32[]{:S(2)}, u32[]{:S(2)}) collective-permute-start(bf16[1,96,768]{2,1,0:T(8,128)(2,1)S(1)} %collective-permute-done.5.refs_12_), channel_id=1, source_target_pairs={{0,4},{4,0},{8,12},{12,8},{16,20},{20,16},{24,28},{28,24},{1,5},{5... | collective-permute-start | bytes 442376 | tf_op jit(solution)/shard_map/ppermute | solution.py:26
  38.7 2.5 %collective-permute-start.12 = (bf16[1,96,896]{2,1,0:T(8,128)(2,1)S(1)}, bf16[1,96,896]{2,1,0:T(8,128)(2,1)S(1)}, u32[]{:S(2)}, u32[]{:S(2)}) collective-permute-start(bf16[1,96,896]{2,1,0:T(8,128)(2,1)S(1)} %pad_maximum_fusion.1.refs_3_), channel_id=1, source_target_pairs={{0,4},{4,0},{8,12},{12,8},{16,20},{20,16},{24,28},{28,24},{1,5},{5... | collective-permute-start | bytes 516104 | tf_op jit(solution)/shard_map/ppermute | solution.py:26
  38.8 1.9 %collective-permute-start.18 = (bf16[1,96,768]{2,1,0:T(8,128)(2,1)S(1)}, bf16[1,96,768]{2,1,0:T(8,128)(2,1)S(1)}, u32[]{:S(2)}, u32[]{:S(2)}) collective-permute-start(bf16[1,96,768]{2,1,0:T(8,128)(2,1)S(1)} %collective-permute-done.9.refs_13_), channel_id=1, source_target_pairs={{0,4},{4,0},{8,12},{12,8},{16,20},{20,16},{24,28},{28,24},{1,5},{5... | collective-permute-start | bytes 442376 | tf_op jit(solution)/shard_map/ppermute | solution.py:26
  39.2 1.5 collective-permute-start.19
  39.5 10.9 %collective-permute-start.20 = (bf16[1,96,1536]{2,1,0:T(8,128)(2,1)S(1)}, bf16[1,96,1536]{2,1,0:T(8,128)(2,1)S(1)}, u32[]{:S(2)}, u32[]{:S(2)}) collective-permute-start(bf16[1,96,1536]{2,1,0:T(8,128)(2,1)S(1)} %bitcast.46), channel_id=1, source_target_pairs={{0,8},{4,12},{8,0},{12,4},{16,24},{20,28},{24,16},{28,20},{1,9},{5... | collective-permute-start | bytes 884744 | tf_op jit(solution)/shard_map/ppermute | solution.py:26
  40.1 10.4 %collective-permute-start.21 = (bf16[1,96,1536]{2,1,0:T(8,128)(2,1)S(1)}, bf16[1,96,1536]{2,1,0:T(8,128)(2,1)S(1)}, u32[]{:S(2)}, u32[]{:S(2)}) collective-permute-start(bf16[1,96,1536]{2,1,0:T(8,128)(2,1)S(1)} %collective-permute-done.11.refs_14_), channel_id=1, source_target_pairs={{0,16},{4,20},{8,24},{12,28},{16,0},{20,4},{24,8},{28,12},{1,17},{... | collective-permute-start | bytes 884744 | tf_op jit(solution)/shard_map/ppermute | solution.py:26
  40.6 1.4 collective-permute-start.13
  40.7 1.6 %collective-permute-start.14 = (bf16[1,96,896]{2,1,0:T(8,128)(2,1)S(1)}, bf16[1,96,896]{2,1,0:T(8,128)(2,1)S(1)}, u32[]{:S(2)}, u32[]{:S(2)}) collective-permute-start(bf16[1,96,896]{2,1,0:T(8,128)(2,1)S(1)} %collective-permute-done.7.refs_5_), channel_id=1, source_target_pairs={{0,4},{4,0},{8,12},{12,8},{16,20},{20,16},{24,28},{28,24},{1,5},{5... | collective-permute-start | bytes 516104 | tf_op jit(solution)/shard_map/ppermute | solution.py:26
  41.2 1.4 collective-permute-start.15
  50.5 23.2 %copy-start.17 = (bf16[1,96,1536]{2,1,0:T(8,128)(2,1)}, bf16[1,96,1536]{2,1,0:T(8,128)(2,1)S(1)}, u32[]{:S(2)}) copy-start(bf16[1,96,1536]{2,1,0:T(8,128)(2,1)S(1)} %collective-permute-done.20.refs_7_) | copy-start | bytes 884740
  50.5 23.1 %copy-start.18 = (bf16[1,96,1536]{2,1,0:T(8,128)(2,1)}, bf16[1,96,1536]{2,1,0:T(8,128)(2,1)S(1)}, u32[]{:S(2)}) copy-start(bf16[1,96,1536]{2,1,0:T(8,128)(2,1)S(1)} %collective-permute-done.21.refs_15_) | copy-start | bytes 884740
  50.5 8.0 %collective-permute-start.22 = (bf16[128,768]{1,0:T(8,128)(2,1)}, bf16[128,768]{1,0:T(8,128)(2,1)S(1)}, u32[]{:S(2)}, u32[]{:S(2)}) collective-permute-start(bf16[128,768]{1,0:T(8,128)(2,1)} %get-tuple-element.142), channel_id=1, source_target_pairs={{0,1},{1,0},{2,3},{3,2},{4,5},{5,4},{6,7},{7,6},{8,9},{9,8},{10,11... | collective-permute-start | bytes 589832 | tf_op jit(solution)/shard_map/ppermute | solution.py:26
  50.6 11.5 %collective-permute-start.28 = (bf16[128,768]{1,0:T(8,128)(2,1)S(1)}, bf16[128,768]{1,0:T(8,128)(2,1)S(1)}, u32[]{:S(2)}, u32[]{:S(2)}) collective-permute-start(bf16[128,768]{1,0:T(8,128)(2,1)S(1)} %copy-done.33), channel_id=1, source_target_pairs={{0,1},{1,0},{2,3},{3,2},{4,5},{5,4},{6,7},{7,6},{8,9},{9,8},{10,11... | collective-permute-start | bytes 589832 | tf_op jit(solution)/shard_map/ppermute | solution.py:26
  52.6 9.9 %collective-permute-start.23 = (bf16[1,96,1536]{2,1,0:T(8,128)(2,1)S(1)}, bf16[1,96,1536]{2,1,0:T(8,128)(2,1)S(1)}, u32[]{:S(2)}, u32[]{:S(2)}) collective-permute-start(bf16[1,96,1536]{2,1,0:T(8,128)(2,1)S(1)} %bitcast.47), channel_id=1, source_target_pairs={{0,16},{4,20},{8,24},{12,28},{16,0},{20,4},{24,8},{28,12},{1,17},{... | collective-permute-start | bytes 884744 | tf_op jit(solution)/shard_map/ppermute | solution.py:26
  54.1 13.5 %collective-permute-start.24 = (bf16[1,96,1536]{2,1,0:T(8,128)(2,1)S(1)}, bf16[1,96,1536]{2,1,0:T(8,128)(2,1)S(1)}, u32[]{:S(2)}, u32[]{:S(2)}) collective-permute-start(bf16[1,96,1536]{2,1,0:T(8,128)(2,1)S(1)} %collective-permute-done.20.refs_7_), channel_id=1, source_target_pairs={{0,16},{4,20},{8,24},{12,28},{16,0},{20,4},{24,8},{28,12},{1,17},{... | collective-permute-start | bytes 884744 | tf_op jit(solution)/shard_map/ppermute | solution.py:26
  54.6 12.9 %collective-permute-start.25 = (bf16[1,96,1536]{2,1,0:T(8,128)(2,1)S(1)}, bf16[1,96,1536]{2,1,0:T(8,128)(2,1)S(1)}, u32[]{:S(2)}, u32[]{:S(2)}) collective-permute-start(bf16[1,96,1536]{2,1,0:T(8,128)(2,1)S(1)} %collective-permute-done.11.refs_14_), channel_id=1, source_target_pairs={{0,8},{4,12},{8,0},{12,4},{16,24},{20,28},{24,16},{28,20},{1,9},{5... | collective-permute-start | bytes 884744 | tf_op jit(solution)/shard_map/ppermute | solution.py:26
  58.5 10.5 %collective-permute-start.26 = (bf16[1,96,1536]{2,1,0:T(8,128)(2,1)S(1)}, bf16[1,96,1536]{2,1,0:T(8,128)(2,1)S(1)}, u32[]{:S(2)}, u32[]{:S(2)}) collective-permute-start(bf16[1,96,1536]{2,1,0:T(8,128)(2,1)S(1)} %collective-permute-done.21.refs_15_), channel_id=1, source_target_pairs={{0,8},{4,12},{8,0},{12,4},{16,24},{20,28},{24,16},{28,20},{1,9},{5... | collective-permute-start | bytes 884744 | tf_op jit(solution)/shard_map/ppermute | solution.py:26
  62.1 6.9 %collective-permute-start.27 = (bf16[128,768]{1,0:T(8,128)(2,1)}, bf16[128,768]{1,0:T(8,128)(2,1)S(1)}, u32[]{:S(2)}, u32[]{:S(2)}) collective-permute-start(bf16[128,768]{1,0:T(8,128)(2,1)} %get-tuple-element.145.refs_1_), channel_id=1, source_target_pairs={{0,1},{1,0},{2,3},{3,2},{4,5},{5,4},{6,7},{7,6},{8,9},{9,8},{10,11... | collective-permute-start | bytes 589832 | tf_op jit(solution)/shard_map/ppermute | solution.py:26
  69.0 1.6 %collective-permute-start.29 = (bf16[1,96,1536]{2,1,0:T(8,128)(2,1)S(1)}, bf16[1,96,1536]{2,1,0:T(8,128)(2,1)S(1)}, u32[]{:S(2)}, u32[]{:S(2)}) collective-permute-start(bf16[1,96,1536]{2,1,0:T(8,128)(2,1)S(1)} %bitcast.48), channel_id=1, source_target_pairs={{0,4},{4,0},{8,12},{12,8},{16,20},{20,16},{24,28},{28,24},{1,5},{5... | collective-permute-start | bytes 884744 | tf_op jit(solution)/shard_map/ppermute | solution.py:26
  69.1 2.0 %collective-permute-start.30 = (bf16[1,96,1536]{2,1,0:T(8,128)(2,1)S(1)}, bf16[1,96,1536]{2,1,0:T(8,128)(2,1)S(1)}, u32[]{:S(2)}, u32[]{:S(2)}) collective-permute-start(bf16[1,96,1536]{2,1,0:T(8,128)(2,1)S(1)} %collective-permute-done.20.refs_7_), channel_id=1, source_target_pairs={{0,4},{4,0},{8,12},{12,8},{16,20},{20,16},{24,28},{28,24},{1,5},{5... | collective-permute-start | bytes 884744 | tf_op jit(solution)/shard_map/ppermute | solution.py:26
  69.6 1.9 %collective-permute-start.31 = (bf16[1,96,1536]{2,1,0:T(8,128)(2,1)S(1)}, bf16[1,96,1536]{2,1,0:T(8,128)(2,1)S(1)}, u32[]{:S(2)}, u32[]{:S(2)}) collective-permute-start(bf16[1,96,1536]{2,1,0:T(8,128)(2,1)S(1)} %collective-permute-done.23.refs_8_), channel_id=1, source_target_pairs={{0,4},{4,0},{8,12},{12,8},{16,20},{20,16},{24,28},{28,24},{1,5},{5... | collective-permute-start | bytes 884744 | tf_op jit(solution)/shard_map/ppermute | solution.py:26
  69.7 2.3 %collective-permute-start.32 = (bf16[1,96,1536]{2,1,0:T(8,128)(2,1)S(1)}, bf16[1,96,1536]{2,1,0:T(8,128)(2,1)S(1)}, u32[]{:S(2)}, u32[]{:S(2)}) collective-permute-start(bf16[1,96,1536]{2,1,0:T(8,128)(2,1)S(1)} %collective-permute-done.24.refs_9_), channel_id=1, source_target_pairs={{0,4},{4,0},{8,12},{12,8},{16,20},{20,16},{24,28},{28,24},{1,5},{5... | collective-permute-start | bytes 884744 | tf_op jit(solution)/shard_map/ppermute | solution.py:26
  70.1 2.2 %collective-permute-start.33 = (bf16[1,96,1536]{2,1,0:T(8,128)(2,1)S(1)}, bf16[1,96,1536]{2,1,0:T(8,128)(2,1)S(1)}, u32[]{:S(2)}, u32[]{:S(2)}) collective-permute-start(bf16[1,96,1536]{2,1,0:T(8,128)(2,1)S(1)} %collective-permute-done.11.refs_14_), channel_id=1, source_target_pairs={{0,4},{4,0},{8,12},{12,8},{16,20},{20,16},{24,28},{28,24},{1,5},{5... | collective-permute-start | bytes 884744 | tf_op jit(solution)/shard_map/ppermute | solution.py:26
  70.7 2.1 %collective-permute-start.34 = (bf16[1,96,1536]{2,1,0:T(8,128)(2,1)S(1)}, bf16[1,96,1536]{2,1,0:T(8,128)(2,1)S(1)}, u32[]{:S(2)}, u32[]{:S(2)}) collective-permute-start(bf16[1,96,1536]{2,1,0:T(8,128)(2,1)S(1)} %collective-permute-done.21.refs_15_), channel_id=1, source_target_pairs={{0,4},{4,0},{8,12},{12,8},{16,20},{20,16},{24,28},{28,24},{1,5},{5... | collective-permute-start | bytes 884744 | tf_op jit(solution)/shard_map/ppermute | solution.py:26
  71.1 2.1 %collective-permute-start.35 = (bf16[1,96,1536]{2,1,0:T(8,128)(2,1)S(1)}, bf16[1,96,1536]{2,1,0:T(8,128)(2,1)S(1)}, u32[]{:S(2)}, u32[]{:S(2)}) collective-permute-start(bf16[1,96,1536]{2,1,0:T(8,128)(2,1)S(1)} %collective-permute-done.25.refs_16_), channel_id=1, source_target_pairs={{0,4},{4,0},{8,12},{12,8},{16,20},{20,16},{24,28},{28,24},{1,5},{5... | collective-permute-start | bytes 884744 | tf_op jit(solution)/shard_map/ppermute | solution.py:26
  71.5 2.1 %collective-permute-start.36 = (bf16[1,96,1536]{2,1,0:T(8,128)(2,1)S(1)}, bf16[1,96,1536]{2,1,0:T(8,128)(2,1)S(1)}, u32[]{:S(2)}, u32[]{:S(2)}) collective-permute-start(bf16[1,96,1536]{2,1,0:T(8,128)(2,1)S(1)} %collective-permute-done.26.refs_17_), channel_id=1, source_target_pairs={{0,4},{4,0},{8,12},{12,8},{16,20},{20,16},{24,28},{28,24},{1,5},{5... | collective-permute-start | bytes 884744 | tf_op jit(solution)/shard_map/ppermute | solution.py:26
  83.2 4.3 %collective-permute-start.38 = (bf16[4,96,1536]{2,1,0:T(8,128)(2,1)}, bf16[4,96,1536]{2,1,0:T(8,128)(2,1)S(1)}, u32[]{:S(2)}, u32[]{:S(2)}) collective-permute-start(bf16[4,96,1536]{2,1,0:T(8,128)(2,1)} %get-tuple-element.172), channel_id=1, source_target_pairs={{0,4},{4,0},{8,12},{12,8},{16,20},{20,16},{24,28},{28,24},{1,5},{5... | collective-permute-start | bytes 3538952 | tf_op jit(solution)/shard_map/ppermute | solution.py:26
  83.3 7.4 %collective-permute-start.37 = (bf16[128,768]{1,0:T(8,128)(2,1)}, bf16[128,768]{1,0:T(8,128)(2,1)S(1)}, u32[]{:S(2)}, u32[]{:S(2)}) collective-permute-start(bf16[128,768]{1,0:T(8,128)(2,1)} %get-tuple-element.163), channel_id=1, source_target_pairs={{0,1},{1,0},{2,3},{3,2},{4,5},{5,4},{6,7},{7,6},{8,9},{9,8},{10,11... | collective-permute-start | bytes 589832 | tf_op jit(solution)/shard_map/ppermute | solution.py:26
  90.8 4.0 %collective-permute-start.39 = (bf16[4,96,1536]{2,1,0:T(8,128)(2,1)S(1)}, bf16[4,96,1536]{2,1,0:T(8,128)(2,1)S(1)}, u32[]{:S(2)}, u32[]{:S(2)}) collective-permute-start(bf16[4,96,1536]{2,1,0:T(8,128)(2,1)S(1)} %copy-done.55), channel_id=1, source_target_pairs={{0,4},{4,0},{8,12},{12,8},{16,20},{20,16},{24,28},{28,24},{1,5},{5... | collective-permute-start | bytes 3538952 | tf_op jit(solution)/shard_map/ppermute | solution.py:26
  90.8 19.2 %collective-permute-start.43 = (bf16[2,96,1536]{2,1,0:T(8,128)(2,1)S(1)}, bf16[2,96,1536]{2,1,0:T(8,128)(2,1)}, u32[]{:S(2)}, u32[]{:S(2)}) collective-permute-start(bf16[2,96,1536]{2,1,0:T(8,128)(2,1)S(1)} %get-tuple-element.193), channel_id=1, source_target_pairs={{0,8},{4,12},{8,0},{12,4},{16,24},{20,28},{24,16},{28,20},{1,9},{5... | collective-permute-start | bytes 1769480 | tf_op jit(solution)/shard_map/ppermute | solution.py:26
  95.9 7.7 %collective-permute-start.40 = (bf16[128,768]{1,0:T(8,128)(2,1)S(1)}, bf16[128,768]{1,0:T(8,128)(2,1)S(1)}, u32[]{:S(2)}, u32[]{:S(2)}) collective-permute-start(bf16[128,768]{1,0:T(8,128)(2,1)S(1)} %copy-done.6), channel_id=1, source_target_pairs={{0,1},{1,0},{2,3},{3,2},{4,5},{5,4},{6,7},{7,6},{8,9},{9,8},{10,11... | collective-permute-start | bytes 589832 | tf_op jit(solution)/shard_map/ppermute | solution.py:26
  96.2 15.3 %collective-permute-start.42 = (bf16[2,96,1536]{2,1,0:T(8,128)(2,1)}, bf16[2,96,1536]{2,1,0:T(8,128)(2,1)S(1)}, u32[]{:S(2)}, u32[]{:S(2)}) collective-permute-start(bf16[2,96,1536]{2,1,0:T(8,128)(2,1)} %get-tuple-element.191), channel_id=1, source_target_pairs={{0,16},{4,20},{8,24},{12,28},{16,0},{20,4},{24,8},{28,12},{1,17},{... | collective-permute-start | bytes 1769480 | tf_op jit(solution)/shard_map/ppermute | solution.py:26
  98.5 13.7 %collective-permute-start.41 = (bf16[128,768]{1,0:T(8,128)(2,1)S(1)}, bf16[128,768]{1,0:T(8,128)(2,1)S(1)}, u32[]{:S(2)}, u32[]{:S(2)}) collective-permute-start(bf16[128,768]{1,0:T(8,128)(2,1)S(1)} %copy-done.56), channel_id=1, source_target_pairs={{0,1},{1,0},{2,3},{3,2},{4,5},{5,4},{6,7},{7,6},{8,9},{9,8},{10,11... | collective-permute-start | bytes 589832 | tf_op jit(solution)/shard_map/ppermute | solution.py:26
  109.9 3.9 %collective-permute-start.44 = (bf16[4,96,768]{2,1,0:T(8,128)(2,1)}, bf16[4,96,768]{2,1,0:T(8,128)(2,1)S(1)}, u32[]{:S(2)}, u32[]{:S(2)}) collective-permute-start(bf16[4,96,768]{2,1,0:T(8,128)(2,1)} %get-tuple-element.200), channel_id=1, source_target_pairs={{0,4},{4,0},{8,12},{12,8},{16,20},{20,16},{24,28},{28,24},{1,5},{5... | collective-permute-start | bytes 1769480 | tf_op jit(solution)/shard_map/ppermute | solution.py:26
  112.3 9.5 %collective-permute-start.45 = (bf16[1,96,1536]{2,1,0:T(8,128)(2,1)S(1)}, bf16[1,96,1536]{2,1,0:T(8,128)(2,1)S(1)}, u32[]{:S(2)}, u32[]{:S(2)}) collective-permute-start(bf16[1,96,1536]{2,1,0:T(8,128)(2,1)S(1)} %slice.146), channel_id=1, source_target_pairs={{0,16},{4,20},{8,24},{12,28},{16,0},{20,4},{24,8},{28,12},{1,17},{... | collective-permute-start | bytes 884744 | tf_op jit(solution)/shard_map/ppermute | solution.py:26
  114.0 9.3 %collective-permute-start.46 = (bf16[2,96,768]{2,1,0:T(8,128)(2,1)S(1)}, bf16[2,96,768]{2,1,0:T(8,128)(2,1)S(1)}, u32[]{:S(2)}, u32[]{:S(2)}) collective-permute-start(bf16[2,96,768]{2,1,0:T(8,128)(2,1)S(1)} %get-tuple-element.212), channel_id=1, source_target_pairs={{0,8},{4,12},{8,0},{12,4},{16,24},{20,28},{24,16},{28,20},{1,9},{5... | collective-permute-start | bytes 884744 | tf_op jit(solution)/shard_map/ppermute | solution.py:26
  121.0 8.0 %collective-permute-start.50 = (bf16[4,96,896]{2,1,0:T(8,128)(2,1)}, bf16[4,96,896]{2,1,0:T(8,128)(2,1)S(1)}, u32[]{:S(2)}, u32[]{:S(2)}) collective-permute-start(bf16[4,96,896]{2,1,0:T(8,128)(2,1)} %get-tuple-element.220), channel_id=1, source_target_pairs={{0,4},{4,0},{8,12},{12,8},{16,20},{20,16},{24,28},{28,24},{1,5},{5... | collective-permute-start | bytes 2064392 | tf_op jit(solution)/shard_map/ppermute | solution.py:26
  123.4 5.6 %collective-permute-start.52 = (bf16[1,96,768]{2,1,0:T(8,128)(2,1)S(1)}, bf16[1,96,768]{2,1,0:T(8,128)(2,1)S(1)}, u32[]{:S(2)}, u32[]{:S(2)}) collective-permute-start(bf16[1,96,768]{2,1,0:T(8,128)(2,1)S(1)} %slice.149), channel_id=1, source_target_pairs={{0,16},{4,20},{8,24},{12,28},{16,0},{20,4},{24,8},{28,12},{1,17},{... | collective-permute-start | bytes 442376 | tf_op jit(solution)/shard_map/ppermute | solution.py:26
  125.8 14.9 %collective-permute-start.47 = (bf16[96,1536]{1,0:T(8,128)(2,1)S(1)}, bf16[96,1536]{1,0:T(8,128)(2,1)S(1)}, u32[]{:S(2)}, u32[]{:S(2)}) collective-permute-start(bf16[96,1536]{1,0:T(8,128)(2,1)S(1)} %add_bitcast_fusion.1), channel_id=1, source_target_pairs={{0,2},{1,3},{2,0},{3,1},{4,6},{5,7},{6,4},{7,5},{8,10},{9,11},{10,... | collective-permute-start | bytes 884744 | tf_op jit(solution)/shard_map/ppermute | solution.py:26
  126.7 7.5 %collective-permute-start.48 = (bf16[1,96,1536]{2,1,0:T(8,128)(2,1)S(1)}, bf16[1,96,1536]{2,1,0:T(8,128)(2,1)S(1)}, u32[]{:S(2)}, u32[]{:S(2)}) collective-permute-start(bf16[1,96,1536]{2,1,0:T(8,128)(2,1)S(1)} %slice.147), channel_id=1, source_target_pairs={{0,8},{4,12},{8,0},{12,4},{16,24},{20,28},{24,16},{28,20},{1,9},{5... | collective-permute-start | bytes 884744 | tf_op jit(solution)/shard_map/ppermute | solution.py:26
  127.3 10.6 %collective-permute-start.49 = (bf16[128,768]{1,0:T(8,128)(2,1)S(1)}, bf16[128,768]{1,0:T(8,128)(2,1)S(1)}, u32[]{:S(2)}, u32[]{:S(2)}) collective-permute-start(bf16[128,768]{1,0:T(8,128)(2,1)S(1)} %copy-done.57), channel_id=1, source_target_pairs={{0,1},{1,0},{2,3},{3,2},{4,5},{5,4},{6,7},{7,6},{8,9},{9,8},{10,11... | collective-permute-start | bytes 589832 | tf_op jit(solution)/shard_map/ppermute | solution.py:26
  129.2 8.6 %collective-permute-start.51 = (bf16[2,96,896]{2,1,0:T(8,128)(2,1)S(1)}, bf16[2,96,896]{2,1,0:T(8,128)(2,1)S(1)}, u32[]{:S(2)}, u32[]{:S(2)}) collective-permute-start(bf16[2,96,896]{2,1,0:T(8,128)(2,1)S(1)} %add_convert_fusion.2), channel_id=1, source_target_pairs={{0,16},{4,20},{8,24},{12,28},{16,0},{20,4},{24,8},{28,12},{1,17},{... | collective-permute-start | bytes 1032200 | tf_op jit(solution)/shard_map/ppermute | solution.py:26
  140.7 6.3 %collective-permute-start.53 = (bf16[1,96,896]{2,1,0:T(8,128)(2,1)S(1)}, bf16[1,96,896]{2,1,0:T(8,128)(2,1)S(1)}, u32[]{:S(2)}, u32[]{:S(2)}) collective-permute-start(bf16[1,96,896]{2,1,0:T(8,128)(2,1)S(1)} %slice.148), channel_id=1, source_target_pairs={{0,8},{4,12},{8,0},{12,4},{16,24},{20,28},{24,16},{28,20},{1,9},{5... | collective-permute-start | bytes 516104 | tf_op jit(solution)/shard_map/ppermute | solution.py:26
  141.8 10.1 %collective-permute-start.54 = (bf16[96,768]{1,0:T(8,128)(2,1)S(1)}, bf16[96,768]{1,0:T(8,128)(2,1)S(1)}, u32[]{:S(2)}, u32[]{:S(2)}) collective-permute-start(bf16[96,768]{1,0:T(8,128)(2,1)S(1)} %bitcast.55), channel_id=1, source_target_pairs={{0,2},{1,3},{2,0},{3,1},{4,6},{5,7},{6,4},{7,5},{8,10},{9,11},{10,... | collective-permute-start | bytes 442376 | tf_op jit(solution)/shard_map/ppermute | solution.py:26
  147.1 6.7 %collective-permute-start.57 = (f32[96,16]{1,0:T(8,128)S(1)}, f32[96,16]{1,0:T(8,128)S(1)}, u32[]{:S(2)}, u32[]{:S(2)}) collective-permute-start(f32[96,16]{1,0:T(8,128)S(1)} %slice.123), channel_id=1, source_target_pairs={{0,3},{1,2},{2,1},{3,0},{4,7},{5,6},{6,5},{7,4},{8,11},{9,10},{10,... | collective-permute-start | bytes 18440 | tf_op jit(solution)/shard_map/ppermute | solution.py:26
  149.1 5.9 %collective-permute-start.56 = (f32[96,16]{1,0:T(8,128)S(1)}, f32[96,16]{1,0:T(8,128)S(1)}, u32[]{:S(2)}, u32[]{:S(2)}) collective-permute-start(f32[96,16]{1,0:T(8,128)S(1)} %slice.123), channel_id=1, source_target_pairs={{0,2},{1,3},{2,0},{3,1},{4,6},{5,7},{6,4},{7,5},{8,10},{9,11},{10,... | collective-permute-start | bytes 18440 | tf_op jit(solution)/shard_map/ppermute | solution.py:26
  149.3 5.6 %collective-permute-start.55 = (f32[96,16]{1,0:T(8,128)S(1)}, f32[96,16]{1,0:T(8,128)S(1)}, u32[]{:S(2)}, u32[]{:S(2)}) collective-permute-start(f32[96,16]{1,0:T(8,128)S(1)} %slice.123), channel_id=1, source_target_pairs={{0,1},{1,0},{2,3},{3,2},{4,5},{5,4},{6,7},{7,6},{8,9},{9,8},{10,11... | collective-permute-start | bytes 18440 | tf_op jit(solution)/shard_map/ppermute | solution.py:26
  (58 other events, 265.5 us)
